TPU v7x, 256 devices: a whole 4x4x8 slice. The times are simulated.
256 devices in a mesh: clip: 16 (over z, core), row: 4 (over y), tm: 4 (over x).
Axes of the slice: x: 4, y: 4, z: 8, core: 2. Of those that a mesh axis runs over, the one named last changes fastest.
Arguments:
- frames: bfloat16 [128, 3, 16, 1024], P('clip', None, 'tm', 'row'), may hold values from -6 to 6
- keep_list: int32 [128], P('clip'), may hold values from -1 to 63, as said below
- train_slot: int32 [64], replicated, may hold values from 0 to 63, as said below
- stem_weight: bfloat16 [81, 128], replicated, may hold values from -0.625 to 0.625
- stem_gain: float32 [128], replicated, may hold values from 0.1 to 1.9
- stem_shift: float32 [128], replicated, may hold values from -3 to 3
- mixer_weight: bfloat16 [3, 3, 384, 256], replicated, may hold values from -0.109375 to 0.109375
- mixer_gain: float32 [256], replicated, may hold values from 0.1 to 1.9
- mixer_shift: float32 [256], replicated, may hold values from -3 to 3
- down_weight: bfloat16 [1024, 256], replicated, may hold values from -0.1875 to 0.1875
- down_bias: float32 [256], replicated, may hold values from -3 to 3
Outputs:
- latents: bfloat16 [64, 8, 8, 32, 256], P('clip', 'tm', 'row')
Inputs may be any that keep to these rules, and one draw needn't show every extreme that they name: `keep_list`: each encoder position 0 to 63 is named by exactly one slot, and -1 marks a dropped slot; encoder position e belongs to index e // 4 of clip. `train_slot`: A permutation; training position t belongs to index t // 4 of clip; at most 1 encoder positions of one index of clip go to one index of clip.
All inputs are finite; a program needn't handle non-finite values.
Results may differ from a plain program's by a relative error of at most 0.0053.
Values may be sent and summed in bfloat16 or wider, within the bound.
No kernel may reach another device: no remote copies, remote signals or barrier semaphores. Data moves between devices by JAX's collectives and lax.ppermute only.
A program may use at most 64 MiB of HBM per device.

v0:
```python
import jax
import jax.numpy as jnp
from jax import lax
from jax.sharding import PartitionSpec as P

GROUPS = 32
COLS = 64


eps = 1e-06


def from_behind(shard, axis, by):
    size = lax.axis_size(axis)
    pairs = [(i, i + by) for i in range(size) if 0 <= i + by < size]
    return lax.ppermute(shard, axis, pairs)


def extended_2(cells, sides, width):
    for axis, dim in sides:
        count = lax.axis_size(axis)
        ends = count - 1
        head = lax.slice_in_dim(cells, 0, width, axis=dim)
        tail = lax.slice_in_dim(cells, cells.shape[dim] - width, cells.shape[dim], axis=dim)
        cells = jnp.concatenate(
            [
                lax.ppermute(tail, axis, [(i, (i + 1) % count) for i in range(ends)]),
                cells,
                lax.ppermute(head, axis, [((i + 1) % count, i) for i in range(ends)]),
            ],
            axis=dim,
        )
    return cells


def surround_time(volume):
    frame_n = volume.shape[1]
    earlier = from_behind(volume[:, frame_n - 2 :], "tm", 1)
    opening = jnp.broadcast_to(volume[:, :1], earlier.shape)
    earlier = jnp.where(lax.axis_index("tm") == 0, opening, earlier)
    extended = jnp.concatenate([earlier, volume], axis=1)
    extended = extended_2(extended, (("row", 2),), 1)
    return jnp.pad(extended, ((0, 0), (0, 0), (0, 0), (1, 1), (0, 0)))


def norm_silu(hidden, gain, shift):
    batch_n, cell_n, chan_n = hidden.shape
    per_group = chan_n // GROUPS
    value_sum = jnp.sum(hidden, axis=1).reshape(batch_n, GROUPS, per_group).sum(-1)
    square_sum = jnp.sum(hidden * hidden, axis=1).reshape(batch_n, GROUPS, per_group).sum(-1)
    value_sum, square_sum = lax.psum((value_sum, square_sum), ("row", "tm"))
    cell_count = cell_n * per_group * lax.axis_size("row") * lax.axis_size("tm")
    group_mean = value_sum / cell_count
    spread = square_sum / cell_count - group_mean * group_mean
    inverse = lax.rsqrt(spread + eps)
    mean_full = jnp.repeat(group_mean, per_group, axis=1)[:, None, :]
    scale_full = jnp.repeat(inverse, per_group, axis=1)[:, None, :] * gain
    return jax.nn.silu((hidden - mean_full) * scale_full + shift)


def encode(clips, params, col_n, surround):
    (
        stem_weight,
        stem_gain,
        stem_shift,
        mixer_weight,
        mixer_gain,
        mixer_shift,
        down_weight,
        down_bias,
    ) = params
    batch_n, chan_in, frame_n, row_cells = clips.shape
    row_n = row_cells // col_n
    cell_n = frame_n * row_n * col_n
    volume = clips.reshape(batch_n, chan_in, frame_n, row_n, col_n).transpose(0, 2, 3, 4, 1)
    padded = surround(volume)
    tap_views = []
    for time_tap in range(3):
        for row_tap in range(3):
            for col_tap in range(3):
                tap_views.append(
                    padded[
                        :,
                        time_tap : time_tap + frame_n,
                        row_tap : row_tap + row_n,
                        col_tap : col_tap + col_n,
                    ]
                )
    patches = jnp.concatenate(tap_views, axis=-1).reshape(batch_n * cell_n, 27 * chan_in)
    stem = jnp.dot(patches, stem_weight, preferred_element_type=jnp.float32).reshape(
        batch_n, cell_n, -1
    )
    hidden = norm_silu(stem, stem_gain, stem_shift).astype(jnp.bfloat16)
    padded = surround(hidden.reshape(batch_n, frame_n, row_n, col_n, -1))
    accumulated = jnp.zeros((batch_n * cell_n, mixer_weight.shape[3]), jnp.float32)
    for time_tap in range(3):
        for row_tap in range(3):
            tap_strip = jnp.concatenate(
                [
                    padded[
                        :,
                        time_tap : time_tap + frame_n,
                        row_tap : row_tap + row_n,
                        col_tap : col_tap + col_n,
                    ]
                    for col_tap in range(3)
                ],
                axis=-1,
            )
            accumulated = accumulated + jnp.dot(
                tap_strip.reshape(-1, tap_strip.shape[-1]),
                mixer_weight[time_tap, row_tap],
                preferred_element_type=jnp.float32,
            )
    activated = norm_silu(accumulated.reshape(batch_n, cell_n, -1), mixer_gain, mixer_shift).astype(
        jnp.bfloat16
    )
    activated = activated.reshape(batch_n, frame_n, row_n, col_n, -1)
    pooled = (
        (activated[:, 0::2].astype(jnp.float32) + activated[:, 1::2].astype(jnp.float32)) * 0.5
    ).astype(jnp.bfloat16)
    chan_out = pooled.shape[-1]
    blocks = (
        pooled.reshape(batch_n, frame_n // 2, row_n // 2, 2, col_n // 2, 2, chan_out)
        .transpose(0, 1, 2, 4, 3, 5, 6)
        .reshape(-1, 4 * chan_out)
    )
    latent = jnp.dot(blocks, down_weight, preferred_element_type=jnp.float32) + down_bias
    return latent.astype(jnp.bfloat16).reshape(
        batch_n, frame_n // 2, row_n // 2, col_n // 2, chan_out
    )


def encode_layout(clips, params):
    return encode(clips, params, COLS, surround_time)


def select_rows(target, items, slot_n):
    flattened = items.reshape(items.shape[0], -1)
    wanted = jnp.arange(slot_n, dtype=jnp.int32)
    picker = (wanted[:, None] == target[None, :]).astype(jnp.bfloat16)
    return jnp.dot(picker, flattened, preferred_element_type=jnp.float32).astype(jnp.bfloat16)


def combine_sources(received):
    return jnp.sum(received.astype(jnp.float32), axis=0).astype(jnp.bfloat16)


def local(
    frames,
    keep_list,
    train_slot,
    stem_weight,
    stem_gain,
    stem_shift,
    mixer_weight,
    mixer_gain,
    mixer_shift,
    down_weight,
    down_bias,
):
    params = (
        stem_weight,
        stem_gain,
        stem_shift,
        mixer_weight,
        mixer_gain,
        mixer_shift,
        down_weight,
        down_bias,
    )
    group_n = lax.axis_size("clip")
    enc_dev = train_slot.shape[0] // group_n
    slot_n = group_n * enc_dev
    safe_keep = jnp.maximum(keep_list, 0)
    composed = jnp.where(keep_list >= 0, train_slot[safe_keep], -1)
    packed = select_rows(composed, frames, slot_n).reshape((group_n, enc_dev) + frames.shape[1:])
    received = lax.all_to_all(packed, "clip", split_axis=0, concat_axis=0, tiled=True)
    return encode_layout(combine_sources(received), params)


def solution(mesh):
    return jax.shard_map(
        local,
        mesh=mesh,
        in_specs=(
            P("clip", None, "tm", "row"),
            P("clip"),
            P(),
            P(),
            P(),
            P(),
            P(),
            P(),
            P(),
            P(),
            P(),
        ),
        out_specs=P("clip", "tm", "row", None, None),
        check_vma=False,
    )
```

profile of v0, /device:TPU:2, one launch (start us, length us, event | category | flops | bytes accessed | tf_op | source)
XLA Modules:
  0.0 239.9 jit_solution(16834706322915642902)
XLA Ops:
  1.6 1.3 gather_fusion
  4.8 8.6 %all-to-all-start = ((bf16[16,4,3,4,256]{4,3,2,1,0:T(4,128)(2,1)}), bf16[16,4,3,4,256]{4,3,2,1,0:T(4,128)(2,1)S(1)}, u32[]{:S(2)}, u32[]{:S(2)}) async-start(bf16[16,4,3,4,256]{4,3,2,1,0:T(4,128)(2,1)} %reshape.120), calls=%async_computation | async-start | bytes 786432 | tf_op jit(solution)/shard_map/all_to_all | solution.py:178
  13.4 13.6 %all-to-all-done = bf16[16,4,3,4,256]{4,3,2,1,0:T(4,128)(2,1)S(1)} async-done(((bf16[16,4,3,4,256]{4,3,2,1,0:T(4,128)(2,1)}), bf16[16,4,3,4,256]{4,3,2,1,0:T(4,128)(2,1)S(1)}, u32[]{:S(2)}, u32[]{:S(2)}) %all-to-all-start) | async-done | bytes 393248 | tf_op jit(solution)/shard_map/all_to_all | solution.py:178
  27.3 3.4 %collective-permute-start = (bf16[4,2,4,64,3]{3,2,4,1,0:T(4,128)(2,1)S(1)}, bf16[4,2,4,64,3]{3,2,4,1,0:T(4,128)(2,1)S(1)}, u32[]{:S(2)}, u32[]{:S(2)}) collective-permute-start(bf16[4,2,4,64,3]{3,2,4,1,0:T(4,128)(2,1)S(1)} %slice.325), channel_id=1, source_target_pairs={{0,1},{1,2},{2,3},{4,5},{5,6},{6,7},{8,9},{9,10},{10,11},{12,13},{... | collective-permute-start | bytes 36872 | tf_op jit(solution)/shard_map/ppermute | solution.py:16
  30.7 2.3 collective-permute-done
  34.5 4.5 %collective-permute-start.1 = (bf16[4,6,1,64,3]{3,2,4,1,0:T(2,128)(2,1)S(1)}, bf16[4,6,1,64,3]{3,2,4,1,0:T(2,128)(2,1)S(1)}, u32[]{:S(2)}, u32[]{:S(2)}) collective-permute-start(bf16[4,6,1,64,3]{3,2,4,1,0:T(2,128)(2,1)S(1)} %get-tuple-element.43), channel_id=1, source_target_pairs={{0,4},{4,8},{8,12},{1,5},{5,9},{9,13},{2,6},{6,10},{10,14},{3,7},{... | collective-permute-start | bytes 27656 | tf_op jit(solution)/shard_map/ppermute | solution.py:27
  39.0 1.6 collective-permute-done.1
  43.0 2.1 copy.36
  45.2 1.7 fusion.49
  47.3 37.7 %all-reduce.3 = (f32[4,32]{1,0:T(4,128)S(1)}, f32[4,32]{1,0:T(4,128)S(1)}) all-reduce(f32[4,32]{1,0:T(4,128)S(1)} %reduce_sum.88, f32[4,32]{1,0:T(4,128)S(1)} %reduce_sum.86), channel_id=1, replica_groups=mesh['clip'=16,'row'=4,'tm'=4] {'row','tm'}, use_global_device_ids=true, to_apply=%region_6.7 | all-reduce | flops 256 | bytes 2048 | tf_op jit(solution)/shard_map/psum | solution.py:51
  86.1 3.1 %collective-permute-start.3 = (bf16[4,2,4,64,128]{4,3,2,1,0:T(8,128)(2,1)S(1)}, bf16[4,2,4,64,128]{4,3,2,1,0:T(8,128)(2,1)S(1)}, u32[]{:S(2)}, u32[]{:S(2)}) collective-permute-start(bf16[4,2,4,64,128]{4,3,2,1,0:T(8,128)(2,1)S(1)} %slice.357), channel_id=1, source_target_pairs={{0,1},{1,2},{2,3},{4,5},{5,6},{6,7},{8,9},{9,10},{10,11},{12,13},{... | collective-permute-start | bytes 1572872 | tf_op jit(solution)/shard_map/ppermute | solution.py:16
  89.3 9.8 %collective-permute-done.3 = bf16[4,2,4,64,128]{4,3,2,1,0:T(8,128)(2,1)S(1)} collective-permute-done((bf16[4,2,4,64,128]{4,3,2,1,0:T(8,128)(2,1)S(1)}, bf16[4,2,4,64,128]{4,3,2,1,0:T(8,128)(2,1)S(1)}, u32[]{:S(2)}, u32[]{:S(2)}) %collective-permute-start.3) | collective-permute-done | bytes 524320 | tf_op jit(solution)/shard_map/ppermute | solution.py:16
  100.5 4.8 %collective-permute-start.4 = (bf16[4,6,1,64,128]{4,3,2,1,0:T(8,128)(2,1)S(1)}, bf16[4,6,1,64,128]{4,3,2,1,0:T(8,128)(2,1)S(1)}, u32[]{:S(2)}, u32[]{:S(2)}) collective-permute-start(bf16[4,6,1,64,128]{4,3,2,1,0:T(8,128)(2,1)S(1)} %get-tuple-element.39), channel_id=1, source_target_pairs={{0,4},{4,8},{8,12},{1,5},{5,9},{9,13},{2,6},{6,10},{10,14},{3,7},{... | collective-permute-start | bytes 1179656 | tf_op jit(solution)/shard_map/ppermute | solution.py:27
  106.3 2.6 %collective-permute-done.5 = bf16[4,6,1,64,128]{4,3,2,1,0:T(8,128)(2,1)S(1)} collective-permute-done((bf16[4,6,1,64,128]{4,3,2,1,0:T(8,128)(2,1)S(1)}, bf16[4,6,1,64,128]{4,3,2,1,0:T(8,128)(2,1)S(1)}, u32[]{:S(2)}, u32[]{:S(2)}) %collective-permute-start.5) | collective-permute-done | bytes 393248 | tf_op jit(solution)/shard_map/ppermute | solution.py:29
  108.8 1.5 collective-permute-done.4
  110.3 1.4 select_maximum_fusion
  111.7 6.2 %fusion.50 = (bf16[4,4,4,64,128]{4,3,2,1,0:T(8,128)(2,1)}, bf16[4,4,4,64,128]{4,3,2,1,0:T(8,128)(2,1)}, bf16[4,4,4,64,128]{4,3,2,1,0:T(8,128)(2,1)}, bf16[4,4,4,...) fusion(bf16[4,6,6,66,128]{4,3,2,1,0:T(8,128)(2,1)S(1)} %select_, ...), kind=kLoop, calls=%fused_computation.143 | loop fusion | bytes 37748736 | tf_op jit(solution)/shard_map/slice | solution.py:100
  130.9 1.3 pad_maximum_fusion.5
  137.9 3.2 %bitcast_reduce_fusion = (f32[4,256]{1,0:T(4,128)S(1)}, f32[4,256]{1,0:T(4,128)S(1)}, f32[4096,256]{1,0:T(8,128)}) fusion(f32[4096,256]{1,0:T(8,128)S(1)} %convolution_add_fusion.1, bf16[4096,384]{1,0:T(8,128)(2,1)S(1)} %bitcast.87, bf16[3,3,384,256]{3,2,1,0:T(8,128)(2,1)S(1)} %copy-done.8), kind=kOutput, calls=%fused_computation.14 | convolution fusion | flops 809498624 | bytes 11739136 | tf_op jit(solution)/shard_map/dot_general | solution.py:110
  141.5 35.0 %all-reduce.2 = (f32[4,32]{1,0:T(4,128)S(1)}, f32[4,32]{1,0:T(4,128)S(1)}) all-reduce(f32[4,32]{1,0:T(4,128)S(1)} %reduce_sum.92, f32[4,32]{1,0:T(4,128)S(1)} %reduce_sum.90), channel_id=1, replica_groups=mesh['clip'=16,'row'=4,'tm'=4] {'row','tm'}, use_global_device_ids=true, to_apply=%region_12.13 | all-reduce | flops 256 | bytes 2048 | tf_op jit(solution)/shard_map/psum | solution.py:51
  176.9 6.2 %fusion.4 = bf16[4,4,4,64,256]{4,1,3,2,0:T(4,128)(2,1)S(1)} fusion(f32[4,4,4,64,256]{4,3,2,1,0:T(8,128)} %bitcast.86, f32[256]{0:T(256)S(1)} %copy-done.13, f32[4,256]{1,0:T(4,128)S(1)} %broadcast_multiply_fusion, f32[4,256]{1,0:T(4,128)S(1)} %sub.31), kind=kLoop, calls=%fused_computation.19 | loop fusion | flops 8388608 | bytes 6300672 | tf_op jit(solution)/shard_map/convert_element_type | solution.py:115
  183.1 25.5 %slice.321 = bf16[4,2,4,64,256]{4,1,3,2,0:T(2,128)(2,1)} slice(bf16[4,4,4,64,256]{4,1,3,2,0:T(4,128)(2,1)S(1)} %fusion.4), slice={[0:4:1], [1:4:2], [0:4:1], [0:64:1], [0:256:1]} | slice | bytes 2097152 | tf_op jit(solution)/shard_map/slice | solution.py:120
  208.6 25.4 %slice.320 = bf16[4,2,4,64,256]{4,1,3,2,0:T(2,128)(2,1)} slice(bf16[4,4,4,64,256]{4,1,3,2,0:T(4,128)(2,1)S(1)} %fusion.4), slice={[0:4:1], [0:4:2], [0:4:1], [0:64:1], [0:256:1]} | slice | bytes 2097152 | tf_op jit(solution)/shard_map/slice | solution.py:120
  234.0 3.1 %multiply_convert_fusion = bf16[4,2,4,64,256]{4,1,3,2,0:T(2,128)(2,1)S(1)} fusion(bf16[4,2,4,64,256]{4,1,3,2,0:T(2,128)(2,1)} %slice.321, bf16[4,2,4,64,256]{4,1,3,2,0:T(2,128)(2,1)} %slice.320), kind=kLoop, calls=%fused_computation.44 | loop fusion | flops 2621440 | bytes 3145728 | tf_op jit(solution)/shard_map/convert_element_type | solution.py:121
  (123 shorter events, 33.3 us)
Async XLA Ops:
  0.0 238.8 %copy-start = (bf16[1024,256]{1,0:T(8,128)(2,1)S(1)}, bf16[1024,256]{1,0:T(8,128)(2,1)}, u32[]{:S(2)}) copy-start(bf16[1024,256]{1,0:T(8,128)(2,1)} %param.20) | copy-start | bytes 1572868
  4.8 22.2 %all-to-all-start = ((bf16[16,4,3,4,256]{4,3,2,1,0:T(4,128)(2,1)}), bf16[16,4,3,4,256]{4,3,2,1,0:T(4,128)(2,1)S(1)}, u32[]{:S(2)}, u32[]{:S(2)}) async-start(bf16[16,4,3,4,256]{4,3,2,1,0:T(4,128)(2,1)} %reshape.120), calls=%async_computation | async-start | bytes 786432 | tf_op jit(solution)/shard_map/all_to_all | solution.py:178
  27.2 18.0 %copy-start.11 = (bf16[81,128]{1,0:T(8,128)(2,1)S(1)}, bf16[81,128]{1,0:T(8,128)(2,1)}, u32[]{:S(2)}) copy-start(bf16[81,128]{1,0:T(8,128)(2,1)} %param.14) | copy-start | bytes 62212
  27.3 5.7 %collective-permute-start = (bf16[4,2,4,64,3]{3,2,4,1,0:T(4,128)(2,1)S(1)}, bf16[4,2,4,64,3]{3,2,4,1,0:T(4,128)(2,1)S(1)}, u32[]{:S(2)}, u32[]{:S(2)}) collective-permute-start(bf16[4,2,4,64,3]{3,2,4,1,0:T(4,128)(2,1)S(1)} %slice.325), channel_id=1, source_target_pairs={{0,1},{1,2},{2,3},{4,5},{5,6},{6,7},{8,9},{9,10},{10,11},{12,13},{... | collective-permute-start | bytes 36872 | tf_op jit(solution)/shard_map/ppermute | solution.py:16
  33.2 5.9 %collective-permute-start.2 = (bf16[4,6,1,64,3]{3,2,4,1,0:T(2,128)(2,1)S(1)}, bf16[4,6,1,64,3]{3,2,4,1,0:T(2,128)(2,1)S(1)}, u32[]{:S(2)}, u32[]{:S(2)}) collective-permute-start(bf16[4,6,1,64,3]{3,2,4,1,0:T(2,128)(2,1)S(1)} %get-tuple-element.44), channel_id=1, source_target_pairs={{4,0},{8,4},{12,8},{5,1},{9,5},{13,9},{6,2},{10,6},{14,10},{7,3},{... | collective-permute-start | bytes 27656 | tf_op jit(solution)/shard_map/ppermute | solution.py:29
  34.5 6.2 %collective-permute-start.1 = (bf16[4,6,1,64,3]{3,2,4,1,0:T(2,128)(2,1)S(1)}, bf16[4,6,1,64,3]{3,2,4,1,0:T(2,128)(2,1)S(1)}, u32[]{:S(2)}, u32[]{:S(2)}) collective-permute-start(bf16[4,6,1,64,3]{3,2,4,1,0:T(2,128)(2,1)S(1)} %get-tuple-element.43), channel_id=1, source_target_pairs={{0,4},{4,8},{8,12},{1,5},{5,9},{9,13},{2,6},{6,10},{10,14},{3,7},{... | collective-permute-start | bytes 27656 | tf_op jit(solution)/shard_map/ppermute | solution.py:27
  42.8 42.6 %copy-start.14 = (f32[128]{0:T(128)S(1)}, f32[128]{0:T(128)}, u32[]{:S(2)}) copy-start(f32[128]{0:T(128)} %param.15) | copy-start | bytes 1540
  42.8 42.6 %copy-start.15 = (f32[128]{0:T(128)S(1)}, f32[128]{0:T(128)}, u32[]{:S(2)}) copy-start(f32[128]{0:T(128)} %param.16) | copy-start | bytes 1540
  86.1 12.9 %collective-permute-start.3 = (bf16[4,2,4,64,128]{4,3,2,1,0:T(8,128)(2,1)S(1)}, bf16[4,2,4,64,128]{4,3,2,1,0:T(8,128)(2,1)S(1)}, u32[]{:S(2)}, u32[]{:S(2)}) collective-permute-start(bf16[4,2,4,64,128]{4,3,2,1,0:T(8,128)(2,1)S(1)} %slice.357), channel_id=1, source_target_pairs={{0,1},{1,2},{2,3},{4,5},{5,6},{6,7},{8,9},{9,10},{10,11},{12,13},{... | collective-permute-start | bytes 1572872 | tf_op jit(solution)/shard_map/ppermute | solution.py:16
  99.2 9.7 %collective-permute-start.5 = (bf16[4,6,1,64,128]{4,3,2,1,0:T(8,128)(2,1)S(1)}, bf16[4,6,1,64,128]{4,3,2,1,0:T(8,128)(2,1)S(1)}, u32[]{:S(2)}, u32[]{:S(2)}) collective-permute-start(bf16[4,6,1,64,128]{4,3,2,1,0:T(8,128)(2,1)S(1)} %get-tuple-element.40), channel_id=1, source_target_pairs={{4,0},{8,4},{12,8},{5,1},{9,5},{13,9},{6,2},{10,6},{14,10},{7,3},{... | collective-permute-start | bytes 1179656 | tf_op jit(solution)/shard_map/ppermute | solution.py:29
  100.5 9.8 %collective-permute-start.4 = (bf16[4,6,1,64,128]{4,3,2,1,0:T(8,128)(2,1)S(1)}, bf16[4,6,1,64,128]{4,3,2,1,0:T(8,128)(2,1)S(1)}, u32[]{:S(2)}, u32[]{:S(2)}) collective-permute-start(bf16[4,6,1,64,128]{4,3,2,1,0:T(8,128)(2,1)S(1)} %get-tuple-element.39), channel_id=1, source_target_pairs={{0,4},{4,8},{8,12},{1,5},{5,9},{9,13},{2,6},{6,10},{10,14},{3,7},{... | collective-permute-start | bytes 1179656 | tf_op jit(solution)/shard_map/ppermute | solution.py:27
  119.4 1.2 copy-start.1
  119.4 1.5 copy-start.2
  119.4 1.8 copy-start.3
  121.3 1.5 copy-start.8
  127.6 1.3 copy-start.6
  127.6 1.5 copy-start.7
  133.5 1.3 copy-start.4
  133.5 1.5 copy-start.5
  135.1 1.2 copy-start.9
  135.1 1.5 copy-start.10
  137.9 39.0 %copy-start.12 = (f32[256]{0:T(256)S(1)}, f32[256]{0:T(256)}, u32[]{:S(2)}) copy-start(f32[256]{0:T(256)} %param.18) | copy-start | bytes 3076
  137.9 39.0 %copy-start.13 = (f32[256]{0:T(256)S(1)}, f32[256]{0:T(256)}, u32[]{:S(2)}) copy-start(f32[256]{0:T(256)} %param.19) | copy-start | bytes 3076
  234.0 4.8 %copy-start.16 = (f32[256]{0:T(256)S(1)}, f32[256]{0:T(256)}, u32[]{:S(2)}) copy-start(f32[256]{0:T(256)} %param.21) | copy-start | bytes 3076
where the time goes:
time: 241 us; the launch traced here: 240 us
  blocking collectives  72.7 us (30%)
  local copies, waits for them, and re-layouts  71.9 us (30%)
  waiting for transfers between devices  31.3 us (13%)
  starting transfers between devices  27 us (11%)
  other arithmetic  20.1 us (8%)
  matrix products  16.2 us (7%)
    psum x2, blocking collectives, norm_silu(): value_sum, square_sum = lax.psum((value_sum, square_sum), ('row', 'tm'))  72.7 us
    slice x1, local copies, waits for them, and re-layouts, encode(): activated[:, 1::2].astype(jnp.float32)  25.5 us
    slice x1, local copies, waits for them, and re-layouts, encode(): activated[:, 0::2].astype(jnp.float32)  25.4 us
    all_to_all x1, waiting for transfers between devices, local(): lax.all_to_all(packed, 'clip', split_axis=0, concat_axis=0, tiled=True)  13.6 us
    dot_general x9, matrix products, encode(): jnp.dot(tap_strip.reshape(-1, tap_strip.shape[-1]), mixer_weight[time_tap...  13.2 us
    ppermute x2, waiting for transfers between devices, from_behind(): return lax.ppermute(shard, axis, pairs)  12.1 us
    ppermute x2, starting transfers between devices, extended_2(): lax.ppermute(tail, axis, [(i, (i + 1) % count) for i in range(ends)])  9.3 us
    all_to_all x1, starting transfers between devices, local(): lax.all_to_all(packed, 'clip', split_axis=0, concat_axis=0, tiled=True)  8.57 us
  transfers between devices with their start and end apart: 7, of which 6 were waited for; matrix products, arithmetic and copies ran while one was open for 0% of the time, Pallas kernels for 0%

commit v1 on v0

v1 whole, which is shorter than its diff:
```python
import jax
import jax.numpy as jnp
import numpy as np
from jax import lax
from jax.experimental import pallas as pl
from jax.experimental.pallas import tpu as pltpu
from jax.sharding import PartitionSpec as P

GROUPS = 32
COLS = 64
F32 = jnp.float32
BF16 = jnp.bfloat16
eps = 1e-06

VMEM = pl.BlockSpec(memory_space=pltpu.VMEM)
SMEM = pl.BlockSpec(memory_space=pltpu.SMEM)


def iota(shape, dim):
    return lax.broadcasted_iota(jnp.int32, shape, dim)


def pack_kernel(core_ref, keep_a, keep_b, train_ref, fr_a, fr_b, out_ref):
    out_ref[...] = jnp.zeros_like(out_ref)
    core = core_ref[0]
    for keep_ref, fr in ((keep_a, fr_a), (keep_b, fr_b)):
        for j in range(fr.shape[0]):
            k = keep_ref[j]
            t = train_ref[jnp.maximum(k, 0)]
            mine = jnp.logical_and(k >= 0, ((t >> 2) & 1) == core)

            @pl.when(mine)
            def _():
                out_ref[t >> 3, t & 3] = fr[j]


def combine_kernel(recv_ref, out_ref, rows_ref):
    for k in range(4):
        for ch in range(3):
            total = recv_ref[0, k, ch].astype(F32)
            for s in range(1, recv_ref.shape[0]):
                total = total + recv_ref[s, k, ch].astype(F32)
            at = (k * 3 + ch) * 4
            rows_ref[at : at + 4, :] = total
    i = iota((256, 256), 0)
    o = iota((256, 256), 1)
    source = ((o >> 5) & 3) * 64 + (o & 31) * 2 + (o >> 7)
    pick = (i == source).astype(F32).astype(BF16)
    split = jnp.dot(rows_ref[...].astype(BF16), pick, preferred_element_type=F32)
    rows_ref[...] = split
    for k in range(4):
        for ch in range(3):
            at = (k * 3 + ch) * 4
            piece = rows_ref[at : at + 4, :].astype(BF16)
            for y in range(4):
                out_ref[y * 4 + k, ch] = piece


def group_scale(total, square, cells, per_group, gain, shift):
    n = total.shape[1]
    gi = iota((n, n), 0) // per_group
    gj = iota((n, n), 1) // per_group
    member = (gi == gj).astype(F32)
    both = jnp.concatenate([total, square, jnp.zeros((6, n), F32)], axis=0)
    sums = jnp.dot(both, member, precision=lax.Precision.HIGHEST, preferred_element_type=F32)
    sums = sums * (1.0 / (cells * per_group))
    mean = sums[0:1]
    spread = sums[1:2] - mean * mean
    scale = gain * lax.rsqrt(spread + eps)
    return scale, shift - mean * scale


def silu(u):
    half = 0.5 * u
    return half + half * jnp.tanh(half)


def mixer_kernel(
    y_ref, raw_ref, w4_ref, gain_ref, shift_ref, mw_ref, mix_ref, stat_ref, dv, tg, stem, hid
):
    y = y_ref[0]
    for yy in range(4):
        for xx in range(4):
            for ch in range(3):
                piece = raw_ref[yy * 4 + xx, ch].astype(F32)
                for par in range(2):
                    dv[1 + par, ch, 4 + 4 * xx : 8 + 4 * xx, 128 * yy : 128 * yy + 128] = piece[
                        :, 128 * par : 128 * par + 128
                    ]
    pair = iota((16, 512), 1) & 31
    for ch in range(3):
        even = dv[1, ch, 4:20, :]
        odd = dv[2, ch, 4:20, :]
        dv[0, ch, 4:20, :] = jnp.where(pair == 0, 0.0, pltpu.roll(odd, 1, 1))
        dv[3, ch, 4:20, :] = jnp.where(pair == 31, 0.0, pltpu.roll(even, 511, 1))
    for v in range(4):
        for ch in range(3):
            dv[v, ch, 0:4, :] = jnp.broadcast_to(dv[v, ch, 4:5, :], (4, 512))
    edge = jnp.zeros((32, 128), BF16)
    for g in range(4):
        tg[g, 0:32, :] = edge
        tg[g, 544:576, :] = edge
        rows = [dv[v, ch, 4 * g : 4 * g + 8, :] for v in range(4) for ch in range(3)]
        block = jnp.concatenate(rows + [jnp.zeros((32, 512), F32)], axis=0)
        tg[g, 32:544, :] = jnp.transpose(block).astype(BF16)
    total = jnp.zeros((8, 1024), F32)
    square = jnp.zeros((8, 1024), F32)
    for g in range(4):
        stem[g, 0:32, :] = jnp.zeros((32, 1024), F32)
        stem[g, 544:576, :] = jnp.zeros((32, 1024), F32)
        left = jnp.concatenate([tg[g, 32 * b : 32 * b + 512, :] for b in range(3)], axis=1)
        out = jnp.dot(left, w4_ref[...], preferred_element_type=F32)
        stem[g, 32:544, :] = out
        parts = out.reshape(64, 8, 1024)
        total = total + jnp.sum(parts, axis=0)
        square = square + jnp.sum(parts * parts, axis=0)
    total = jnp.sum(total, axis=0, keepdims=True)
    square = jnp.sum(square, axis=0, keepdims=True)
    total = sum(total[:, 128 * k : 128 * k + 128] for k in range(8))
    square = sum(square[:, 128 * k : 128 * k + 128] for k in range(8))
    scale, offset = group_scale(total, square, 16384, 4, gain_ref[...], shift_ref[...])
    at = iota((192, 128), 0)
    row = at >> 5
    valid = jnp.logical_and(
        jnp.logical_or(row > 0, y > 0), jnp.logical_or(row < 5, y < 3)
    )
    first = (at & 31) == 0
    last = (at & 31) == 31
    start = pl.multiple_of(y * 128, 128)
    for f in range(16):
        g, fo = divmod(f, 4)
        val = stem[g, pl.ds(start, 192), 256 * fo : 256 * fo + 256]
        even = jnp.where(valid, silu(val[:, :128] * scale + offset), 0.0)
        odd = jnp.where(valid, silu(val[:, 128:] * scale + offset), 0.0)
        before = jnp.where(first, 0.0, pltpu.roll(odd, 1, 0))
        after = jnp.where(last, 0.0, pltpu.roll(even, 191, 0))
        for k, part in enumerate((before, even, odd, after)):
            part = part.astype(BF16)
            hid[f + 2, :, 128 * k : 128 * k + 128] = part
            if f == 0:
                hid[0, :, 128 * k : 128 * k + 128] = part
                hid[1, :, 128 * k : 128 * k + 128] = part

    def frame(f, carry):
        s, q = carry
        for par in range(2):
            taps = [
                hid[f + a, 32 * b : 32 * b + 128, 128 * par : 128 * par + 384]
                for a in range(3)
                for b in range(3)
            ]
            left = jnp.concatenate(taps, axis=1)
            out = jnp.dot(left, mw_ref[...], preferred_element_type=F32)
            mix_ref[par, f] = out
            parts = out.reshape(16, 8, 256)
            s = s + jnp.sum(parts, axis=0)
            q = q + jnp.sum(parts * parts, axis=0)
        return s, q

    zero = jnp.zeros((8, 256), F32)
    s, q = lax.fori_loop(0, 16, frame, (zero, zero))
    stat_ref[0:1, :] = jnp.sum(s, axis=0, keepdims=True)
    stat_ref[1:2, :] = jnp.sum(q, axis=0, keepdims=True)


def down_kernel(mix_ref, stat_ref, gain_ref, shift_ref, dw_ref, bias_ref, out_ref, left):
    scale, offset = group_scale(
        stat_ref[0:1, :], stat_ref[1:2, :], 16384, 8, gain_ref[...], shift_ref[...]
    )
    for g in range(8):
        for par in range(2):
            one = silu(mix_ref[par, 2 * g] * scale + offset)
            two = silu(mix_ref[par, 2 * g + 1] * scale + offset)
            pooled = ((one + two) * 0.5).astype(BF16)
            for r in range(4):
                lane = ((r & 1) * 2 + par) * 256
                to = g * 64 + (r >> 1) * 32
                left[to : to + 32, lane : lane + 256] = pooled[32 * r : 32 * r + 32]
    out = jnp.dot(left[...], dw_ref[...], preferred_element_type=F32) + bias_ref[...]
    out_ref[...] = out.astype(BF16)


def stem_places():
    place = np.zeros((8, 3, 128, 81), np.float32)
    for fo in range(4):
        for par in range(2):
            for a in range(3):
                for b in range(3):
                    for c in range(3):
                        for ch in range(3):
                            row = (par + c) * 24 + ch * 8 + fo + 2 + a
                            place[fo * 2 + par, b, row, ((a * 3 + b) * 3 + c) * 3 + ch] = 1
    return place.reshape(8, 384, 81)


def call(kernel, out_shape, specs, scratch=(), mib=48):
    return pl.pallas_call(
        kernel,
        out_shape=out_shape,
        in_specs=specs,
        out_specs=jax.tree.map(lambda _: VMEM, out_shape),
        scratch_shapes=list(scratch),
        compiler_params=pltpu.CompilerParams(vmem_limit_bytes=mib << 20),
    )


def local(
    frames,
    keep_list,
    train_slot,
    stem_weight,
    stem_gain,
    stem_shift,
    mixer_weight,
    mixer_gain,
    mixer_shift,
    down_weight,
    down_bias,
):
    sds = jax.ShapeDtypeStruct
    index = lax.axis_index("clip")
    core = (index % 2).astype(jnp.int32).reshape(1)
    row = lax.axis_index("row").astype(jnp.int32).reshape(1)
    pairs = [(i, i ^ 1) for i in range(16)]
    frames_b = lax.ppermute(frames, "clip", pairs)
    keep_b = lax.ppermute(keep_list, "clip", pairs)
    packed = call(
        pack_kernel, sds((8, 4, 3, 4, 256), BF16), [SMEM] * 4 + [VMEM] * 2
    )(core, keep_list, keep_b, train_slot, frames, frames_b)
    along_z = [[2 * z + k for z in range(8)] for k in range(2)]
    received = lax.all_to_all(
        packed, "clip", split_axis=0, concat_axis=0, tiled=True, axis_index_groups=along_z
    )
    pieces = call(
        combine_kernel, sds((16, 3, 4, 256), BF16), [VMEM], [pltpu.VMEM((48, 256), F32)]
    )(received)
    raw = lax.all_to_all(pieces, ("row", "tm"), split_axis=0, concat_axis=0, tiled=True)
    places = jnp.asarray(stem_places(), BF16)
    w4 = jnp.einsum("nkp,pc->knc", places, stem_weight).reshape(384, 1024)
    mix, stat = call(
        mixer_kernel,
        (sds((2, 16, 128, 256), F32), sds((2, 256), F32)),
        [SMEM] + [VMEM] * 5,
        [
            pltpu.VMEM((4, 3, 24, 512), F32),
            pltpu.VMEM((4, 576, 128), BF16),
            pltpu.VMEM((4, 576, 1024), F32),
            pltpu.VMEM((18, 192, 512), BF16),
        ],
    )(
        row,
        raw,
        w4,
        stem_gain.reshape(1, -1),
        stem_shift.reshape(1, -1),
        mixer_weight.reshape(3456, 256),
    )
    stat = lax.psum(stat, "row")
    latent = call(
        down_kernel, sds((512, 256), BF16), [VMEM] * 6, [pltpu.VMEM((512, 1024), BF16)]
    )(
        mix,
        stat,
        mixer_gain.reshape(1, -1),
        mixer_shift.reshape(1, -1),
        down_weight,
        down_bias.reshape(1, -1),
    )
    return lax.all_to_all(
        latent.reshape(4, 2, 2, 32, 256), "tm", split_axis=0, concat_axis=0, tiled=True
    )


def solution(mesh):
    return jax.shard_map(
        local,
        mesh=mesh,
        in_specs=(P("clip", None, "tm", "row"), P("clip")) + (P(),) * 9,
        out_specs=P("clip", "tm", "row", None, None),
        check_vma=False,
    )
```

time: 241 us -> 79.9 us (0.33)
  local copies, waits for them, and re-layouts: 71.9 us -> 7.73 us
  blocking collectives: 72.7 us -> 37.1 us
  waiting for transfers between devices: 31.3 us -> 3.62 us
  Pallas kernels: 0 us -> 20.3 us
  other arithmetic: 20.1 us -> 0 us
  starting transfers between devices: 27 us -> 8.07 us
  matrix products: 16.2 us -> 2.37 us
    psum x2 -> x1, blocking collectives: 72.7 us -> 8.65 us  [local(): stat = lax.psum(stat, 'row')]
    slice x7 -> x0, local copies, waits for them, and re-layouts: 59.1 us -> none  [the longest x1 25.5 us: encode(): activated[:, 1::2].astype(jnp.float32)]
    all_to_all x0 -> x2, blocking collectives: none -> 28.4 us  [the longest x1 19.2 us: local(): lax.all_to_all(packed, 'clip', split_axis=0, concat_axis=0, tiled=True, a...]
    pallas_call x0 -> x4, Pallas kernels: none -> 20.3 us  [the longest x1 17.1 us: local(): call(mixer_kernel, (sds((2, 16, 128, 256), F32), sds((2, 256), F32)), [SM...]
    ppermute x6 -> x2, starting transfers between devices: 18.4 us -> 0.59 us  [the longest x1 0.5 us: local(): keep_b = lax.ppermute(keep_list, 'clip', pairs)]
    ppermute x6 -> x2, waiting for transfers between devices: 17.7 us -> 0.96 us  [the longest x1 0.95 us: local(): keep_b = lax.ppermute(keep_list, 'clip', pairs)]
    dot_general x12 -> x1, matrix products: 16.2 us -> 2.37 us  [local(): w4 = jnp.einsum('nkp,pc->knc', places, stem_weight).reshape(384, 1024)]
    all_to_all x1, waiting for transfers between devices: 13.6 us -> 2.66 us  [local(): lax.all_to_all(pieces, ('row', 'tm'), split_axis=0, concat_axis=0, tiled=...]
  transfers between devices with their start and end apart: 7 -> 3, of which waited for: 6 -> 2; matrix products, arithmetic and copies ran while one was open for 0% -> 5% of each run, Pallas kernels for 0% -> 0%
where the time goes in v1:
time: 79.9 us; the launch traced here: 79.2 us
  blocking collectives  37.1 us (46%)
  Pallas kernels  20.3 us (25%)
  starting transfers between devices  8.07 us (10%)
  local copies, waits for them, and re-layouts  7.73 us (10%)
  waiting for transfers between devices  3.62 us (5%)
  matrix products  2.37 us (3%)
    all_to_all x1, blocking collectives, local(): lax.all_to_all(packed, 'clip', split_axis=0, concat_axis=0, tiled=True, a...  19.2 us
    pallas_call x1, Pallas kernels, local(): call(mixer_kernel, (sds((2, 16, 128, 256), F32), sds((2, 256), F32)), [SM...  17.1 us
    all_to_all x1, blocking collectives, local(): lax.all_to_all(latent.reshape(4, 2, 2, 32, 256), 'tm', split_axis=0, conc...  9.18 us
    psum x1, blocking collectives, local(): stat = lax.psum(stat, 'row')  8.65 us
    all_to_all x1, starting transfers between devices, local(): lax.all_to_all(pieces, ('row', 'tm'), split_axis=0, concat_axis=0, tiled=...  7.48 us
    unnamed x25, local copies, waits for them, and re-layouts  6.33 us
    all_to_all x1, waiting for transfers between devices, local(): lax.all_to_all(pieces, ('row', 'tm'), split_axis=0, concat_axis=0, tiled=...  2.66 us
    dot_general x1, matrix products, local(): w4 = jnp.einsum('nkp,pc->knc', places, stem_weight).reshape(384, 1024)  2.37 us
  transfers between devices with their start and end apart: 3, of which 2 were waited for; matrix products, arithmetic and copies ran while one was open for 5% of the time, Pallas kernels for 0%

profile of v1, /device:TPU:2, one launch (start us, length us, event | category | flops | bytes accessed | tf_op | source)
XLA Modules:
  0.0 79.2 jit_solution(683297955685677038)
XLA Ops:
  0.0 0.1 collective-permute-start.1
  0.1 0.5 collective-permute-start
  0.6 1.0 %collective-permute-done.keep_b = s32[8]{0:T(128)S(1)} collective-permute-done((s32[8]{0:T(128)}, s32[8]{0:T(128)S(1)}, u32[]{:S(2)}, u32[]{:S(2)}) %collective-permute-start) | collective-permute-done | bytes 64 | tf_op jit(solution)/shard_map/ppermute | solution.py:226
  1.6 0.0 collective-permute-done.1.fr_b
  1.6 0.8 %copy-done.4 = bf16[8,3,4,256]{3,2,1,0:T(4,128)(2,1)S(1)} copy-done((bf16[8,3,4,256]{3,2,1,0:T(4,128)(2,1)S(1)}, bf16[8,3,4,256]{3,2,1,0:T(4,128)(2,1)}, u32[]{:S(2)}) %copy-start.4) | copy-done | bytes 49176
  2.4 0.7 copy-done.8
  3.0 0.7 copy-done.9
  3.7 0.8 %shard_map.118 = bf16[8,4,3,4,256]{4,3,2,1,0:T(4,128)(2,1)S(1)} custom-call(s32[1]{0:T(128)} %bitcast.1.core_ref, s32[8]{0:T(128)S(1)} %copy-done.8, s32[8]{0:T(128)S(1)} %collective-permute-done.keep_b, s32[64]{0:T(128)S(1)} %copy-done.9, bf16[8,3,4,256]{3,2,1,0:T(4,128)(2,1)S(1)} %copy-done.4, bf16[8,3,4,256]{3,2,1,0:T(4,128)(2,1)S(1)} %collective-permute-done.1.fr_b), custom_call_target="tpu_custom_call" | custom-call | tf_op jit(solution)/shard_map/pallas_call | solution.py:227
  4.5 19.2 %all_to_all.15.recv_ref = bf16[8,4,3,4,256]{4,3,2,1,0:T(4,128)(2,1)S(1)} all-to-all(bf16[8,4,3,4,256]{4,3,2,1,0:T(4,128)(2,1)S(1)} %shard_map.118), channel_id=1, replica_groups={{0,32,64,96,128,160,192,224},{16,48,80,112,144,176,208,240},{1,33,65,97..., dimensions={0} | all-to-all | bytes 393216 | tf_op jit(solution)/shard_map/all_to_all | solution.py:231
  23.7 0.8 %shard_map.119 = bf16[16,3,4,256]{3,2,1,0:T(4,128)(2,1)} custom-call(bf16[8,4,3,4,256]{4,3,2,1,0:T(4,128)(2,1)S(1)} %all_to_all.15.recv_ref), custom_call_target="tpu_custom_call" | custom-call | tf_op jit(solution)/shard_map/pallas_call | solution.py:234
  24.6 7.5 %all-to-all-start.1 = ((bf16[16,3,4,256]{3,2,1,0:T(4,128)(2,1)}), bf16[16,3,4,256]{3,2,1,0:T(4,128)(2,1)S(1)}, u32[]{:S(2)}, u32[]{:S(2)}) async-start(bf16[16,3,4,256]{3,2,1,0:T(4,128)(2,1)} %shard_map.119), calls=%async_computation.1 | async-start | bytes 196608 | tf_op jit(solution)/shard_map/all_to_all | solution.py:237
  32.0 0.0 copy-done
  32.1 2.4 %fusion = bf16[8,384,128]{1,2,0:T(8,128)(2,1)} fusion(bf16[8,384,81]{1,2,0:T(8,128)(2,1)} %constant.25.clone, bf16[81,128]{1,0:T(8,128)(2,1)S(1)} %copy-done), kind=kOutput, calls=%fused_computation | convolution fusion | flops 63700992 | bytes 1304832 | tf_op jit(solution)/shard_map/nkp,pc->knc/dot_general | solution.py:239
  34.4 1.4 %copy.14.w4_ref = bf16[384,1024]{1,0:T(8,128)(2,1)S(1)} copy(bf16[384,1024]{0,1:T(8,128)(2,1)} %bitcast.23) | data formatting | bytes 1572864 | tf_op jit(solution)/shard_map/reshape | solution.py:239
  35.8 2.7 %all-to-all-done.1.raw_ref = bf16[16,3,4,256]{3,2,1,0:T(4,128)(2,1)S(1)} async-done(((bf16[16,3,4,256]{3,2,1,0:T(4,128)(2,1)}), bf16[16,3,4,256]{3,2,1,0:T(4,128)(2,1)S(1)}, u32[]{:S(2)}, u32[]{:S(2)}) %all-to-all-start.1) | async-done | bytes 98336 | tf_op jit(solution)/shard_map/all_to_all | solution.py:237
  38.5 0.7 copy-done.10
  39.2 0.7 copy-done.11
  39.8 17.1 %shard_map.120 = (f32[2,16,128,256]{3,2,1,0:T(8,128)}, f32[2,256]{1,0:T(2,128)S(1)}) custom-call(s32[1]{0:T(128)} %bitcast.y_ref, bf16[16,3,4,256]{3,2,1,0:T(4,128)(2,1)S(1)} %all-to-all-done.1.raw_ref, bf16[384,1024]{1,0:T(8,128)(2,1)S(1)} %copy.14.w4_ref, f32[1,128]{1,0:T(1,128)S(1)} %bitcast.21, f32[1,128]{1,0:T(1,128)S(1)} %bitcast.22, ...), custom_call_target="tpu_custom_call" | custom-call | tf_op jit(solution)/shard_map/pallas_call | solution.py:240
  56.9 8.6 %psum.7.stat_ref = f32[2,256]{1,0:T(2,128)S(1)} all-reduce(f32[2,256]{1,0:T(2,128)S(1)} %get-tuple-element.8), channel_id=1, replica_groups=mesh['clip'=16,'row'=4,'tm'=4] {'row'}, use_global_device_ids=true, to_apply=%region_0.1 | all-reduce | flops 512 | bytes 4096 | tf_op jit(solution)/shard_map/psum | solution.py:258
  65.5 0.0 copy-done.3
  65.6 2.2 %copy-done.1 = f32[2,16,128,256]{3,2,1,0:T(8,128)S(1)} copy-done((f32[2,16,128,256]{3,2,1,0:T(8,128)S(1)}, f32[2,16,128,256]{3,2,1,0:T(8,128)}, u32[]{:S(2)}) %copy-start.1) | copy-done | bytes 4194328
  67.8 1.6 %shard_map.121 = bf16[512,256]{1,0:T(8,128)(2,1)S(1)} custom-call(f32[2,16,128,256]{3,2,1,0:T(8,128)S(1)} %copy-done.1, f32[2,256]{1,0:T(2,128)S(1)} %psum.7.stat_ref, f32[1,256]{1,0:T(1,128)S(1)} %bitcast.18, f32[1,256]{1,0:T(1,128)S(1)} %bitcast.19, bf16[1024,256]{1,0:T(8,128)(2,1)S(1)} %copy-done.3, f32[1,256]{1,0:T(1,128)S(1)} %bitcast.20), custom_call_target="tpu_custom_call" | custom-call | tf_op jit(solution)/shard_map/pallas_call | solution.py:259
  69.3 9.2 %all_to_all.16 = bf16[4,2,2,32,256]{4,3,2,1,0:T(8,128)(2,1)S(1)} all-to-all(bf16[4,2,2,32,256]{4,3,2,1,0:T(8,128)(2,1)S(1)} %bitcast.17), channel_id=1, replica_groups=mesh['clip'=16,'row'=4,'tm'=4] {'tm'}, dimensions={0} | all-to-all | bytes 524288 | tf_op jit(solution)/shard_map/all_to_all | solution.py:269
  78.5 0.7 copy.16
  (16 shorter events, 0.0 us)
Async XLA Ops:
  0.0 32.0 %copy-start = (bf16[81,128]{1,0:T(8,128)(2,1)S(1)}, bf16[81,128]{1,0:T(8,128)(2,1)}, u32[]{:S(2)}) copy-start(bf16[81,128]{1,0:T(8,128)(2,1)} %param.15) | copy-start | bytes 62212
  0.0 38.5 %copy-start.2 = (bf16[3,3,384,256]{3,2,1,0:T(8,128)(2,1)S(1)}, bf16[3,3,384,256]{3,2,1,0:T(8,128)(2,1)}, u32[]{:S(2)}) copy-start(bf16[3,3,384,256]{3,2,1,0:T(8,128)(2,1)} %param.18) | copy-start | bytes 5308420
  0.0 65.5 %copy-start.3 = (bf16[1024,256]{1,0:T(8,128)(2,1)S(1)}, bf16[1024,256]{1,0:T(8,128)(2,1)}, u32[]{:S(2)}) copy-start(bf16[1024,256]{1,0:T(8,128)(2,1)} %dw_ref.1) | copy-start | bytes 1572868
  0.0 1.6 %collective-permute-start.1 = (bf16[8,3,4,256]{3,2,1,0:T(4,128)(2,1)}, bf16[8,3,4,256]{3,2,1,0:T(4,128)(2,1)S(1)}, u32[]{:S(2)}, u32[]{:S(2)}) collective-permute-start(bf16[8,3,4,256]{3,2,1,0:T(4,128)(2,1)} %fr_a.1), channel_id=1, source_target_pairs={{0,16},{16,0},{32,48},{48,32},{64,80},{80,64},{96,112},{112,96},{1... | collective-permute-start | bytes 147464 | tf_op jit(solution)/shard_map/ppermute | solution.py:225
  0.1 1.5 %collective-permute-start = (s32[8]{0:T(128)}, s32[8]{0:T(128)S(1)}, u32[]{:S(2)}, u32[]{:S(2)}) collective-permute-start(s32[8]{0:T(128)} %keep_a.1), channel_id=1, source_target_pairs={{0,16},{16,0},{32,48},{48,32},{64,80},{80,64},{96,112},{112,96},{1... | collective-permute-start | bytes 104 | tf_op jit(solution)/shard_map/ppermute | solution.py:226
  1.6 0.8 %copy-start.4 = (bf16[8,3,4,256]{3,2,1,0:T(4,128)(2,1)S(1)}, bf16[8,3,4,256]{3,2,1,0:T(4,128)(2,1)}, u32[]{:S(2)}) copy-start(bf16[8,3,4,256]{3,2,1,0:T(4,128)(2,1)} %fr_a.1) | copy-start | bytes 147460
  2.4 0.7 copy-start.8
  3.0 0.7 copy-start.9
  3.7 61.9 %copy-start.5 = (f32[256]{0:T(256)S(1)}, f32[256]{0:T(256)}, u32[]{:S(2)}) copy-start(f32[256]{0:T(256)} %param.19) | copy-start | bytes 3076
  3.7 61.9 %copy-start.6 = (f32[256]{0:T(256)S(1)}, f32[256]{0:T(256)}, u32[]{:S(2)}) copy-start(f32[256]{0:T(256)} %param.20) | copy-start | bytes 3076
  3.7 61.9 %copy-start.7 = (f32[256]{0:T(256)S(1)}, f32[256]{0:T(256)}, u32[]{:S(2)}) copy-start(f32[256]{0:T(256)} %param.22) | copy-start | bytes 3076
  24.6 13.9 %all-to-all-start.1 = ((bf16[16,3,4,256]{3,2,1,0:T(4,128)(2,1)}), bf16[16,3,4,256]{3,2,1,0:T(4,128)(2,1)S(1)}, u32[]{:S(2)}, u32[]{:S(2)}) async-start(bf16[16,3,4,256]{3,2,1,0:T(4,128)(2,1)} %shard_map.119), calls=%async_computation.1 | async-start | bytes 196608 | tf_op jit(solution)/shard_map/all_to_all | solution.py:237
  38.5 0.7 copy-start.10
  39.2 0.7 copy-start.11
  65.6 2.2 %copy-start.1 = (f32[2,16,128,256]{3,2,1,0:T(8,128)S(1)}, f32[2,16,128,256]{3,2,1,0:T(8,128)}, u32[]{:S(2)}) copy-start(f32[2,16,128,256]{3,2,1,0:T(8,128)} %get-tuple-element.7.mix_ref) | copy-start | bytes 12582916

commit v2 on v1

--- a/solution.py
+++ b/solution.py
@@ -14,19 +14,29 @@
 
 VMEM = pl.BlockSpec(memory_space=pltpu.VMEM)
 SMEM = pl.BlockSpec(memory_space=pltpu.SMEM)
+ANY = pl.BlockSpec(memory_space=pl.ANY)
+HBM = pl.BlockSpec(memory_space=pltpu.HBM)
 
 
 def iota(shape, dim):
     return lax.broadcasted_iota(jnp.int32, shape, dim)
 
 
-def pack_kernel(core_ref, keep_a, keep_b, train_ref, fr_a, fr_b, out_ref):
+def pack_kernel(
+    core_ref, keep_a, keep_b, train, fr_a, fr_b, out_ref, keep_s, keep_t, train_s, fra, frb, sems
+):
+    pairs = ((keep_a, keep_s), (keep_b, keep_t), (train, train_s), (fr_a, fra), (fr_b, frb))
+    copies = [pltpu.make_async_copy(src, dst, sems.at[i]) for i, (src, dst) in enumerate(pairs)]
+    for copy in copies:
+        copy.start()
     out_ref[...] = jnp.zeros_like(out_ref)
+    for copy in copies:
+        copy.wait()
     core = core_ref[0]
-    for keep_ref, fr in ((keep_a, fr_a), (keep_b, fr_b)):
+    for keep_ref, fr in ((keep_s, fra), (keep_t, frb)):
         for j in range(fr.shape[0]):
             k = keep_ref[j]
-            t = train_ref[jnp.maximum(k, 0)]
+            t = train_s[jnp.maximum(k, 0)]
             mine = jnp.logical_and(k >= 0, ((t >> 2) & 1) == core)
 
             @pl.when(mine)
@@ -76,9 +86,29 @@
 
 
 def mixer_kernel(
-    y_ref, raw_ref, w4_ref, gain_ref, shift_ref, mw_ref, mix_ref, stat_ref, dv, tg, stem, hid
+    y_ref,
+    raw_ref,
+    w4_ref,
+    gain_hbm,
+    shift_hbm,
+    mw_ref,
+    mix_ref,
+    stat_ref,
+    dv,
+    tg,
+    stem,
+    hid,
+    gain_ref,
+    shift_ref,
+    sems,
 ):
     y = y_ref[0]
+    copies = [
+        pltpu.make_async_copy(gain_hbm, gain_ref, sems.at[0]),
+        pltpu.make_async_copy(shift_hbm, shift_ref, sems.at[1]),
+    ]
+    for copy in copies:
+        copy.start()
     for yy in range(4):
         for xx in range(4):
             for ch in range(3):
@@ -109,7 +139,8 @@
         stem[g, 0:32, :] = jnp.zeros((32, 1024), F32)
         stem[g, 544:576, :] = jnp.zeros((32, 1024), F32)
         left = jnp.concatenate([tg[g, 32 * b : 32 * b + 512, :] for b in range(3)], axis=1)
-        out = jnp.dot(left, w4_ref[...], preferred_element_type=F32)
+        w4 = jnp.concatenate([w4_ref[n] for n in range(8)], axis=1)
+        out = jnp.dot(left, w4, preferred_element_type=F32)
         stem[g, 32:544, :] = out
         parts = out.reshape(64, 8, 1024)
         total = total + jnp.sum(parts, axis=0)
@@ -118,6 +149,8 @@
     square = jnp.sum(square, axis=0, keepdims=True)
     total = sum(total[:, 128 * k : 128 * k + 128] for k in range(8))
     square = sum(square[:, 128 * k : 128 * k + 128] for k in range(8))
+    for copy in copies:
+        copy.wait()
     scale, offset = group_scale(total, square, 16384, 4, gain_ref[...], shift_ref[...])
     at = iota((192, 128), 0)
     row = at >> 5
@@ -163,9 +196,10 @@
     stat_ref[1:2, :] = jnp.sum(q, axis=0, keepdims=True)
 
 
-def down_kernel(mix_ref, stat_ref, gain_ref, shift_ref, dw_ref, bias_ref, out_ref, left):
+def down_kernel(mix_ref, stat_a, stat_b, stat_c, stat_d, gain_ref, shift_ref, dw_ref, bias_ref, out_ref, left):
+    stat = (stat_a[...] + stat_b[...]) + (stat_c[...] + stat_d[...])
     scale, offset = group_scale(
-        stat_ref[0:1, :], stat_ref[1:2, :], 16384, 8, gain_ref[...], shift_ref[...]
+        stat[0:1, :], stat[1:2, :], 16384, 8, gain_ref[...], shift_ref[...]
     )
     for g in range(8):
         for par in range(2):
@@ -190,10 +224,10 @@
                         for ch in range(3):
                             row = (par + c) * 24 + ch * 8 + fo + 2 + a
                             place[fo * 2 + par, b, row, ((a * 3 + b) * 3 + c) * 3 + ch] = 1
-    return place.reshape(8, 384, 81)
-
-
-def call(kernel, out_shape, specs, scratch=(), mib=48):
+    return place.reshape(3072, 81)
+
+
+def call(kernel, out_shape, specs, scratch=(), mib=16):
     return pl.pallas_call(
         kernel,
         out_shape=out_shape,
@@ -225,7 +259,17 @@
     frames_b = lax.ppermute(frames, "clip", pairs)
     keep_b = lax.ppermute(keep_list, "clip", pairs)
     packed = call(
-        pack_kernel, sds((8, 4, 3, 4, 256), BF16), [SMEM] * 4 + [VMEM] * 2
+        pack_kernel,
+        sds((8, 4, 3, 4, 256), BF16),
+        [SMEM, HBM, ANY, HBM, HBM, ANY],
+        [
+            pltpu.SMEM((8,), jnp.int32),
+            pltpu.SMEM((8,), jnp.int32),
+            pltpu.SMEM((64,), jnp.int32),
+            pltpu.VMEM((8, 3, 4, 256), BF16),
+            pltpu.VMEM((8, 3, 4, 256), BF16),
+            pltpu.SemaphoreType.DMA((5,)),
+        ],
     )(core, keep_list, keep_b, train_slot, frames, frames_b)
     along_z = [[2 * z + k for z in range(8)] for k in range(2)]
     received = lax.all_to_all(
@@ -234,33 +278,41 @@
     pieces = call(
         combine_kernel, sds((16, 3, 4, 256), BF16), [VMEM], [pltpu.VMEM((48, 256), F32)]
     )(received)
+    places = jnp.asarray(stem_places(), BF16)
+    w4 = jnp.dot(places, stem_weight, preferred_element_type=F32).astype(BF16)
+    pieces, w4 = lax.optimization_barrier((pieces, w4))
     raw = lax.all_to_all(pieces, ("row", "tm"), split_axis=0, concat_axis=0, tiled=True)
-    places = jnp.asarray(stem_places(), BF16)
-    w4 = jnp.einsum("nkp,pc->knc", places, stem_weight).reshape(384, 1024)
     mix, stat = call(
         mixer_kernel,
         (sds((2, 16, 128, 256), F32), sds((2, 256), F32)),
-        [SMEM] + [VMEM] * 5,
+        [SMEM, VMEM, VMEM, HBM, HBM, VMEM],
         [
             pltpu.VMEM((4, 3, 24, 512), F32),
             pltpu.VMEM((4, 576, 128), BF16),
             pltpu.VMEM((4, 576, 1024), F32),
             pltpu.VMEM((18, 192, 512), BF16),
+            pltpu.VMEM((1, 128), F32),
+            pltpu.VMEM((1, 128), F32),
+            pltpu.SemaphoreType.DMA((2,)),
         ],
+        mib=24,
     )(
         row,
         raw,
-        w4,
+        w4.reshape(8, 384, 128),
         stem_gain.reshape(1, -1),
         stem_shift.reshape(1, -1),
         mixer_weight.reshape(3456, 256),
     )
-    stat = lax.psum(stat, "row")
+    others = [
+        lax.ppermute(stat, "row", [(i, (i + by) % 4) for i in range(4)]) for by in (1, 2, 3)
+    ]
     latent = call(
-        down_kernel, sds((512, 256), BF16), [VMEM] * 6, [pltpu.VMEM((512, 1024), BF16)]
+        down_kernel, sds((512, 256), BF16), [VMEM] * 9, [pltpu.VMEM((512, 1024), BF16)], mib=16
     )(
         mix,
         stat,
+        *others,
         mixer_gain.reshape(1, -1),
         mixer_shift.reshape(1, -1),
         down_weight,

time: 79.9 us -> 73.8 us (0.924)
  blocking collectives: 37.1 us -> 9.23 us
  waiting for transfers between devices: 3.62 us -> 21.6 us
  starting transfers between devices: 8.07 us -> 19.1 us
  local copies, waits for them, and re-layouts: 7.73 us -> 2.85 us
  Pallas kernels: 20.3 us -> 19.1 us
  matrix products: 2.37 us -> 1.48 us
    all_to_all x1 -> x0, blocking collectives: 19.2 us -> none  [local(): lax.all_to_all(packed, 'clip', split_axis=0, concat_axis=0, tiled=True, a...]
    all_to_all x0 -> x1, waiting for transfers between devices: none -> 9.44 us  [local(): lax.all_to_all(packed, 'clip', split_axis=0, concat_axis=0, tiled=True, a...]
    psum x1 -> x0, blocking collectives: 8.65 us -> none  [local(): stat = lax.psum(stat, 'row')]
    all_to_all x0 -> x1, starting transfers between devices: none -> 8.48 us  [local(): lax.all_to_all(packed, 'clip', split_axis=0, concat_axis=0, tiled=True, a...]
    ppermute x0 -> x3, waiting for transfers between devices: none -> 4.72 us  [local(): lax.ppermute(stat, 'row', [(i, (i + by) % 4) for i in range(4)])]
    all_to_all x1, waiting for transfers between devices: 2.66 us -> 6.45 us  [local(): lax.all_to_all(pieces, ('row', 'tm'), split_axis=0, concat_axis=0, tiled=...]
    unnamed x25 -> x23, local copies, waits for them, and re-layouts: 6.33 us -> 2.85 us
    ppermute x0 -> x3, starting transfers between devices: none -> 2.61 us  [local(): lax.ppermute(stat, 'row', [(i, (i + by) % 4) for i in range(4)])]
  transfers between devices with their start and end apart: 3 -> 7, of which waited for: 2 -> 6; matrix products, arithmetic and copies ran while one was open for 5% -> 2% of each run, Pallas kernels for 0% -> 0%
where the time goes in v2:
time: 73.8 us; the launch traced here: 73.4 us
  waiting for transfers between devices  21.6 us (29%)
  starting transfers between devices  19.1 us (26%)
  Pallas kernels  19.1 us (26%)
  blocking collectives  9.23 us (13%)
  local copies, waits for them, and re-layouts  2.85 us (4%)
  matrix products  1.48 us (2%)
    pallas_call x1, Pallas kernels, local(): call(mixer_kernel, (sds((2, 16, 128, 256), F32), sds((2, 256), F32)), [SM...  15.2 us
    all_to_all x1, waiting for transfers between devices, local(): lax.all_to_all(packed, 'clip', split_axis=0, concat_axis=0, tiled=True, a...  9.44 us
    all_to_all x1, blocking collectives, local(): lax.all_to_all(latent.reshape(4, 2, 2, 32, 256), 'tm', split_axis=0, conc...  9.23 us
    all_to_all x1, starting transfers between devices, local(): lax.all_to_all(packed, 'clip', split_axis=0, concat_axis=0, tiled=True, a...  8.48 us
    all_to_all x1, starting transfers between devices, local(): lax.all_to_all(pieces, ('row', 'tm'), split_axis=0, concat_axis=0, tiled=...  7.48 us
    all_to_all x1, waiting for transfers between devices, local(): lax.all_to_all(pieces, ('row', 'tm'), split_axis=0, concat_axis=0, tiled=...  6.45 us
    ppermute x3, waiting for transfers between devices, local(): lax.ppermute(stat, 'row', [(i, (i + by) % 4) for i in range(4)])  4.72 us
    unnamed x23, local copies, waits for them, and re-layouts  2.85 us
  transfers between devices with their start and end apart: 7, of which 6 were waited for; matrix products, arithmetic and copies ran while one was open for 2% of the time, Pallas kernels for 0%

profile of v2, /device:TPU:2, one launch (start us, length us, event | category | flops | bytes accessed | tf_op | source)
XLA Modules:
  0.0 73.4 jit_solution(3769811583755089835)
XLA Ops:
  0.0 0.5 collective-permute-start
  0.5 1.0 %collective-permute-done.keep_b = s32[8]{0:T(128)S(1)} collective-permute-done((s32[8]{0:T(128)}, s32[8]{0:T(128)S(1)}, u32[]{:S(2)}, u32[]{:S(2)}) %collective-permute-start) | collective-permute-done | bytes 64 | tf_op jit(solution)/shard_map/ppermute | solution.py:260
  1.5 0.8 %copy-done.3 = bf16[8,3,4,256]{3,2,1,0:T(4,128)(2,1)S(1)} copy-done((bf16[8,3,4,256]{3,2,1,0:T(4,128)(2,1)S(1)}, bf16[8,3,4,256]{3,2,1,0:T(4,128)(2,1)}, u32[]{:S(2)}) %copy-start.3) | copy-done | bytes 49176
  2.3 0.7 copy-done.7
  2.9 0.7 copy-done.8
  3.6 1.5 %shard_map.118 = bf16[8,4,3,4,256]{4,3,2,1,0:T(4,128)(2,1)} custom-call(s32[1]{0:T(128)} %bitcast.1.core_ref, s32[8]{0:T(128)S(1)} %copy-done.7, s32[8]{0:T(128)S(1)} %collective-permute-done.keep_b, s32[64]{0:T(128)S(1)} %copy-done.8, bf16[8,3,4,256]{3,2,1,0:T(4,128)(2,1)S(1)} %copy-done.3, bf16[8,3,4,256]{3,2,1,0:T(4,128)(2,1)S(1)} %collective-permute-done.1.fr_b), custom_call_target="tpu_custom_call" | custom-call | tf_op jit(solution)/shard_map/pallas_call | solution.py:261
  5.1 8.5 %all-to-all-start = ((bf16[8,4,3,4,256]{4,3,2,1,0:T(4,128)(2,1)}), bf16[8,4,3,4,256]{4,3,2,1,0:T(4,128)(2,1)S(1)}, u32[]{:S(2)}, u32[]{:S(2)}) async-start(bf16[8,4,3,4,256]{4,3,2,1,0:T(4,128)(2,1)} %shard_map.118), calls=%async_computation | async-start | bytes 393216 | tf_op jit(solution)/shard_map/all_to_all | solution.py:275
  13.6 1.5 %convolution_convert_fusion = bf16[3072,128]{1,0:T(8,128)(2,1)S(1)} fusion(bf16[3072,81]{1,0:T(8,128)(2,1)} %constant.25.clone, bf16[81,128]{1,0:T(8,128)(2,1)S(1)} %copy-done), kind=kOutput, calls=%fused_computation | convolution fusion | flops 64094208 | bytes 1304832 | tf_op jit(solution)/shard_map/dot_general | solution.py:282
  15.1 0.0 copy-start.4
  15.1 0.0 copy-start.5
  15.1 9.4 %all-to-all-done.recv_ref = bf16[8,4,3,4,256]{4,3,2,1,0:T(4,128)(2,1)S(1)} async-done(((bf16[8,4,3,4,256]{4,3,2,1,0:T(4,128)(2,1)}), bf16[8,4,3,4,256]{4,3,2,1,0:T(4,128)(2,1)S(1)}, u32[]{:S(2)}, u32[]{:S(2)}) %all-to-all-start) | async-done | bytes 196640 | tf_op jit(solution)/shard_map/all_to_all | solution.py:275
  24.6 0.8 %shard_map.119 = bf16[16,3,4,256]{3,2,1,0:T(4,128)(2,1)} custom-call(bf16[8,4,3,4,256]{4,3,2,1,0:T(4,128)(2,1)S(1)} %all-to-all-done.recv_ref), custom_call_target="tpu_custom_call" | custom-call | tf_op jit(solution)/shard_map/pallas_call | solution.py:278
  25.4 7.5 %all-to-all-start.1 = ((bf16[16,3,4,256]{3,2,1,0:T(4,128)(2,1)}), bf16[16,3,4,256]{3,2,1,0:T(4,128)(2,1)S(1)}, u32[]{:S(2)}, u32[]{:S(2)}) async-start(bf16[16,3,4,256]{3,2,1,0:T(4,128)(2,1)} %shard_map.119), calls=%async_computation.1 | async-start | bytes 196608 | tf_op jit(solution)/shard_map/all_to_all | solution.py:284
  32.9 6.5 %all-to-all-done.1.raw_ref = bf16[16,3,4,256]{3,2,1,0:T(4,128)(2,1)S(1)} async-done(((bf16[16,3,4,256]{3,2,1,0:T(4,128)(2,1)}), bf16[16,3,4,256]{3,2,1,0:T(4,128)(2,1)S(1)}, u32[]{:S(2)}, u32[]{:S(2)}) %all-to-all-start.1) | async-done | bytes 98336 | tf_op jit(solution)/shard_map/all_to_all | solution.py:284
  39.3 15.2 %shard_map.120 = (f32[2,16,128,256]{3,2,1,0:T(8,128)S(1)}, f32[2,256]{1,0:T(2,128)S(1)}) custom-call(s32[1]{0:T(128)} %bitcast.y_ref, bf16[16,3,4,256]{3,2,1,0:T(4,128)(2,1)S(1)} %all-to-all-done.1.raw_ref, bf16[8,384,128]{2,1,0:T(8,128)(2,1)S(1)} %bitcast.12, f32[1,128]{1,0:T(1,128)S(1)} %bitcast.18, f32[1,128]{1,0:T(1,128)S(1)} %bitcast.19, ...), custom_call_target="tpu_custom_call" | custom-call | tf_op jit(solution)/shard_map/pallas_call | solution.py:285
  54.5 1.1 %collective-permute-start.4 = (f32[2,256]{1,0:T(2,128)S(1)}, f32[2,256]{1,0:T(2,128)S(1)}, u32[]{:S(2)}, u32[]{:S(2)}) collective-permute-start(f32[2,256]{1,0:T(2,128)S(1)} %get-tuple-element.12.stat_a), channel_id=1, source_target_pairs={{0,12},{4,0},{8,4},{12,8},{1,13},{5,1},{9,5},{13,9},{2,14},{6,2},{... | collective-permute-start | bytes 6152 | tf_op jit(solution)/shard_map/ppermute | solution.py:308
  55.6 1.4 %collective-permute-start.3 = (f32[2,256]{1,0:T(2,128)S(1)}, f32[2,256]{1,0:T(2,128)S(1)}, u32[]{:S(2)}, u32[]{:S(2)}) collective-permute-start(f32[2,256]{1,0:T(2,128)S(1)} %get-tuple-element.12.stat_a), channel_id=1, source_target_pairs={{0,8},{4,12},{8,0},{12,4},{1,9},{5,13},{9,1},{13,5},{2,10},{6,14},... | collective-permute-start | bytes 6152 | tf_op jit(solution)/shard_map/ppermute | solution.py:308
  57.1 0.1 collective-permute-start.2
  57.1 1.0 %collective-permute-done.4.stat_d = f32[2,256]{1,0:T(2,128)S(1)} collective-permute-done((f32[2,256]{1,0:T(2,128)S(1)}, f32[2,256]{1,0:T(2,128)S(1)}, u32[]{:S(2)}, u32[]{:S(2)}) %collective-permute-start.4) | collective-permute-done | bytes 2080 | tf_op jit(solution)/shard_map/ppermute | solution.py:308
  58.2 2.6 %collective-permute-done.3.stat_c = f32[2,256]{1,0:T(2,128)S(1)} collective-permute-done((f32[2,256]{1,0:T(2,128)S(1)}, f32[2,256]{1,0:T(2,128)S(1)}, u32[]{:S(2)}, u32[]{:S(2)}) %collective-permute-start.3) | collective-permute-done | bytes 2080 | tf_op jit(solution)/shard_map/ppermute | solution.py:308
  60.7 1.1 %collective-permute-done.2.stat_b = f32[2,256]{1,0:T(2,128)S(1)} collective-permute-done((f32[2,256]{1,0:T(2,128)S(1)}, f32[2,256]{1,0:T(2,128)S(1)}, u32[]{:S(2)}, u32[]{:S(2)}) %collective-permute-start.2) | collective-permute-done | bytes 2080 | tf_op jit(solution)/shard_map/ppermute | solution.py:308
  61.9 1.6 %shard_map.121 = bf16[512,256]{1,0:T(8,128)(2,1)S(1)} custom-call(f32[2,16,128,256]{3,2,1,0:T(8,128)S(1)} %get-tuple-element.11.mix_ref, f32[2,256]{1,0:T(2,128)S(1)} %get-tuple-element.12.stat_a, f32[2,256]{1,0:T(2,128)S(1)} %collective-permute-done.2.stat_b, f32[2,256]{1,0:T(2,128)S(1)} %collective-permute-done.3.stat_c, ...), custom_call_target="tpu_custom_call" | custom-call | tf_op jit(solution)/shard_map/pallas_call | solution.py:310
  63.4 9.2 %all_to_all.15 = bf16[4,2,2,32,256]{4,3,2,1,0:T(8,128)(2,1)S(1)} all-to-all(bf16[4,2,2,32,256]{4,3,2,1,0:T(8,128)(2,1)S(1)} %bitcast.14), channel_id=1, replica_groups=mesh['clip'=16,'row'=4,'tm'=4] {'tm'}, dimensions={0} | all-to-all | bytes 524288 | tf_op jit(solution)/shard_map/all_to_all | solution.py:321
  72.7 0.7 copy.14
  (19 shorter events, 0.0 us)
Async XLA Ops:
  0.0 13.6 %copy-start = (bf16[81,128]{1,0:T(8,128)(2,1)S(1)}, bf16[81,128]{1,0:T(8,128)(2,1)}, u32[]{:S(2)}) copy-start(bf16[81,128]{1,0:T(8,128)(2,1)} %param.15) | copy-start | bytes 62212
  0.0 39.3 %copy-start.1 = (bf16[3,3,384,256]{3,2,1,0:T(8,128)(2,1)S(1)}, bf16[3,3,384,256]{3,2,1,0:T(8,128)(2,1)}, u32[]{:S(2)}) copy-start(bf16[3,3,384,256]{3,2,1,0:T(8,128)(2,1)} %param.18) | copy-start | bytes 5308420
  0.0 1.5 %collective-permute-start.1 = (bf16[8,3,4,256]{3,2,1,0:T(4,128)(2,1)}, bf16[8,3,4,256]{3,2,1,0:T(4,128)(2,1)S(1)}, u32[]{:S(2)}, u32[]{:S(2)}) collective-permute-start(bf16[8,3,4,256]{3,2,1,0:T(4,128)(2,1)} %fr_a.1), channel_id=1, source_target_pairs={{0,16},{16,0},{32,48},{48,32},{64,80},{80,64},{96,112},{112,96},{1... | collective-permute-start | bytes 147464 | tf_op jit(solution)/shard_map/ppermute | solution.py:259
  0.0 1.5 %collective-permute-start = (s32[8]{0:T(128)}, s32[8]{0:T(128)S(1)}, u32[]{:S(2)}, u32[]{:S(2)}) collective-permute-start(s32[8]{0:T(128)} %keep_a.1), channel_id=1, source_target_pairs={{0,16},{16,0},{32,48},{48,32},{64,80},{80,64},{96,112},{112,96},{1... | collective-permute-start | bytes 104 | tf_op jit(solution)/shard_map/ppermute | solution.py:260
  1.5 0.8 %copy-start.3 = (bf16[8,3,4,256]{3,2,1,0:T(4,128)(2,1)S(1)}, bf16[8,3,4,256]{3,2,1,0:T(4,128)(2,1)}, u32[]{:S(2)}) copy-start(bf16[8,3,4,256]{3,2,1,0:T(4,128)(2,1)} %fr_a.1) | copy-start | bytes 147460
  2.3 0.7 copy-start.7
  2.9 0.7 copy-start.8
  3.6 35.8 %copy-start.9 = (f32[128]{0:T(128)S(1)}, f32[128]{0:T(128)}, u32[]{:S(2)}) copy-start(f32[128]{0:T(128)} %param.16) | copy-start | bytes 1540
  3.6 35.8 %copy-start.10 = (f32[128]{0:T(128)S(1)}, f32[128]{0:T(128)}, u32[]{:S(2)}) copy-start(f32[128]{0:T(128)} %param.17) | copy-start | bytes 1540
  5.1 19.5 %all-to-all-start = ((bf16[8,4,3,4,256]{4,3,2,1,0:T(4,128)(2,1)}), bf16[8,4,3,4,256]{4,3,2,1,0:T(4,128)(2,1)S(1)}, u32[]{:S(2)}, u32[]{:S(2)}) async-start(bf16[8,4,3,4,256]{4,3,2,1,0:T(4,128)(2,1)} %shard_map.118), calls=%async_computation | async-start | bytes 393216 | tf_op jit(solution)/shard_map/all_to_all | solution.py:275
  15.1 46.8 %copy-start.2 = (bf16[1024,256]{1,0:T(8,128)(2,1)S(1)}, bf16[1024,256]{1,0:T(8,128)(2,1)}, u32[]{:S(2)}) copy-start(bf16[1024,256]{1,0:T(8,128)(2,1)} %dw_ref.1) | copy-start | bytes 1572868
  15.1 46.8 %copy-start.4 = (f32[256]{0:T(256)S(1)}, f32[256]{0:T(256)}, u32[]{:S(2)}) copy-start(f32[256]{0:T(256)} %param.19) | copy-start | bytes 3076
  15.1 46.8 %copy-start.5 = (f32[256]{0:T(256)S(1)}, f32[256]{0:T(256)}, u32[]{:S(2)}) copy-start(f32[256]{0:T(256)} %param.20) | copy-start | bytes 3076
  15.1 46.8 %copy-start.6 = (f32[256]{0:T(256)S(1)}, f32[256]{0:T(256)}, u32[]{:S(2)}) copy-start(f32[256]{0:T(256)} %param.22) | copy-start | bytes 3076
  25.4 13.9 %all-to-all-start.1 = ((bf16[16,3,4,256]{3,2,1,0:T(4,128)(2,1)}), bf16[16,3,4,256]{3,2,1,0:T(4,128)(2,1)S(1)}, u32[]{:S(2)}, u32[]{:S(2)}) async-start(bf16[16,3,4,256]{3,2,1,0:T(4,128)(2,1)} %shard_map.119), calls=%async_computation.1 | async-start | bytes 196608 | tf_op jit(solution)/shard_map/all_to_all | solution.py:284
  54.5 3.7 %collective-permute-start.4 = (f32[2,256]{1,0:T(2,128)S(1)}, f32[2,256]{1,0:T(2,128)S(1)}, u32[]{:S(2)}, u32[]{:S(2)}) collective-permute-start(f32[2,256]{1,0:T(2,128)S(1)} %get-tuple-element.12.stat_a), channel_id=1, source_target_pairs={{0,12},{4,0},{8,4},{12,8},{1,13},{5,1},{9,5},{13,9},{2,14},{6,2},{... | collective-permute-start | bytes 6152 | tf_op jit(solution)/shard_map/ppermute | solution.py:308
  55.6 5.1 %collective-permute-start.3 = (f32[2,256]{1,0:T(2,128)S(1)}, f32[2,256]{1,0:T(2,128)S(1)}, u32[]{:S(2)}, u32[]{:S(2)}) collective-permute-start(f32[2,256]{1,0:T(2,128)S(1)} %get-tuple-element.12.stat_a), channel_id=1, source_target_pairs={{0,8},{4,12},{8,0},{12,4},{1,9},{5,13},{9,1},{13,5},{2,10},{6,14},... | collective-permute-start | bytes 6152 | tf_op jit(solution)/shard_map/ppermute | solution.py:308
  57.1 4.8 %collective-permute-start.2 = (f32[2,256]{1,0:T(2,128)S(1)}, f32[2,256]{1,0:T(2,128)S(1)}, u32[]{:S(2)}, u32[]{:S(2)}) collective-permute-start(f32[2,256]{1,0:T(2,128)S(1)} %get-tuple-element.12.stat_a), channel_id=1, source_target_pairs={{0,4},{4,8},{8,12},{12,0},{1,5},{5,9},{9,13},{13,1},{2,6},{6,10},{... | collective-permute-start | bytes 6152 | tf_op jit(solution)/shard_map/ppermute | solution.py:308

commit v3 on v2

--- a/solution.py
+++ b/solution.py
@@ -174,24 +174,21 @@
                 hid[0, :, 128 * k : 128 * k + 128] = part
                 hid[1, :, 128 * k : 128 * k + 128] = part
 
-    def frame(f, carry):
-        s, q = carry
+    s = jnp.zeros((8, 256), F32)
+    q = jnp.zeros((8, 256), F32)
+    for f in range(0, 16, 4):
         for par in range(2):
             taps = [
-                hid[f + a, 32 * b : 32 * b + 128, 128 * par : 128 * par + 384]
+                hid[f + a : f + a + 4, 32 * b : 32 * b + 128, 128 * par : 128 * par + 384]
                 for a in range(3)
                 for b in range(3)
             ]
-            left = jnp.concatenate(taps, axis=1)
+            left = jnp.concatenate([tap.reshape(512, 384) for tap in taps], axis=1)
             out = jnp.dot(left, mw_ref[...], preferred_element_type=F32)
-            mix_ref[par, f] = out
-            parts = out.reshape(16, 8, 256)
+            mix_ref[par, f : f + 4] = out.reshape(4, 128, 256)
+            parts = out.reshape(64, 8, 256)
             s = s + jnp.sum(parts, axis=0)
             q = q + jnp.sum(parts * parts, axis=0)
-        return s, q
-
-    zero = jnp.zeros((8, 256), F32)
-    s, q = lax.fori_loop(0, 16, frame, (zero, zero))
     stat_ref[0:1, :] = jnp.sum(s, axis=0, keepdims=True)
     stat_ref[1:2, :] = jnp.sum(q, axis=0, keepdims=True)
 
@@ -225,6 +222,10 @@
                             row = (par + c) * 24 + ch * 8 + fo + 2 + a
                             place[fo * 2 + par, b, row, ((a * 3 + b) * 3 + c) * 3 + ch] = 1
     return place.reshape(3072, 81)
+
+
+def in_hbm(array):
+    return pltpu.with_memory_space_constraint(array, pltpu.HBM)
 
 
 def call(kernel, out_shape, specs, scratch=(), mib=16):
@@ -270,7 +271,7 @@
             pltpu.VMEM((8, 3, 4, 256), BF16),
             pltpu.SemaphoreType.DMA((5,)),
         ],
-    )(core, keep_list, keep_b, train_slot, frames, frames_b)
+    )(core, in_hbm(keep_list), keep_b, in_hbm(train_slot), in_hbm(frames), frames_b)
     along_z = [[2 * z + k for z in range(8)] for k in range(2)]
     received = lax.all_to_all(
         packed, "clip", split_axis=0, concat_axis=0, tiled=True, axis_index_groups=along_z
@@ -300,8 +301,8 @@
         row,
         raw,
         w4.reshape(8, 384, 128),
-        stem_gain.reshape(1, -1),
-        stem_shift.reshape(1, -1),
+        in_hbm(stem_gain.reshape(1, -1)),
+        in_hbm(stem_shift.reshape(1, -1)),
         mixer_weight.reshape(3456, 256),
     )
     others = [

time: 73.8 us -> 67.8 us (0.919)
  Pallas kernels: 19.1 us -> 15.3 us
  local copies, waits for them, and re-layouts: 2.85 us -> 0.74 us
    pallas_call x1, Pallas kernels: 15.2 us -> 11.2 us  [local(): call(mixer_kernel, (sds((2, 16, 128, 256), F32), sds((2, 256), F32)), [SM...]
    unnamed x23 -> x13, local copies, waits for them, and re-layouts: 2.85 us -> 0.74 us
where the time goes in v3:
time: 67.8 us; the launch traced here: 67.4 us
  waiting for transfers between devices  21.6 us (32%)
  starting transfers between devices  19 us (28%)
  Pallas kernels  15.3 us (23%)
  blocking collectives  9.18 us (14%)
  matrix products  1.47 us (2%)
  local copies, waits for them, and re-layouts  0.74 us (1%)
    pallas_call x1, Pallas kernels, local(): call(mixer_kernel, (sds((2, 16, 128, 256), F32), sds((2, 256), F32)), [SM...  11.2 us
    all_to_all x1, waiting for transfers between devices, local(): lax.all_to_all(packed, 'clip', split_axis=0, concat_axis=0, tiled=True, a...  9.44 us
    all_to_all x1, blocking collectives, local(): lax.all_to_all(latent.reshape(4, 2, 2, 32, 256), 'tm', split_axis=0, conc...  9.18 us
    all_to_all x1, starting transfers between devices, local(): lax.all_to_all(packed, 'clip', split_axis=0, concat_axis=0, tiled=True, a...  8.48 us
    all_to_all x1, starting transfers between devices, local(): lax.all_to_all(pieces, ('row', 'tm'), split_axis=0, concat_axis=0, tiled=...  7.48 us
    all_to_all x1, waiting for transfers between devices, local(): lax.all_to_all(pieces, ('row', 'tm'), split_axis=0, concat_axis=0, tiled=...  6.45 us
    ppermute x3, waiting for transfers between devices, local(): lax.ppermute(stat, 'row', [(i, (i + by) % 4) for i in range(4)])  4.77 us
    ppermute x3, starting transfers between devices, local(): lax.ppermute(stat, 'row', [(i, (i + by) % 4) for i in range(4)])  2.56 us
  transfers between devices with their start and end apart: 7, of which 6 were waited for; matrix products, arithmetic and copies ran while one was open for 2% of the time, Pallas kernels for 0%

profile of v3, /device:TPU:2, one launch (start us, length us, event | category | flops | bytes accessed | tf_op | source)
XLA Modules:
  0.0 67.4 jit_solution(2268114051661152859)
XLA Ops:
  0.0 0.0 collective-permute-start.1
  0.0 0.5 collective-permute-start
  0.5 1.0 %collective-permute-done.keep_b = s32[8]{0:T(128)S(1)} collective-permute-done((s32[8]{0:T(128)}, s32[8]{0:T(128)S(1)}, u32[]{:S(2)}, u32[]{:S(2)}) %collective-permute-start) | collective-permute-done | bytes 64 | tf_op jit(solution)/shard_map/ppermute | solution.py:261
  1.5 1.6 %shard_map.118 = bf16[8,4,3,4,256]{4,3,2,1,0:T(4,128)(2,1)} custom-call(s32[1]{0:T(128)} %bitcast.1.core_ref, s32[8]{0:T(128)} %keep_a.1, s32[8]{0:T(128)S(1)} %collective-permute-done.keep_b, s32[64]{0:T(128)} %train.1, bf16[8,3,4,256]{3,2,1,0:T(4,128)(2,1)} %fr_a.1, bf16[8,3,4,256]{3,2,1,0:T(4,128)(2,1)S(1)} %collective-permute-done.1.fr_b), custom_call_target="tpu_custom_call" | custom-call | tf_op jit(solution)/shard_map/pallas_call | solution.py:262
  3.1 8.5 %all-to-all-start = ((bf16[8,4,3,4,256]{4,3,2,1,0:T(4,128)(2,1)}), bf16[8,4,3,4,256]{4,3,2,1,0:T(4,128)(2,1)S(1)}, u32[]{:S(2)}, u32[]{:S(2)}) async-start(bf16[8,4,3,4,256]{4,3,2,1,0:T(4,128)(2,1)} %shard_map.118), calls=%async_computation | async-start | bytes 393216 | tf_op jit(solution)/shard_map/all_to_all | solution.py:276
  11.6 1.5 %convolution_convert_fusion = bf16[3072,128]{1,0:T(8,128)(2,1)S(1)} fusion(bf16[3072,81]{1,0:T(8,128)(2,1)} %constant.25.clone, bf16[81,128]{1,0:T(8,128)(2,1)S(1)} %copy-done), kind=kOutput, calls=%fused_computation | convolution fusion | flops 64094208 | bytes 1304832 | tf_op jit(solution)/shard_map/dot_general | solution.py:283
  13.1 0.0 copy-start.2
  13.1 0.0 copy-start.3
  13.1 0.0 copy-start.4
  13.1 0.0 copy-start.5
  13.1 9.4 %all-to-all-done.recv_ref = bf16[8,4,3,4,256]{4,3,2,1,0:T(4,128)(2,1)S(1)} async-done(((bf16[8,4,3,4,256]{4,3,2,1,0:T(4,128)(2,1)}), bf16[8,4,3,4,256]{4,3,2,1,0:T(4,128)(2,1)S(1)}, u32[]{:S(2)}, u32[]{:S(2)}) %all-to-all-start) | async-done | bytes 196640 | tf_op jit(solution)/shard_map/all_to_all | solution.py:276
  22.6 0.8 %shard_map.119 = bf16[16,3,4,256]{3,2,1,0:T(4,128)(2,1)} custom-call(bf16[8,4,3,4,256]{4,3,2,1,0:T(4,128)(2,1)S(1)} %all-to-all-done.recv_ref), custom_call_target="tpu_custom_call" | custom-call | tf_op jit(solution)/shard_map/pallas_call | solution.py:279
  23.4 7.5 %all-to-all-start.1 = ((bf16[16,3,4,256]{3,2,1,0:T(4,128)(2,1)}), bf16[16,3,4,256]{3,2,1,0:T(4,128)(2,1)S(1)}, u32[]{:S(2)}, u32[]{:S(2)}) async-start(bf16[16,3,4,256]{3,2,1,0:T(4,128)(2,1)} %shard_map.119), calls=%async_computation.1 | async-start | bytes 196608 | tf_op jit(solution)/shard_map/all_to_all | solution.py:285
  30.9 6.5 %all-to-all-done.1.raw_ref = bf16[16,3,4,256]{3,2,1,0:T(4,128)(2,1)S(1)} async-done(((bf16[16,3,4,256]{3,2,1,0:T(4,128)(2,1)}), bf16[16,3,4,256]{3,2,1,0:T(4,128)(2,1)S(1)}, u32[]{:S(2)}, u32[]{:S(2)}) %all-to-all-start.1) | async-done | bytes 98336 | tf_op jit(solution)/shard_map/all_to_all | solution.py:285
  37.3 11.2 %shard_map.120 = (f32[2,16,128,256]{3,2,1,0:T(8,128)S(1)}, f32[2,256]{1,0:T(2,128)S(1)}) custom-call(s32[1]{0:T(128)} %bitcast.y_ref, bf16[16,3,4,256]{3,2,1,0:T(4,128)(2,1)S(1)} %all-to-all-done.1.raw_ref, bf16[8,384,128]{2,1,0:T(8,128)(2,1)S(1)} %bitcast.12, f32[1,128]{1,0:T(1,128)} %bitcast.18, f32[1,128]{1,0:T(1,128)} %bitcast.19, ...), custom_call_target="tpu_custom_call" | custom-call | tf_op jit(solution)/shard_map/pallas_call | solution.py:286
  48.6 1.1 %collective-permute-start.4 = (f32[2,256]{1,0:T(2,128)S(1)}, f32[2,256]{1,0:T(2,128)S(1)}, u32[]{:S(2)}, u32[]{:S(2)}) collective-permute-start(f32[2,256]{1,0:T(2,128)S(1)} %get-tuple-element.12.stat_a), channel_id=1, source_target_pairs={{0,12},{4,0},{8,4},{12,8},{1,13},{5,1},{9,5},{13,9},{2,14},{6,2},{... | collective-permute-start | bytes 6152 | tf_op jit(solution)/shard_map/ppermute | solution.py:309
  49.7 1.5 %collective-permute-start.3 = (f32[2,256]{1,0:T(2,128)S(1)}, f32[2,256]{1,0:T(2,128)S(1)}, u32[]{:S(2)}, u32[]{:S(2)}) collective-permute-start(f32[2,256]{1,0:T(2,128)S(1)} %get-tuple-element.12.stat_a), channel_id=1, source_target_pairs={{0,8},{4,12},{8,0},{12,4},{1,9},{5,13},{9,1},{13,5},{2,10},{6,14},... | collective-permute-start | bytes 6152 | tf_op jit(solution)/shard_map/ppermute | solution.py:309
  51.1 0.0 collective-permute-start.2
  51.2 1.1 %collective-permute-done.4.stat_d = f32[2,256]{1,0:T(2,128)S(1)} collective-permute-done((f32[2,256]{1,0:T(2,128)S(1)}, f32[2,256]{1,0:T(2,128)S(1)}, u32[]{:S(2)}, u32[]{:S(2)}) %collective-permute-start.4) | collective-permute-done | bytes 2080 | tf_op jit(solution)/shard_map/ppermute | solution.py:309
  52.3 2.5 %collective-permute-done.3.stat_c = f32[2,256]{1,0:T(2,128)S(1)} collective-permute-done((f32[2,256]{1,0:T(2,128)S(1)}, f32[2,256]{1,0:T(2,128)S(1)}, u32[]{:S(2)}, u32[]{:S(2)}) %collective-permute-start.3) | collective-permute-done | bytes 2080 | tf_op jit(solution)/shard_map/ppermute | solution.py:309
  54.8 1.2 %collective-permute-done.2.stat_b = f32[2,256]{1,0:T(2,128)S(1)} collective-permute-done((f32[2,256]{1,0:T(2,128)S(1)}, f32[2,256]{1,0:T(2,128)S(1)}, u32[]{:S(2)}, u32[]{:S(2)}) %collective-permute-start.2) | collective-permute-done | bytes 2080 | tf_op jit(solution)/shard_map/ppermute | solution.py:309
  56.0 1.6 %shard_map.121 = bf16[512,256]{1,0:T(8,128)(2,1)S(1)} custom-call(f32[2,16,128,256]{3,2,1,0:T(8,128)S(1)} %get-tuple-element.11.mix_ref, f32[2,256]{1,0:T(2,128)S(1)} %get-tuple-element.12.stat_a, f32[2,256]{1,0:T(2,128)S(1)} %collective-permute-done.2.stat_b, f32[2,256]{1,0:T(2,128)S(1)} %collective-permute-done.3.stat_c, ...), custom_call_target="tpu_custom_call" | custom-call | tf_op jit(solution)/shard_map/pallas_call | solution.py:311
  57.5 9.2 %all_to_all.15 = bf16[4,2,2,32,256]{4,3,2,1,0:T(8,128)(2,1)S(1)} all-to-all(bf16[4,2,2,32,256]{4,3,2,1,0:T(8,128)(2,1)S(1)} %bitcast.14), channel_id=1, replica_groups=mesh['clip'=16,'row'=4,'tm'=4] {'tm'}, dimensions={0} | all-to-all | bytes 524288 | tf_op jit(solution)/shard_map/all_to_all | solution.py:322
  66.7 0.7 %copy.14 = bf16[4,2,2,32,256]{4,3,2,1,0:T(8,128)(2,1)} copy(bf16[4,2,2,32,256]{4,3,2,1,0:T(8,128)(2,1)S(1)} %all_to_all.15) | data formatting | bytes 524288
  (9 shorter events, 0.0 us)
Async XLA Ops:
  0.0 11.6 %copy-start = (bf16[81,128]{1,0:T(8,128)(2,1)S(1)}, bf16[81,128]{1,0:T(8,128)(2,1)}, u32[]{:S(2)}) copy-start(bf16[81,128]{1,0:T(8,128)(2,1)} %param.15) | copy-start | bytes 62212
  0.0 37.3 %copy-start.1 = (bf16[3,3,384,256]{3,2,1,0:T(8,128)(2,1)S(1)}, bf16[3,3,384,256]{3,2,1,0:T(8,128)(2,1)}, u32[]{:S(2)}) copy-start(bf16[3,3,384,256]{3,2,1,0:T(8,128)(2,1)} %param.18) | copy-start | bytes 5308420
  0.0 1.5 %collective-permute-start.1 = (bf16[8,3,4,256]{3,2,1,0:T(4,128)(2,1)}, bf16[8,3,4,256]{3,2,1,0:T(4,128)(2,1)S(1)}, u32[]{:S(2)}, u32[]{:S(2)}) collective-permute-start(bf16[8,3,4,256]{3,2,1,0:T(4,128)(2,1)} %fr_a.1), channel_id=1, source_target_pairs={{0,16},{16,0},{32,48},{48,32},{64,80},{80,64},{96,112},{112,96},{1... | collective-permute-start | bytes 147464 | tf_op jit(solution)/shard_map/ppermute | solution.py:260
  0.0 1.5 %collective-permute-start = (s32[8]{0:T(128)}, s32[8]{0:T(128)S(1)}, u32[]{:S(2)}, u32[]{:S(2)}) collective-permute-start(s32[8]{0:T(128)} %keep_a.1), channel_id=1, source_target_pairs={{0,16},{16,0},{32,48},{48,32},{64,80},{80,64},{96,112},{112,96},{1... | collective-permute-start | bytes 104 | tf_op jit(solution)/shard_map/ppermute | solution.py:261
  3.1 19.5 %all-to-all-start = ((bf16[8,4,3,4,256]{4,3,2,1,0:T(4,128)(2,1)}), bf16[8,4,3,4,256]{4,3,2,1,0:T(4,128)(2,1)S(1)}, u32[]{:S(2)}, u32[]{:S(2)}) async-start(bf16[8,4,3,4,256]{4,3,2,1,0:T(4,128)(2,1)} %shard_map.118), calls=%async_computation | async-start | bytes 393216 | tf_op jit(solution)/shard_map/all_to_all | solution.py:276
  13.1 42.8 %copy-start.2 = (bf16[1024,256]{1,0:T(8,128)(2,1)S(1)}, bf16[1024,256]{1,0:T(8,128)(2,1)}, u32[]{:S(2)}) copy-start(bf16[1024,256]{1,0:T(8,128)(2,1)} %dw_ref.1) | copy-start | bytes 1572868
  13.1 42.8 %copy-start.3 = (f32[256]{0:T(256)S(1)}, f32[256]{0:T(256)}, u32[]{:S(2)}) copy-start(f32[256]{0:T(256)} %param.19) | copy-start | bytes 3076
  13.1 42.8 %copy-start.4 = (f32[256]{0:T(256)S(1)}, f32[256]{0:T(256)}, u32[]{:S(2)}) copy-start(f32[256]{0:T(256)} %param.20) | copy-start | bytes 3076
  13.1 42.8 %copy-start.5 = (f32[256]{0:T(256)S(1)}, f32[256]{0:T(256)}, u32[]{:S(2)}) copy-start(f32[256]{0:T(256)} %param.22) | copy-start | bytes 3076
  23.4 13.9 %all-to-all-start.1 = ((bf16[16,3,4,256]{3,2,1,0:T(4,128)(2,1)}), bf16[16,3,4,256]{3,2,1,0:T(4,128)(2,1)S(1)}, u32[]{:S(2)}, u32[]{:S(2)}) async-start(bf16[16,3,4,256]{3,2,1,0:T(4,128)(2,1)} %shard_map.119), calls=%async_computation.1 | async-start | bytes 196608 | tf_op jit(solution)/shard_map/all_to_all | solution.py:285
  48.6 3.7 %collective-permute-start.4 = (f32[2,256]{1,0:T(2,128)S(1)}, f32[2,256]{1,0:T(2,128)S(1)}, u32[]{:S(2)}, u32[]{:S(2)}) collective-permute-start(f32[2,256]{1,0:T(2,128)S(1)} %get-tuple-element.12.stat_a), channel_id=1, source_target_pairs={{0,12},{4,0},{8,4},{12,8},{1,13},{5,1},{9,5},{13,9},{2,14},{6,2},{... | collective-permute-start | bytes 6152 | tf_op jit(solution)/shard_map/ppermute | solution.py:309
  49.7 5.1 %collective-permute-start.3 = (f32[2,256]{1,0:T(2,128)S(1)}, f32[2,256]{1,0:T(2,128)S(1)}, u32[]{:S(2)}, u32[]{:S(2)}) collective-permute-start(f32[2,256]{1,0:T(2,128)S(1)} %get-tuple-element.12.stat_a), channel_id=1, source_target_pairs={{0,8},{4,12},{8,0},{12,4},{1,9},{5,13},{9,1},{13,5},{2,10},{6,14},... | collective-permute-start | bytes 6152 | tf_op jit(solution)/shard_map/ppermute | solution.py:309
  51.1 4.8 %collective-permute-start.2 = (f32[2,256]{1,0:T(2,128)S(1)}, f32[2,256]{1,0:T(2,128)S(1)}, u32[]{:S(2)}, u32[]{:S(2)}) collective-permute-start(f32[2,256]{1,0:T(2,128)S(1)} %get-tuple-element.12.stat_a), channel_id=1, source_target_pairs={{0,4},{4,8},{8,12},{12,0},{1,5},{5,9},{9,13},{13,1},{2,6},{6,10},{... | collective-permute-start | bytes 6152 | tf_op jit(solution)/shard_map/ppermute | solution.py:309

commit v4 on v3

--- a/solution.py
+++ b/solution.py
@@ -22,16 +22,31 @@
     return lax.broadcasted_iota(jnp.int32, shape, dim)
 
 
-def pack_kernel(
-    core_ref, keep_a, keep_b, train, fr_a, fr_b, out_ref, keep_s, keep_t, train_s, fra, frb, sems
-):
-    pairs = ((keep_a, keep_s), (keep_b, keep_t), (train, train_s), (fr_a, fra), (fr_b, frb))
+def weights_kernel(places_ref, stem_ref, mw_ref, w4_ref, mid_ref):
+    for n in range(8):
+        part = places_ref[384 * n : 384 * n + 384, :]
+        w4_ref[n] = jnp.dot(part, stem_ref[...], preferred_element_type=F32).astype(BF16)
+    for k in range(9):
+        g0, g1, g2 = (
+            mw_ref[384 * k + 128 * c : 384 * k + 128 * c + 128].astype(F32) for c in range(3)
+        )
+        outer = (g0 + g2) * 0.5
+        inner = g1 * 0.5
+        mid_ref[0, 128 * k : 128 * k + 128] = (outer + inner).astype(BF16)
+        mid_ref[1, 128 * k : 128 * k + 128] = (outer - inner).astype(BF16)
+
+
+def fetch_kernel(keep, train, fr, keep_out, train_out, fr_out, sems):
+    pairs = ((keep, keep_out), (train, train_out), (fr, fr_out))
     copies = [pltpu.make_async_copy(src, dst, sems.at[i]) for i, (src, dst) in enumerate(pairs)]
     for copy in copies:
         copy.start()
-    out_ref[...] = jnp.zeros_like(out_ref)
     for copy in copies:
         copy.wait()
+
+
+def pack_kernel(core_ref, keep_s, keep_t, train_s, fra, frb, out_ref):
+    out_ref[...] = jnp.zeros_like(out_ref)
     core = core_ref[0]
     for keep_ref, fr in ((keep_s, fra), (keep_t, frb)):
         for j in range(fr.shape[0]):
@@ -88,16 +103,18 @@
 def mixer_kernel(
     y_ref,
     raw_ref,
-    w4_ref,
+    w4_hbm,
     gain_hbm,
     shift_hbm,
     mw_ref,
+    mid_ref,
     mix_ref,
     stat_ref,
     dv,
     tg,
     stem,
     hid,
+    w4_ref,
     gain_ref,
     shift_ref,
     sems,
@@ -106,6 +123,7 @@
     copies = [
         pltpu.make_async_copy(gain_hbm, gain_ref, sems.at[0]),
         pltpu.make_async_copy(shift_hbm, shift_ref, sems.at[1]),
+        pltpu.make_async_copy(w4_hbm, w4_ref, sems.at[2]),
     ]
     for copy in copies:
         copy.start()
@@ -133,6 +151,8 @@
         rows = [dv[v, ch, 4 * g : 4 * g + 8, :] for v in range(4) for ch in range(3)]
         block = jnp.concatenate(rows + [jnp.zeros((32, 512), F32)], axis=0)
         tg[g, 32:544, :] = jnp.transpose(block).astype(BF16)
+    for copy in copies:
+        copy.wait()
     total = jnp.zeros((8, 1024), F32)
     square = jnp.zeros((8, 1024), F32)
     for g in range(4):
@@ -149,8 +169,6 @@
     square = jnp.sum(square, axis=0, keepdims=True)
     total = sum(total[:, 128 * k : 128 * k + 128] for k in range(8))
     square = sum(square[:, 128 * k : 128 * k + 128] for k in range(8))
-    for copy in copies:
-        copy.wait()
     scale, offset = group_scale(total, square, 16384, 4, gain_ref[...], shift_ref[...])
     at = iota((192, 128), 0)
     row = at >> 5
@@ -167,7 +185,8 @@
         odd = jnp.where(valid, silu(val[:, 128:] * scale + offset), 0.0)
         before = jnp.where(first, 0.0, pltpu.roll(odd, 1, 0))
         after = jnp.where(last, 0.0, pltpu.roll(even, 191, 0))
-        for k, part in enumerate((before, even, odd, after)):
+        parts = (before - odd, even + odd, odd - even, even - after)
+        for k, part in enumerate(parts):
             part = part.astype(BF16)
             hid[f + 2, :, 128 * k : 128 * k + 128] = part
             if f == 0:
@@ -176,15 +195,35 @@
 
     s = jnp.zeros((8, 256), F32)
     q = jnp.zeros((8, 256), F32)
+    steps = [(a, b) for a in range(3) for b in range(3)]
+    first_tap = [mw_ref[384 * k : 384 * k + 128] for k in range(9)]
+    last_tap = [mw_ref[384 * k + 256 : 384 * k + 384] for k in range(9)]
+    weights = (
+        jnp.concatenate(first_tap[:8], axis=0),
+        mid_ref[0, :1024],
+        mid_ref[1, :1024],
+        jnp.concatenate(last_tap[:8], axis=0),
+    )
+    tail_even = jnp.concatenate([first_tap[8], mid_ref[0, 1024:]], axis=0)
+    tail_odd = jnp.concatenate([mid_ref[0, 1024:], -last_tap[8]], axis=0)
+    tail_both = mid_ref[1, 1024:]
     for f in range(0, 16, 4):
-        for par in range(2):
-            taps = [
-                hid[f + a : f + a + 4, 32 * b : 32 * b + 128, 128 * par : 128 * par + 384]
-                for a in range(3)
-                for b in range(3)
-            ]
-            left = jnp.concatenate([tap.reshape(512, 384) for tap in taps], axis=1)
-            out = jnp.dot(left, mw_ref[...], preferred_element_type=F32)
+
+        def tap(k, a, b):
+            cut = hid[f + a : f + a + 4, 32 * b : 32 * b + 128, 128 * k : 128 * k + 128]
+            return cut.reshape(512, 128)
+
+        m = []
+        for k in range(4):
+            left = jnp.concatenate([tap(k, a, b) for a, b in steps[:8]], axis=1)
+            m.append(jnp.dot(left, weights[k], preferred_element_type=F32))
+        t = [tap(k, 2, 2) for k in range(4)]
+        even = jnp.dot(jnp.concatenate([t[0], t[1]], axis=1), tail_even, preferred_element_type=F32)
+        odd = jnp.dot(jnp.concatenate([t[1], t[3]], axis=1), tail_odd, preferred_element_type=F32)
+        both = jnp.dot(t[2], tail_both, preferred_element_type=F32) + m[2]
+        even = even + m[0] + (m[1] + both)
+        odd = odd - m[3] + (m[1] - both)
+        for par, out in enumerate((even, odd)):
             mix_ref[par, f : f + 4] = out.reshape(4, 128, 256)
             parts = out.reshape(64, 8, 256)
             s = s + jnp.sum(parts, axis=0)
@@ -259,19 +298,22 @@
     pairs = [(i, i ^ 1) for i in range(16)]
     frames_b = lax.ppermute(frames, "clip", pairs)
     keep_b = lax.ppermute(keep_list, "clip", pairs)
+    keep_a, train, frames_a = call(
+        fetch_kernel,
+        (sds((8,), jnp.int32), sds((64,), jnp.int32), sds((8, 3, 4, 256), BF16)),
+        [HBM] * 3,
+        [pltpu.SemaphoreType.DMA((3,))],
+    )(in_hbm(keep_list), in_hbm(train_slot), in_hbm(frames))
     packed = call(
-        pack_kernel,
-        sds((8, 4, 3, 4, 256), BF16),
-        [SMEM, HBM, ANY, HBM, HBM, ANY],
-        [
-            pltpu.SMEM((8,), jnp.int32),
-            pltpu.SMEM((8,), jnp.int32),
-            pltpu.SMEM((64,), jnp.int32),
-            pltpu.VMEM((8, 3, 4, 256), BF16),
-            pltpu.VMEM((8, 3, 4, 256), BF16),
-            pltpu.SemaphoreType.DMA((5,)),
-        ],
-    )(core, in_hbm(keep_list), keep_b, in_hbm(train_slot), in_hbm(frames), frames_b)
+        pack_kernel, sds((8, 4, 3, 4, 256), BF16), [SMEM] * 4 + [VMEM] * 2
+    )(core, keep_a, keep_b, train, frames_a, frames_b)
+    places = jnp.asarray(stem_places(), BF16)
+    packed, mixer_weight = lax.optimization_barrier((packed, mixer_weight.reshape(3456, 256)))
+    w4, middle = call(
+        weights_kernel,
+        (sds((8, 384, 128), BF16), sds((2, 1152, 256), BF16)),
+        [VMEM] * 3,
+    )(places, stem_weight, mixer_weight)
     along_z = [[2 * z + k for z in range(8)] for k in range(2)]
     received = lax.all_to_all(
         packed, "clip", split_axis=0, concat_axis=0, tiled=True, axis_index_groups=along_z
@@ -279,31 +321,31 @@
     pieces = call(
         combine_kernel, sds((16, 3, 4, 256), BF16), [VMEM], [pltpu.VMEM((48, 256), F32)]
     )(received)
-    places = jnp.asarray(stem_places(), BF16)
-    w4 = jnp.dot(places, stem_weight, preferred_element_type=F32).astype(BF16)
-    pieces, w4 = lax.optimization_barrier((pieces, w4))
+    pieces, w4, middle = lax.optimization_barrier((pieces, w4, middle))
     raw = lax.all_to_all(pieces, ("row", "tm"), split_axis=0, concat_axis=0, tiled=True)
     mix, stat = call(
         mixer_kernel,
         (sds((2, 16, 128, 256), F32), sds((2, 256), F32)),
-        [SMEM, VMEM, VMEM, HBM, HBM, VMEM],
+        [SMEM, VMEM, HBM, HBM, HBM, VMEM, VMEM],
         [
             pltpu.VMEM((4, 3, 24, 512), F32),
             pltpu.VMEM((4, 576, 128), BF16),
             pltpu.VMEM((4, 576, 1024), F32),
             pltpu.VMEM((18, 192, 512), BF16),
+            pltpu.VMEM((8, 384, 128), BF16),
             pltpu.VMEM((1, 128), F32),
             pltpu.VMEM((1, 128), F32),
-            pltpu.SemaphoreType.DMA((2,)),
+            pltpu.SemaphoreType.DMA((3,)),
         ],
         mib=24,
     )(
         row,
         raw,
-        w4.reshape(8, 384, 128),
+        in_hbm(w4),
         in_hbm(stem_gain.reshape(1, -1)),
         in_hbm(stem_shift.reshape(1, -1)),
-        mixer_weight.reshape(3456, 256),
+        mixer_weight,
+        middle,
     )
     others = [
         lax.ppermute(stat, "row", [(i, (i + by) % 4) for i in range(4)]) for by in (1, 2, 3)

time: 67.8 us -> 66.3 us (0.978)
  waiting for transfers between devices: 21.6 us -> 17.3 us
  local copies, waits for them, and re-layouts: 0.74 us -> 4.94 us
  matrix products: 1.47 us -> 0 us
    unnamed x13 -> x19, local copies, waits for them, and re-layouts: 0.74 us -> 4.94 us
    all_to_all x1, waiting for transfers between devices: 9.44 us -> 6.01 us  [local(): lax.all_to_all(packed, 'clip', split_axis=0, concat_axis=0, tiled=True, a...]
    dot_general x1 -> x0, matrix products: 1.47 us -> none  [local(): w4 = jnp.dot(places, stem_weight, preferred_element_type=F32).astype(BF16)]
    pallas_call x1 -> x3, Pallas kernels: 1.64 us -> 3.06 us  [the longest x1 1.48 us: local(): call(pack_kernel, sds((8, 4, 3, 4, 256), BF16), [SMEM] * 4 + [VMEM] * 2)]
    pallas_call x1, Pallas kernels: 11.2 us -> 9.82 us  [local(): call(mixer_kernel, (sds((2, 16, 128, 256), F32), sds((2, 256), F32)), [SM...]
    ppermute x1, waiting for transfers between devices: 0.95 us -> 0.08 us  [local(): keep_b = lax.ppermute(keep_list, 'clip', pairs)]
  transfers between devices with their start and end apart: 7 -> 7, of which waited for: 6 -> 6; matrix products, arithmetic and copies ran while one was open for 2% -> 0% of each run, Pallas kernels for 0% -> 2%
where the time goes in v4:
time: 66.3 us; the launch traced here: 65.8 us
  starting transfers between devices  19 us (29%)
  waiting for transfers between devices  17.3 us (26%)
  Pallas kernels  15.3 us (23%)
  blocking collectives  9.18 us (14%)
  local copies, waits for them, and re-layouts  4.94 us (7%)
    pallas_call x1, Pallas kernels, local(): call(mixer_kernel, (sds((2, 16, 128, 256), F32), sds((2, 256), F32)), [SM...  9.82 us
    all_to_all x1, blocking collectives, local(): lax.all_to_all(latent.reshape(4, 2, 2, 32, 256), 'tm', split_axis=0, conc...  9.18 us
    all_to_all x1, starting transfers between devices, local(): lax.all_to_all(packed, 'clip', split_axis=0, concat_axis=0, tiled=True, a...  8.47 us
    all_to_all x1, starting transfers between devices, local(): lax.all_to_all(pieces, ('row', 'tm'), split_axis=0, concat_axis=0, tiled=...  7.48 us
    all_to_all x1, waiting for transfers between devices, local(): lax.all_to_all(pieces, ('row', 'tm'), split_axis=0, concat_axis=0, tiled=...  6.45 us
    all_to_all x1, waiting for transfers between devices, local(): lax.all_to_all(packed, 'clip', split_axis=0, concat_axis=0, tiled=True, a...  6.01 us
    unnamed x19, local copies, waits for them, and re-layouts  4.94 us
    ppermute x3, waiting for transfers between devices, local(): lax.ppermute(stat, 'row', [(i, (i + by) % 4) for i in range(4)])  4.77 us
  transfers between devices with their start and end apart: 7, of which 6 were waited for; matrix products, arithmetic and copies ran while one was open for 0% of the time, Pallas kernels for 2%

profile of v4, /device:TPU:2, one launch (start us, length us, event | category | flops | bytes accessed | tf_op | source)
XLA Modules:
  0.0 65.8 jit_solution(2294445530603371579)
XLA Ops:
  0.0 0.5 collective-permute-start
  0.5 0.9 %shard_map.118 = (s32[8]{0:T(128)S(1)}, s32[64]{0:T(128)S(1)}, bf16[8,3,4,256]{3,2,1,0:T(4,128)(2,1)S(1)}) custom-call(s32[8]{0:T(128)} %keep.1, s32[64]{0:T(128)} %train.1, bf16[8,3,4,256]{3,2,1,0:T(4,128)(2,1)} %fr.1), custom_call_target="tpu_custom_call" | custom-call | tf_op jit(solution)/shard_map/pallas_call | solution.py:301
  1.4 0.1 collective-permute-done.keep_t
  1.5 1.5 %shard_map.119 = bf16[8,4,3,4,256]{4,3,2,1,0:T(4,128)(2,1)} custom-call(s32[1]{0:T(128)} %bitcast.1.core_ref, s32[8]{0:T(128)S(1)} %get-tuple-element.17.keep_s, s32[8]{0:T(128)S(1)} %collective-permute-done.keep_t, s32[64]{0:T(128)S(1)} %get-tuple-element.18.train_s, bf16[8,3,4,256]{3,2,1,0:T(4,128)(2,1)S(1)} %get-tuple-element.19.fra, ...), custom_call_target="tpu_custom_call" | custom-call | tf_op jit(solution)/shard_map/pallas_call | solution.py:307
  2.9 8.5 %all-to-all-start = ((bf16[8,4,3,4,256]{4,3,2,1,0:T(4,128)(2,1)}), bf16[8,4,3,4,256]{4,3,2,1,0:T(4,128)(2,1)S(1)}, u32[]{:S(2)}, u32[]{:S(2)}) async-start(bf16[8,4,3,4,256]{4,3,2,1,0:T(4,128)(2,1)} %shard_map.119), calls=%async_computation | async-start | bytes 393216 | tf_op jit(solution)/shard_map/all_to_all | solution.py:318
  11.4 1.5 %copy-done = bf16[3,3,384,256]{3,2,1,0:T(8,128)(2,1)S(1)} copy-done((bf16[3,3,384,256]{3,2,1,0:T(8,128)(2,1)S(1)}, bf16[3,3,384,256]{3,2,1,0:T(8,128)(2,1)}, u32[]{:S(2)}) %copy-start) | copy-done | bytes 1769496
  12.9 1.1 %copy-done.2 = bf16[3072,81]{1,0:T(8,128)(2,1)S(1)} copy-done((bf16[3072,81]{1,0:T(8,128)(2,1)S(1)}, bf16[3072,81]{1,0:T(8,128)(2,1)}, u32[]{:S(2)}) %copy-start.2) | copy-done | bytes 497688
  14.0 0.7 %copy-done.5 = bf16[81,128]{1,0:T(8,128)(2,1)S(1)} copy-done((bf16[81,128]{1,0:T(8,128)(2,1)S(1)}, bf16[81,128]{1,0:T(8,128)(2,1)}, u32[]{:S(2)}) %copy-start.5) | copy-done | bytes 20760
  14.8 0.7 %shard_map.121 = (bf16[8,384,128]{2,1,0:T(8,128)(2,1)S(1)}, bf16[2,1152,256]{2,1,0:T(8,128)(2,1)S(1)}) custom-call(bf16[3072,81]{1,0:T(8,128)(2,1)S(1)} %copy-done.2, bf16[81,128]{1,0:T(8,128)(2,1)S(1)} %copy-done.5, bf16[3456,256]{1,0:T(8,128)(2,1)S(1)} %bitcast.9), custom_call_target="tpu_custom_call" | custom-call | tf_op jit(solution)/shard_map/pallas_call | solution.py:312
  15.5 0.9 %copy-done.3 = bf16[8,384,128]{2,1,0:T(8,128)(2,1)} copy-done((bf16[8,384,128]{2,1,0:T(8,128)(2,1)}, bf16[8,384,128]{2,1,0:T(8,128)(2,1)S(1)}, u32[]{:S(2)}) %copy-start.3) | copy-done | bytes 786456
  16.4 6.0 %all-to-all-done.recv_ref = bf16[8,4,3,4,256]{4,3,2,1,0:T(4,128)(2,1)S(1)} async-done(((bf16[8,4,3,4,256]{4,3,2,1,0:T(4,128)(2,1)}), bf16[8,4,3,4,256]{4,3,2,1,0:T(4,128)(2,1)S(1)}, u32[]{:S(2)}, u32[]{:S(2)}) %all-to-all-start) | async-done | bytes 196640 | tf_op jit(solution)/shard_map/all_to_all | solution.py:318
  22.4 0.8 %shard_map.120 = bf16[16,3,4,256]{3,2,1,0:T(4,128)(2,1)} custom-call(bf16[8,4,3,4,256]{4,3,2,1,0:T(4,128)(2,1)S(1)} %all-to-all-done.recv_ref), custom_call_target="tpu_custom_call" | custom-call | tf_op jit(solution)/shard_map/pallas_call | solution.py:321
  23.2 7.5 %all-to-all-start.1 = ((bf16[16,3,4,256]{3,2,1,0:T(4,128)(2,1)}), bf16[16,3,4,256]{3,2,1,0:T(4,128)(2,1)S(1)}, u32[]{:S(2)}, u32[]{:S(2)}) async-start(bf16[16,3,4,256]{3,2,1,0:T(4,128)(2,1)} %shard_map.120), calls=%async_computation.1 | async-start | bytes 196608 | tf_op jit(solution)/shard_map/all_to_all | solution.py:325
  30.7 6.5 %all-to-all-done.1.raw_ref = bf16[16,3,4,256]{3,2,1,0:T(4,128)(2,1)S(1)} async-done(((bf16[16,3,4,256]{3,2,1,0:T(4,128)(2,1)}), bf16[16,3,4,256]{3,2,1,0:T(4,128)(2,1)S(1)}, u32[]{:S(2)}, u32[]{:S(2)}) %all-to-all-start.1) | async-done | bytes 98336 | tf_op jit(solution)/shard_map/all_to_all | solution.py:325
  37.2 9.8 %shard_map.122 = (f32[2,16,128,256]{3,2,1,0:T(8,128)S(1)}, f32[2,256]{1,0:T(2,128)S(1)}) custom-call(s32[1]{0:T(128)} %bitcast.y_ref, bf16[16,3,4,256]{3,2,1,0:T(4,128)(2,1)S(1)} %all-to-all-done.1.raw_ref, bf16[8,384,128]{2,1,0:T(8,128)(2,1)} %copy-done.3, f32[1,128]{1,0:T(1,128)} %bitcast.15, f32[1,128]{1,0:T(1,128)} %bitcast.16, ...), custom_call_target="tpu_custom_call" | custom-call | tf_op jit(solution)/shard_map/pallas_call | solution.py:326
  47.0 1.1 %collective-permute-start.4 = (f32[2,256]{1,0:T(2,128)S(1)}, f32[2,256]{1,0:T(2,128)S(1)}, u32[]{:S(2)}, u32[]{:S(2)}) collective-permute-start(f32[2,256]{1,0:T(2,128)S(1)} %get-tuple-element.28.stat_a), channel_id=1, source_target_pairs={{0,12},{4,0},{8,4},{12,8},{1,13},{5,1},{9,5},{13,9},{2,14},{6,2},{... | collective-permute-start | bytes 6152 | tf_op jit(solution)/shard_map/ppermute | solution.py:351
  48.1 1.5 %collective-permute-start.3 = (f32[2,256]{1,0:T(2,128)S(1)}, f32[2,256]{1,0:T(2,128)S(1)}, u32[]{:S(2)}, u32[]{:S(2)}) collective-permute-start(f32[2,256]{1,0:T(2,128)S(1)} %get-tuple-element.28.stat_a), channel_id=1, source_target_pairs={{0,8},{4,12},{8,0},{12,4},{1,9},{5,13},{9,1},{13,5},{2,10},{6,14},... | collective-permute-start | bytes 6152 | tf_op jit(solution)/shard_map/ppermute | solution.py:351
  49.6 0.0 collective-permute-start.2
  49.6 1.1 %collective-permute-done.4.stat_d = f32[2,256]{1,0:T(2,128)S(1)} collective-permute-done((f32[2,256]{1,0:T(2,128)S(1)}, f32[2,256]{1,0:T(2,128)S(1)}, u32[]{:S(2)}, u32[]{:S(2)}) %collective-permute-start.4) | collective-permute-done | bytes 2080 | tf_op jit(solution)/shard_map/ppermute | solution.py:351
  50.7 2.5 %collective-permute-done.3.stat_c = f32[2,256]{1,0:T(2,128)S(1)} collective-permute-done((f32[2,256]{1,0:T(2,128)S(1)}, f32[2,256]{1,0:T(2,128)S(1)}, u32[]{:S(2)}, u32[]{:S(2)}) %collective-permute-start.3) | collective-permute-done | bytes 2080 | tf_op jit(solution)/shard_map/ppermute | solution.py:351
  53.2 1.2 %collective-permute-done.2.stat_b = f32[2,256]{1,0:T(2,128)S(1)} collective-permute-done((f32[2,256]{1,0:T(2,128)S(1)}, f32[2,256]{1,0:T(2,128)S(1)}, u32[]{:S(2)}, u32[]{:S(2)}) %collective-permute-start.2) | collective-permute-done | bytes 2080 | tf_op jit(solution)/shard_map/ppermute | solution.py:351
  54.4 1.6 %shard_map.123 = bf16[512,256]{1,0:T(8,128)(2,1)S(1)} custom-call(f32[2,16,128,256]{3,2,1,0:T(8,128)S(1)} %get-tuple-element.27.mix_ref, f32[2,256]{1,0:T(2,128)S(1)} %get-tuple-element.28.stat_a, f32[2,256]{1,0:T(2,128)S(1)} %collective-permute-done.2.stat_b, f32[2,256]{1,0:T(2,128)S(1)} %collective-permute-done.3.stat_c, ...), custom_call_target="tpu_custom_call" | custom-call | tf_op jit(solution)/shard_map/pallas_call | solution.py:353
  55.9 9.2 %all_to_all.15 = bf16[4,2,2,32,256]{4,3,2,1,0:T(8,128)(2,1)S(1)} all-to-all(bf16[4,2,2,32,256]{4,3,2,1,0:T(8,128)(2,1)S(1)} %bitcast.11), channel_id=1, replica_groups=mesh['clip'=16,'row'=4,'tm'=4] {'tm'}, dimensions={0} | all-to-all | bytes 524288 | tf_op jit(solution)/shard_map/all_to_all | solution.py:364
  65.1 0.7 %copy.14 = bf16[4,2,2,32,256]{4,3,2,1,0:T(8,128)(2,1)} copy(bf16[4,2,2,32,256]{4,3,2,1,0:T(8,128)(2,1)S(1)} %all_to_all.15) | data formatting | bytes 524288
  (16 shorter events, 0.0 us)
Async XLA Ops:
  0.0 1.5 %collective-permute-start.1 = (bf16[8,3,4,256]{3,2,1,0:T(4,128)(2,1)}, bf16[8,3,4,256]{3,2,1,0:T(4,128)(2,1)S(1)}, u32[]{:S(2)}, u32[]{:S(2)}) collective-permute-start(bf16[8,3,4,256]{3,2,1,0:T(4,128)(2,1)} %fr.1), channel_id=1, source_target_pairs={{0,16},{16,0},{32,48},{48,32},{64,80},{80,64},{96,112},{112,96},{1... | collective-permute-start | bytes 147464 | tf_op jit(solution)/shard_map/ppermute | solution.py:299
  0.0 1.5 %collective-permute-start = (s32[8]{0:T(128)}, s32[8]{0:T(128)S(1)}, u32[]{:S(2)}, u32[]{:S(2)}) collective-permute-start(s32[8]{0:T(128)} %keep.1), channel_id=1, source_target_pairs={{0,16},{16,0},{32,48},{48,32},{64,80},{80,64},{96,112},{112,96},{1... | collective-permute-start | bytes 104 | tf_op jit(solution)/shard_map/ppermute | solution.py:300
  2.9 19.4 %all-to-all-start = ((bf16[8,4,3,4,256]{4,3,2,1,0:T(4,128)(2,1)}), bf16[8,4,3,4,256]{4,3,2,1,0:T(4,128)(2,1)S(1)}, u32[]{:S(2)}, u32[]{:S(2)}) async-start(bf16[8,4,3,4,256]{4,3,2,1,0:T(4,128)(2,1)} %shard_map.119), calls=%async_computation | async-start | bytes 393216 | tf_op jit(solution)/shard_map/all_to_all | solution.py:318
  11.4 1.5 %copy-start = (bf16[3,3,384,256]{3,2,1,0:T(8,128)(2,1)S(1)}, bf16[3,3,384,256]{3,2,1,0:T(8,128)(2,1)}, u32[]{:S(2)}) copy-start(bf16[3,3,384,256]{3,2,1,0:T(8,128)(2,1)} %param.18) | copy-start | bytes 5308420
  12.9 1.1 %copy-start.2 = (bf16[3072,81]{1,0:T(8,128)(2,1)S(1)}, bf16[3072,81]{1,0:T(8,128)(2,1)}, u32[]{:S(2)}) copy-start(bf16[3072,81]{1,0:T(8,128)(2,1)} %constant.25.clone.places_ref) | copy-start | bytes 1492996
  14.0 0.7 %copy-start.5 = (bf16[81,128]{1,0:T(8,128)(2,1)S(1)}, bf16[81,128]{1,0:T(8,128)(2,1)}, u32[]{:S(2)}) copy-start(bf16[81,128]{1,0:T(8,128)(2,1)} %stem_ref.1) | copy-start | bytes 62212
  14.8 22.4 %copy-start.1 = (bf16[3,3,384,256]{3,2,1,0:T(8,128)(2,1)S(1)}, bf16[3,3,384,256]{3,2,1,0:T(8,128)(2,1)}, u32[]{:S(2)}) copy-start(bf16[3,3,384,256]{3,2,1,0:T(8,128)(2,1)} %param.18) | copy-start | bytes 5308420
  15.5 0.9 %copy-start.3 = (bf16[8,384,128]{2,1,0:T(8,128)(2,1)}, bf16[8,384,128]{2,1,0:T(8,128)(2,1)S(1)}, u32[]{:S(2)}) copy-start(bf16[8,384,128]{2,1,0:T(8,128)(2,1)S(1)} %get-tuple-element.25.w4_hbm) | copy-start | bytes 2359300
  23.2 13.9 %all-to-all-start.1 = ((bf16[16,3,4,256]{3,2,1,0:T(4,128)(2,1)}), bf16[16,3,4,256]{3,2,1,0:T(4,128)(2,1)S(1)}, u32[]{:S(2)}, u32[]{:S(2)}) async-start(bf16[16,3,4,256]{3,2,1,0:T(4,128)(2,1)} %shard_map.120), calls=%async_computation.1 | async-start | bytes 196608 | tf_op jit(solution)/shard_map/all_to_all | solution.py:325
  37.2 17.2 %copy-start.4 = (bf16[1024,256]{1,0:T(8,128)(2,1)S(1)}, bf16[1024,256]{1,0:T(8,128)(2,1)}, u32[]{:S(2)}) copy-start(bf16[1024,256]{1,0:T(8,128)(2,1)} %dw_ref.1) | copy-start | bytes 1572868
  37.2 17.2 %copy-start.6 = (f32[256]{0:T(256)S(1)}, f32[256]{0:T(256)}, u32[]{:S(2)}) copy-start(f32[256]{0:T(256)} %param.19) | copy-start | bytes 3076
  37.2 17.2 %copy-start.7 = (f32[256]{0:T(256)S(1)}, f32[256]{0:T(256)}, u32[]{:S(2)}) copy-start(f32[256]{0:T(256)} %param.20) | copy-start | bytes 3076
  37.2 17.2 %copy-start.8 = (f32[256]{0:T(256)S(1)}, f32[256]{0:T(256)}, u32[]{:S(2)}) copy-start(f32[256]{0:T(256)} %param.22) | copy-start | bytes 3076
  47.0 3.7 %collective-permute-start.4 = (f32[2,256]{1,0:T(2,128)S(1)}, f32[2,256]{1,0:T(2,128)S(1)}, u32[]{:S(2)}, u32[]{:S(2)}) collective-permute-start(f32[2,256]{1,0:T(2,128)S(1)} %get-tuple-element.28.stat_a), channel_id=1, source_target_pairs={{0,12},{4,0},{8,4},{12,8},{1,13},{5,1},{9,5},{13,9},{2,14},{6,2},{... | collective-permute-start | bytes 6152 | tf_op jit(solution)/shard_map/ppermute | solution.py:351
  48.1 5.1 %collective-permute-start.3 = (f32[2,256]{1,0:T(2,128)S(1)}, f32[2,256]{1,0:T(2,128)S(1)}, u32[]{:S(2)}, u32[]{:S(2)}) collective-permute-start(f32[2,256]{1,0:T(2,128)S(1)} %get-tuple-element.28.stat_a), channel_id=1, source_target_pairs={{0,8},{4,12},{8,0},{12,4},{1,9},{5,13},{9,1},{13,5},{2,10},{6,14},... | collective-permute-start | bytes 6152 | tf_op jit(solution)/shard_map/ppermute | solution.py:351
  49.6 4.8 %collective-permute-start.2 = (f32[2,256]{1,0:T(2,128)S(1)}, f32[2,256]{1,0:T(2,128)S(1)}, u32[]{:S(2)}, u32[]{:S(2)}) collective-permute-start(f32[2,256]{1,0:T(2,128)S(1)} %get-tuple-element.28.stat_a), channel_id=1, source_target_pairs={{0,4},{4,8},{8,12},{12,0},{1,5},{5,9},{9,13},{13,1},{2,6},{6,10},{... | collective-permute-start | bytes 6152 | tf_op jit(solution)/shard_map/ppermute | solution.py:351

commit v5 on v4

--- a/solution.py
+++ b/solution.py
@@ -22,18 +22,26 @@
     return lax.broadcasted_iota(jnp.int32, shape, dim)
 
 
-def weights_kernel(places_ref, stem_ref, mw_ref, w4_ref, mid_ref):
+def weights_kernel(places_hbm, stem_hbm, mw_hbm, w4_ref, taps_ref, places, stem, mw, sems):
+    pairs = ((places_hbm, places), (stem_hbm, stem), (mw_hbm, mw))
+    copies = [pltpu.make_async_copy(src, dst, sems.at[i]) for i, (src, dst) in enumerate(pairs)]
+    for copy in copies:
+        copy.start()
+    copies[0].wait()
+    copies[1].wait()
     for n in range(8):
-        part = places_ref[384 * n : 384 * n + 384, :]
-        w4_ref[n] = jnp.dot(part, stem_ref[...], preferred_element_type=F32).astype(BF16)
+        part = places[256 * n : 256 * n + 256, :]
+        w4_ref[n] = jnp.dot(part, stem[...], preferred_element_type=F32).astype(BF16)
+    copies[2].wait()
     for k in range(9):
-        g0, g1, g2 = (
-            mw_ref[384 * k + 128 * c : 384 * k + 128 * c + 128].astype(F32) for c in range(3)
-        )
-        outer = (g0 + g2) * 0.5
-        inner = g1 * 0.5
-        mid_ref[0, 128 * k : 128 * k + 128] = (outer + inner).astype(BF16)
-        mid_ref[1, 128 * k : 128 * k + 128] = (outer - inner).astype(BF16)
+        g0, g1, g2 = (mw[384 * k + 128 * c : 384 * k + 128 * c + 128] for c in range(3))
+        outer = (g0.astype(F32) + g2.astype(F32)) * 0.5
+        inner = g1.astype(F32) * 0.5
+        at = slice(128 * k, 128 * k + 128)
+        taps_ref[0, at] = g0
+        taps_ref[1, at] = (outer + inner).astype(BF16)
+        taps_ref[2, at] = (outer - inner).astype(BF16)
+        taps_ref[3, at] = g2
 
 
 def fetch_kernel(keep, train, fr, keep_out, train_out, fr_out, sems):
@@ -103,18 +111,17 @@
 def mixer_kernel(
     y_ref,
     raw_ref,
-    w4_hbm,
+    w4_ref,
     gain_hbm,
     shift_hbm,
-    mw_ref,
-    mid_ref,
+    taps_ref,
     mix_ref,
     stat_ref,
     dv,
+    rows,
     tg,
     stem,
     hid,
-    w4_ref,
     gain_ref,
     shift_ref,
     sems,
@@ -123,7 +130,6 @@
     copies = [
         pltpu.make_async_copy(gain_hbm, gain_ref, sems.at[0]),
         pltpu.make_async_copy(shift_hbm, shift_ref, sems.at[1]),
-        pltpu.make_async_copy(w4_hbm, w4_ref, sems.at[2]),
     ]
     for copy in copies:
         copy.start()
@@ -132,35 +138,38 @@
             for ch in range(3):
                 piece = raw_ref[yy * 4 + xx, ch].astype(F32)
                 for par in range(2):
-                    dv[1 + par, ch, 4 + 4 * xx : 8 + 4 * xx, 128 * yy : 128 * yy + 128] = piece[
+                    dv[par, ch, 4 * xx : 4 * xx + 4, 128 * yy : 128 * yy + 128] = piece[
                         :, 128 * par : 128 * par + 128
                     ]
-    pair = iota((16, 512), 1) & 31
+    lane = iota((16, 512), 1)
+    pair = lane & 31
     for ch in range(3):
-        even = dv[1, ch, 4:20, :]
-        odd = dv[2, ch, 4:20, :]
-        dv[0, ch, 4:20, :] = jnp.where(pair == 0, 0.0, pltpu.roll(odd, 1, 1))
-        dv[3, ch, 4:20, :] = jnp.where(pair == 31, 0.0, pltpu.roll(even, 511, 1))
-    for v in range(4):
-        for ch in range(3):
-            dv[v, ch, 0:4, :] = jnp.broadcast_to(dv[v, ch, 4:5, :], (4, 512))
-    edge = jnp.zeros((32, 128), BF16)
+        even = dv[0, ch]
+        odd = dv[1, ch]
+        before = jnp.where(pair == 0, 0.0, pltpu.roll(odd, 1, 1))
+        after = jnp.where(pair == 31, 0.0, pltpu.roll(even, 511, 1))
+        for v, plane in enumerate((before, even, odd, after)):
+            above = jnp.where(lane < 32, 0.0, pltpu.roll(plane, 32, 1))
+            below = jnp.where(lane >= 480, 0.0, pltpu.roll(plane, 480, 1))
+            at = v * 3 + ch
+            for b, part in enumerate((above, plane, below)):
+                for j in range(4):
+                    cut = part[:, 128 * j : 128 * j + 128]
+                    rows[b, j, pl.ds(24 + at, 16, stride=12), :] = cut
+                    rows[b, j, at : at + 1, :] = cut[0:1]
+                    rows[b, j, 12 + at : 13 + at, :] = cut[0:1]
     for g in range(4):
-        tg[g, 0:32, :] = edge
-        tg[g, 544:576, :] = edge
-        rows = [dv[v, ch, 4 * g : 4 * g + 8, :] for v in range(4) for ch in range(3)]
-        block = jnp.concatenate(rows + [jnp.zeros((32, 512), F32)], axis=0)
-        tg[g, 32:544, :] = jnp.transpose(block).astype(BF16)
-    for copy in copies:
-        copy.wait()
+        for j in range(4):
+            taps = [rows[b, j, 48 * g : 48 * g + 72, :] for b in range(3)]
+            block = jnp.concatenate(taps + [jnp.zeros((40, 128), F32)], axis=0)
+            tg[g, 128 * j : 128 * j + 128, :] = jnp.transpose(block).astype(BF16)
     total = jnp.zeros((8, 1024), F32)
     square = jnp.zeros((8, 1024), F32)
     for g in range(4):
         stem[g, 0:32, :] = jnp.zeros((32, 1024), F32)
         stem[g, 544:576, :] = jnp.zeros((32, 1024), F32)
-        left = jnp.concatenate([tg[g, 32 * b : 32 * b + 512, :] for b in range(3)], axis=1)
         w4 = jnp.concatenate([w4_ref[n] for n in range(8)], axis=1)
-        out = jnp.dot(left, w4, preferred_element_type=F32)
+        out = jnp.dot(tg[g], w4, preferred_element_type=F32)
         stem[g, 32:544, :] = out
         parts = out.reshape(64, 8, 1024)
         total = total + jnp.sum(parts, axis=0)
@@ -169,20 +178,28 @@
     square = jnp.sum(square, axis=0, keepdims=True)
     total = sum(total[:, 128 * k : 128 * k + 128] for k in range(8))
     square = sum(square[:, 128 * k : 128 * k + 128] for k in range(8))
+    for copy in copies:
+        copy.wait()
     scale, offset = group_scale(total, square, 16384, 4, gain_ref[...], shift_ref[...])
     at = iota((192, 128), 0)
-    row = at >> 5
-    valid = jnp.logical_and(
-        jnp.logical_or(row > 0, y > 0), jnp.logical_or(row < 5, y < 3)
-    )
     first = (at & 31) == 0
     last = (at & 31) == 31
     start = pl.multiple_of(y * 128, 128)
-    for f in range(16):
+    top = jnp.where(y > 0, 1.0, 0.0)
+    bottom = jnp.where(y < 3, 1.0, 0.0)
+    scale = scale * 0.5
+    offset = offset * 0.5
+
+    def act(val):
+        half = val * scale + offset
+        out = half + half * jnp.tanh(half)
+        return jnp.concatenate([out[:32] * top, out[32:160], out[160:] * bottom], axis=0)
+
+    def make_hidden(f):
         g, fo = divmod(f, 4)
         val = stem[g, pl.ds(start, 192), 256 * fo : 256 * fo + 256]
-        even = jnp.where(valid, silu(val[:, :128] * scale + offset), 0.0)
-        odd = jnp.where(valid, silu(val[:, 128:] * scale + offset), 0.0)
+        even = act(val[:, :128])
+        odd = act(val[:, 128:])
         before = jnp.where(first, 0.0, pltpu.roll(odd, 1, 0))
         after = jnp.where(last, 0.0, pltpu.roll(even, 191, 0))
         parts = (before - odd, even + odd, odd - even, even - after)
@@ -196,17 +213,11 @@
     s = jnp.zeros((8, 256), F32)
     q = jnp.zeros((8, 256), F32)
     steps = [(a, b) for a in range(3) for b in range(3)]
-    first_tap = [mw_ref[384 * k : 384 * k + 128] for k in range(9)]
-    last_tap = [mw_ref[384 * k + 256 : 384 * k + 384] for k in range(9)]
-    weights = (
-        jnp.concatenate(first_tap[:8], axis=0),
-        mid_ref[0, :1024],
-        mid_ref[1, :1024],
-        jnp.concatenate(last_tap[:8], axis=0),
-    )
-    tail_even = jnp.concatenate([first_tap[8], mid_ref[0, 1024:]], axis=0)
-    tail_odd = jnp.concatenate([mid_ref[0, 1024:], -last_tap[8]], axis=0)
-    tail_both = mid_ref[1, 1024:]
+    tail_even = jnp.concatenate([taps_ref[0, 1024:], taps_ref[1, 1024:]], axis=0)
+    tail_odd = jnp.concatenate([taps_ref[1, 1024:], -taps_ref[3, 1024:]], axis=0)
+    tail_both = taps_ref[2, 1024:]
+    for k in range(16):
+        make_hidden(k)
     for f in range(0, 16, 4):
 
         def tap(k, a, b):
@@ -216,7 +227,7 @@
         m = []
         for k in range(4):
             left = jnp.concatenate([tap(k, a, b) for a, b in steps[:8]], axis=1)
-            m.append(jnp.dot(left, weights[k], preferred_element_type=F32))
+            m.append(jnp.dot(left, taps_ref[k, :1024], preferred_element_type=F32))
         t = [tap(k, 2, 2) for k in range(4)]
         even = jnp.dot(jnp.concatenate([t[0], t[1]], axis=1), tail_even, preferred_element_type=F32)
         odd = jnp.dot(jnp.concatenate([t[1], t[3]], axis=1), tail_odd, preferred_element_type=F32)
@@ -251,16 +262,16 @@
 
 
 def stem_places():
-    place = np.zeros((8, 3, 128, 81), np.float32)
+    place = np.zeros((8, 256, 81), np.float32)
     for fo in range(4):
         for par in range(2):
             for a in range(3):
                 for b in range(3):
                     for c in range(3):
                         for ch in range(3):
-                            row = (par + c) * 24 + ch * 8 + fo + 2 + a
-                            place[fo * 2 + par, b, row, ((a * 3 + b) * 3 + c) * 3 + ch] = 1
-    return place.reshape(3072, 81)
+                            row = b * 72 + (fo + a) * 12 + (par + c) * 3 + ch
+                            place[fo * 2 + par, row, ((a * 3 + b) * 3 + c) * 3 + ch] = 1
+    return place.reshape(2048, 81)
 
 
 def in_hbm(array):
@@ -307,13 +318,6 @@
     packed = call(
         pack_kernel, sds((8, 4, 3, 4, 256), BF16), [SMEM] * 4 + [VMEM] * 2
     )(core, keep_a, keep_b, train, frames_a, frames_b)
-    places = jnp.asarray(stem_places(), BF16)
-    packed, mixer_weight = lax.optimization_barrier((packed, mixer_weight.reshape(3456, 256)))
-    w4, middle = call(
-        weights_kernel,
-        (sds((8, 384, 128), BF16), sds((2, 1152, 256), BF16)),
-        [VMEM] * 3,
-    )(places, stem_weight, mixer_weight)
     along_z = [[2 * z + k for z in range(8)] for k in range(2)]
     received = lax.all_to_all(
         packed, "clip", split_axis=0, concat_axis=0, tiled=True, axis_index_groups=along_z
@@ -321,31 +325,42 @@
     pieces = call(
         combine_kernel, sds((16, 3, 4, 256), BF16), [VMEM], [pltpu.VMEM((48, 256), F32)]
     )(received)
-    pieces, w4, middle = lax.optimization_barrier((pieces, w4, middle))
+    places = jnp.asarray(stem_places(), BF16)
+    pieces, places = lax.optimization_barrier((pieces, places))
+    w4, taps = call(
+        weights_kernel,
+        (sds((8, 256, 128), BF16), sds((4, 1152, 256), BF16)),
+        [HBM] * 3,
+        [
+            pltpu.VMEM((2048, 81), BF16),
+            pltpu.VMEM((81, 128), BF16),
+            pltpu.VMEM((3456, 256), BF16),
+            pltpu.SemaphoreType.DMA((3,)),
+        ],
+    )(in_hbm(places), in_hbm(stem_weight), in_hbm(mixer_weight.reshape(3456, 256)))
     raw = lax.all_to_all(pieces, ("row", "tm"), split_axis=0, concat_axis=0, tiled=True)
     mix, stat = call(
         mixer_kernel,
         (sds((2, 16, 128, 256), F32), sds((2, 256), F32)),
-        [SMEM, VMEM, HBM, HBM, HBM, VMEM, VMEM],
+        [SMEM, VMEM, VMEM, HBM, HBM, VMEM],
         [
-            pltpu.VMEM((4, 3, 24, 512), F32),
-            pltpu.VMEM((4, 576, 128), BF16),
+            pltpu.VMEM((2, 3, 16, 512), F32),
+            pltpu.VMEM((3, 4, 216, 128), F32),
+            pltpu.VMEM((4, 512, 256), BF16),
             pltpu.VMEM((4, 576, 1024), F32),
             pltpu.VMEM((18, 192, 512), BF16),
-            pltpu.VMEM((8, 384, 128), BF16),
             pltpu.VMEM((1, 128), F32),
             pltpu.VMEM((1, 128), F32),
-            pltpu.SemaphoreType.DMA((3,)),
+            pltpu.SemaphoreType.DMA((2,)),
         ],
         mib=24,
     )(
         row,
         raw,
-        in_hbm(w4),
+        w4,
         in_hbm(stem_gain.reshape(1, -1)),
         in_hbm(stem_shift.reshape(1, -1)),
-        mixer_weight,
-        middle,
+        taps,
     )
     others = [
         lax.ppermute(stat, "row", [(i, (i + by) % 4) for i in range(4)]) for by in (1, 2, 3)

time: 66.3 us -> 63.3 us (0.955)
  blocking collectives: 9.18 us -> 28.4 us
  starting transfers between devices: 19 us -> 10.6 us
  waiting for transfers between devices: 17.3 us -> 9.12 us
  local copies, waits for them, and re-layouts: 4.94 us -> 0.73 us
  Pallas kernels: 15.3 us -> 14.1 us
    all_to_all x0 -> x1, blocking collectives: none -> 19.2 us  [local(): lax.all_to_all(packed, 'clip', split_axis=0, concat_axis=0, tiled=True, a...]
    all_to_all x1 -> x0, starting transfers between devices: 8.47 us -> none  [local(): lax.all_to_all(packed, 'clip', split_axis=0, concat_axis=0, tiled=True, a...]
    all_to_all x1 -> x0, waiting for transfers between devices: 6.01 us -> none  [local(): lax.all_to_all(packed, 'clip', split_axis=0, concat_axis=0, tiled=True, a...]
    unnamed x19 -> x9, local copies, waits for them, and re-layouts: 4.94 us -> 0.73 us
    all_to_all x1, waiting for transfers between devices: 6.45 us -> 4.27 us  [local(): lax.all_to_all(pieces, ('row', 'tm'), split_axis=0, concat_axis=0, tiled=...]
    pallas_call x1, Pallas kernels: 9.82 us -> 7.89 us  [local(): call(mixer_kernel, (sds((2, 16, 128, 256), F32), sds((2, 256), F32)), [SM...]
    pallas_call x1, Pallas kernels: 0.73 us -> 2.13 us  [local(): call(weights_kernel, (sds((8, 256, 128), BF16), sds((4, 1152, 256), BF16)...]
    pallas_call x1, Pallas kernels: 1.48 us -> 0.8 us  [local(): call(pack_kernel, sds((8, 4, 3, 4, 256), BF16), [SMEM] * 4 + [VMEM] * 2)]
  transfers between devices with their start and end apart: 7 -> 6, of which waited for: 6 -> 5; matrix products, arithmetic and copies ran while one was open for 0% -> 0% of each run, Pallas kernels for 2% -> 5%
where the time goes in v5:
time: 63.3 us; the launch traced here: 63 us
  blocking collectives  28.4 us (45%)
  Pallas kernels  14.1 us (22%)
  starting transfers between devices  10.6 us (17%)
  waiting for transfers between devices  9.12 us (14%)
  local copies, waits for them, and re-layouts  0.73 us (1%)
    all_to_all x1, blocking collectives, local(): lax.all_to_all(packed, 'clip', split_axis=0, concat_axis=0, tiled=True, a...  19.2 us
    all_to_all x1, blocking collectives, local(): lax.all_to_all(latent.reshape(4, 2, 2, 32, 256), 'tm', split_axis=0, conc...  9.18 us
    pallas_call x1, Pallas kernels, local(): call(mixer_kernel, (sds((2, 16, 128, 256), F32), sds((2, 256), F32)), [SM...  7.89 us
    all_to_all x1, starting transfers between devices, local(): lax.all_to_all(pieces, ('row', 'tm'), split_axis=0, concat_axis=0, tiled=...  7.48 us
    ppermute x3, waiting for transfers between devices, local(): lax.ppermute(stat, 'row', [(i, (i + by) % 4) for i in range(4)])  4.77 us
    all_to_all x1, waiting for transfers between devices, local(): lax.all_to_all(pieces, ('row', 'tm'), split_axis=0, concat_axis=0, tiled=...  4.27 us
    ppermute x3, starting transfers between devices, local(): lax.ppermute(stat, 'row', [(i, (i + by) % 4) for i in range(4)])  2.56 us
    pallas_call x1, Pallas kernels, local(): call(weights_kernel, (sds((8, 256, 128), BF16), sds((4, 1152, 256), BF16)...  2.13 us
  transfers between devices with their start and end apart: 6, of which 5 were waited for; matrix products, arithmetic and copies ran while one was open for 0% of the time, Pallas kernels for 5%

profile of v5, /device:TPU:2, one launch (start us, length us, event | category | flops | bytes accessed | tf_op | source)
XLA Modules:
  0.0 63.0 jit_solution(954800406398318829)
XLA Ops:
  0.0 0.0 collective-permute-start.1
  0.0 0.5 collective-permute-start
  0.5 0.9 %shard_map.118 = (s32[8]{0:T(128)S(1)}, s32[64]{0:T(128)S(1)}, bf16[8,3,4,256]{3,2,1,0:T(4,128)(2,1)S(1)}) custom-call(s32[8]{0:T(128)} %keep.1, s32[64]{0:T(128)} %train.1, bf16[8,3,4,256]{3,2,1,0:T(4,128)(2,1)} %fr.1), custom_call_target="tpu_custom_call" | custom-call | tf_op jit(solution)/shard_map/pallas_call | solution.py:312
  1.4 0.1 collective-permute-done.keep_t
  1.5 0.0 collective-permute-done.1.frb
  1.5 0.8 %shard_map.119 = bf16[8,4,3,4,256]{4,3,2,1,0:T(4,128)(2,1)S(1)} custom-call(s32[1]{0:T(128)} %bitcast.1.core_ref, s32[8]{0:T(128)S(1)} %get-tuple-element.14.keep_s, s32[8]{0:T(128)S(1)} %collective-permute-done.keep_t, s32[64]{0:T(128)S(1)} %get-tuple-element.15.train_s, bf16[8,3,4,256]{3,2,1,0:T(4,128)(2,1)S(1)} %get-tuple-element.16.fra, ...), custom_call_target="tpu_custom_call" | custom-call | tf_op jit(solution)/shard_map/pallas_call | solution.py:318
  2.3 19.2 %all_to_all.15.recv_ref = bf16[8,4,3,4,256]{4,3,2,1,0:T(4,128)(2,1)S(1)} all-to-all(bf16[8,4,3,4,256]{4,3,2,1,0:T(4,128)(2,1)S(1)} %shard_map.119), channel_id=1, replica_groups={{0,32,64,96,128,160,192,224},{16,48,80,112,144,176,208,240},{1,33,65,97..., dimensions={0} | all-to-all | bytes 393216 | tf_op jit(solution)/shard_map/all_to_all | solution.py:322
  21.5 0.8 %shard_map.120 = bf16[16,3,4,256]{3,2,1,0:T(4,128)(2,1)} custom-call(bf16[8,4,3,4,256]{4,3,2,1,0:T(4,128)(2,1)S(1)} %all_to_all.15.recv_ref), custom_call_target="tpu_custom_call" | custom-call | tf_op jit(solution)/shard_map/pallas_call | solution.py:325
  22.4 7.5 %all-to-all-start.1 = ((bf16[16,3,4,256]{3,2,1,0:T(4,128)(2,1)}), bf16[16,3,4,256]{3,2,1,0:T(4,128)(2,1)S(1)}, u32[]{:S(2)}, u32[]{:S(2)}) async-start(bf16[16,3,4,256]{3,2,1,0:T(4,128)(2,1)} %shard_map.120), calls=%async_computation.1 | async-start | bytes 196608 | tf_op jit(solution)/shard_map/all_to_all | solution.py:341
  29.8 0.0 copy-start.1
  29.9 0.0 copy-start.2
  29.9 0.0 copy-start.3
  29.9 2.1 %shard_map.121 = (bf16[8,256,128]{2,1,0:T(8,128)(2,1)S(1)}, bf16[4,1152,256]{2,1,0:T(8,128)(2,1)S(1)}) custom-call(bf16[2048,81]{1,0:T(8,128)(2,1)} %constant.25.clone.places_hbm, bf16[81,128]{1,0:T(8,128)(2,1)} %stem_hbm.1, bf16[3456,256]{1,0:T(8,128)(2,1)} %bitcast.13), custom_call_target="tpu_custom_call" | custom-call | tf_op jit(solution)/shard_map/pallas_call | solution.py:330
  32.0 4.3 %all-to-all-done.1.raw_ref = bf16[16,3,4,256]{3,2,1,0:T(4,128)(2,1)S(1)} async-done(((bf16[16,3,4,256]{3,2,1,0:T(4,128)(2,1)}), bf16[16,3,4,256]{3,2,1,0:T(4,128)(2,1)S(1)}, u32[]{:S(2)}, u32[]{:S(2)}) %all-to-all-start.1) | async-done | bytes 98336 | tf_op jit(solution)/shard_map/all_to_all | solution.py:341
  36.3 7.9 %shard_map.122 = (f32[2,16,128,256]{3,2,1,0:T(8,128)S(1)}, f32[2,256]{1,0:T(2,128)S(1)}) custom-call(s32[1]{0:T(128)} %bitcast.y_ref, bf16[16,3,4,256]{3,2,1,0:T(4,128)(2,1)S(1)} %all-to-all-done.1.raw_ref, bf16[8,256,128]{2,1,0:T(8,128)(2,1)S(1)} %get-tuple-element.19.w4_ref, f32[1,128]{1,0:T(1,128)} %bitcast.14, f32[1,128]{1,0:T(1,128)} %bitcast.15, ...), custom_call_target="tpu_custom_call" | custom-call | tf_op jit(solution)/shard_map/pallas_call | solution.py:342
  44.2 1.1 %collective-permute-start.4 = (f32[2,256]{1,0:T(2,128)S(1)}, f32[2,256]{1,0:T(2,128)S(1)}, u32[]{:S(2)}, u32[]{:S(2)}) collective-permute-start(f32[2,256]{1,0:T(2,128)S(1)} %get-tuple-element.22.stat_a), channel_id=1, source_target_pairs={{0,12},{4,0},{8,4},{12,8},{1,13},{5,1},{9,5},{13,9},{2,14},{6,2},{... | collective-permute-start | bytes 6152 | tf_op jit(solution)/shard_map/ppermute | solution.py:366
  45.3 1.5 %collective-permute-start.3 = (f32[2,256]{1,0:T(2,128)S(1)}, f32[2,256]{1,0:T(2,128)S(1)}, u32[]{:S(2)}, u32[]{:S(2)}) collective-permute-start(f32[2,256]{1,0:T(2,128)S(1)} %get-tuple-element.22.stat_a), channel_id=1, source_target_pairs={{0,8},{4,12},{8,0},{12,4},{1,9},{5,13},{9,1},{13,5},{2,10},{6,14},... | collective-permute-start | bytes 6152 | tf_op jit(solution)/shard_map/ppermute | solution.py:366
  46.7 0.0 collective-permute-start.2
  46.8 1.1 %collective-permute-done.4.stat_d = f32[2,256]{1,0:T(2,128)S(1)} collective-permute-done((f32[2,256]{1,0:T(2,128)S(1)}, f32[2,256]{1,0:T(2,128)S(1)}, u32[]{:S(2)}, u32[]{:S(2)}) %collective-permute-start.4) | collective-permute-done | bytes 2080 | tf_op jit(solution)/shard_map/ppermute | solution.py:366
  47.8 2.5 %collective-permute-done.3.stat_c = f32[2,256]{1,0:T(2,128)S(1)} collective-permute-done((f32[2,256]{1,0:T(2,128)S(1)}, f32[2,256]{1,0:T(2,128)S(1)}, u32[]{:S(2)}, u32[]{:S(2)}) %collective-permute-start.3) | collective-permute-done | bytes 2080 | tf_op jit(solution)/shard_map/ppermute | solution.py:366
  50.3 1.2 %collective-permute-done.2.stat_b = f32[2,256]{1,0:T(2,128)S(1)} collective-permute-done((f32[2,256]{1,0:T(2,128)S(1)}, f32[2,256]{1,0:T(2,128)S(1)}, u32[]{:S(2)}, u32[]{:S(2)}) %collective-permute-start.2) | collective-permute-done | bytes 2080 | tf_op jit(solution)/shard_map/ppermute | solution.py:366
  51.5 1.6 %shard_map.123 = bf16[512,256]{1,0:T(8,128)(2,1)S(1)} custom-call(f32[2,16,128,256]{3,2,1,0:T(8,128)S(1)} %get-tuple-element.21.mix_ref, f32[2,256]{1,0:T(2,128)S(1)} %get-tuple-element.22.stat_a, f32[2,256]{1,0:T(2,128)S(1)} %collective-permute-done.2.stat_b, f32[2,256]{1,0:T(2,128)S(1)} %collective-permute-done.3.stat_c, ...), custom_call_target="tpu_custom_call" | custom-call | tf_op jit(solution)/shard_map/pallas_call | solution.py:368
  53.1 9.2 %all_to_all.16 = bf16[4,2,2,32,256]{4,3,2,1,0:T(8,128)(2,1)S(1)} all-to-all(bf16[4,2,2,32,256]{4,3,2,1,0:T(8,128)(2,1)S(1)} %bitcast.9), channel_id=1, replica_groups=mesh['clip'=16,'row'=4,'tm'=4] {'tm'}, dimensions={0} | all-to-all | bytes 524288 | tf_op jit(solution)/shard_map/all_to_all | solution.py:379
  62.3 0.7 %copy.14 = bf16[4,2,2,32,256]{4,3,2,1,0:T(8,128)(2,1)} copy(bf16[4,2,2,32,256]{4,3,2,1,0:T(8,128)(2,1)S(1)} %all_to_all.16) | data formatting | bytes 524288
  (5 shorter events, 0.0 us)
Async XLA Ops:
  0.0 1.5 %collective-permute-start.1 = (bf16[8,3,4,256]{3,2,1,0:T(4,128)(2,1)}, bf16[8,3,4,256]{3,2,1,0:T(4,128)(2,1)S(1)}, u32[]{:S(2)}, u32[]{:S(2)}) collective-permute-start(bf16[8,3,4,256]{3,2,1,0:T(4,128)(2,1)} %fr.1), channel_id=1, source_target_pairs={{0,16},{16,0},{32,48},{48,32},{64,80},{80,64},{96,112},{112,96},{1... | collective-permute-start | bytes 147464 | tf_op jit(solution)/shard_map/ppermute | solution.py:310
  0.0 1.5 %collective-permute-start = (s32[8]{0:T(128)}, s32[8]{0:T(128)S(1)}, u32[]{:S(2)}, u32[]{:S(2)}) collective-permute-start(s32[8]{0:T(128)} %keep.1), channel_id=1, source_target_pairs={{0,16},{16,0},{32,48},{48,32},{64,80},{80,64},{96,112},{112,96},{1... | collective-permute-start | bytes 104 | tf_op jit(solution)/shard_map/ppermute | solution.py:311
  22.4 13.9 %all-to-all-start.1 = ((bf16[16,3,4,256]{3,2,1,0:T(4,128)(2,1)}), bf16[16,3,4,256]{3,2,1,0:T(4,128)(2,1)S(1)}, u32[]{:S(2)}, u32[]{:S(2)}) async-start(bf16[16,3,4,256]{3,2,1,0:T(4,128)(2,1)} %shard_map.120), calls=%async_computation.1 | async-start | bytes 196608 | tf_op jit(solution)/shard_map/all_to_all | solution.py:341
  29.8 21.7 %copy-start = (bf16[1024,256]{1,0:T(8,128)(2,1)S(1)}, bf16[1024,256]{1,0:T(8,128)(2,1)}, u32[]{:S(2)}) copy-start(bf16[1024,256]{1,0:T(8,128)(2,1)} %dw_ref.1) | copy-start | bytes 1572868
  29.8 21.7 %copy-start.1 = (f32[256]{0:T(256)S(1)}, f32[256]{0:T(256)}, u32[]{:S(2)}) copy-start(f32[256]{0:T(256)} %param.19) | copy-start | bytes 3076
  29.9 21.7 %copy-start.2 = (f32[256]{0:T(256)S(1)}, f32[256]{0:T(256)}, u32[]{:S(2)}) copy-start(f32[256]{0:T(256)} %param.20) | copy-start | bytes 3076
  29.9 21.7 %copy-start.3 = (f32[256]{0:T(256)S(1)}, f32[256]{0:T(256)}, u32[]{:S(2)}) copy-start(f32[256]{0:T(256)} %param.22) | copy-start | bytes 3076
  44.2 3.7 %collective-permute-start.4 = (f32[2,256]{1,0:T(2,128)S(1)}, f32[2,256]{1,0:T(2,128)S(1)}, u32[]{:S(2)}, u32[]{:S(2)}) collective-permute-start(f32[2,256]{1,0:T(2,128)S(1)} %get-tuple-element.22.stat_a), channel_id=1, source_target_pairs={{0,12},{4,0},{8,4},{12,8},{1,13},{5,1},{9,5},{13,9},{2,14},{6,2},{... | collective-permute-start | bytes 6152 | tf_op jit(solution)/shard_map/ppermute | solution.py:366
  45.3 5.1 %collective-permute-start.3 = (f32[2,256]{1,0:T(2,128)S(1)}, f32[2,256]{1,0:T(2,128)S(1)}, u32[]{:S(2)}, u32[]{:S(2)}) collective-permute-start(f32[2,256]{1,0:T(2,128)S(1)} %get-tuple-element.22.stat_a), channel_id=1, source_target_pairs={{0,8},{4,12},{8,0},{12,4},{1,9},{5,13},{9,1},{13,5},{2,10},{6,14},... | collective-permute-start | bytes 6152 | tf_op jit(solution)/shard_map/ppermute | solution.py:366
  46.7 4.8 %collective-permute-start.2 = (f32[2,256]{1,0:T(2,128)S(1)}, f32[2,256]{1,0:T(2,128)S(1)}, u32[]{:S(2)}, u32[]{:S(2)}) collective-permute-start(f32[2,256]{1,0:T(2,128)S(1)} %get-tuple-element.22.stat_a), channel_id=1, source_target_pairs={{0,4},{4,8},{8,12},{12,0},{1,5},{5,9},{9,13},{13,1},{2,6},{6,10},{... | collective-permute-start | bytes 6152 | tf_op jit(solution)/shard_map/ppermute | solution.py:366

commit v6 on v5

--- a/solution.py
+++ b/solution.py
@@ -1,3 +1,5 @@
+import functools
+
 import jax
 import jax.numpy as jnp
 import numpy as np
@@ -6,8 +8,6 @@
 from jax.experimental.pallas import tpu as pltpu
 from jax.sharding import PartitionSpec as P
 
-GROUPS = 32
-COLS = 64
 F32 = jnp.float32
 BF16 = jnp.bfloat16
 eps = 1e-06
@@ -101,11 +101,6 @@
     spread = sums[1:2] - mean * mean
     scale = gain * lax.rsqrt(spread + eps)
     return scale, shift - mean * scale
-
-
-def silu(u):
-    half = 0.5 * u
-    return half + half * jnp.tanh(half)
 
 
 def mixer_kernel(
@@ -243,22 +238,64 @@
     stat_ref[1:2, :] = jnp.sum(q, axis=0, keepdims=True)
 
 
-def down_kernel(mix_ref, stat_a, stat_b, stat_c, stat_d, gain_ref, shift_ref, dw_ref, bias_ref, out_ref, left):
+def quarter(to, mix_ref, scale, offset, dw_ref, bias_ref, out_ref, left):
+    for g in range(2):
+        for par in range(2):
+            acts = []
+            for i in range(2):
+                half = mix_ref[par, 4 * to + 2 * g + i] * scale + offset
+                acts.append(half + half * jnp.tanh(half))
+            pooled = ((acts[0] + acts[1]) * 0.5).astype(BF16)
+            for r in range(4):
+                lane = ((r & 1) * 2 + par) * 256
+                at = g * 64 + (r >> 1) * 32
+                left[at : at + 32, lane : lane + 256] = pooled[32 * r : 32 * r + 32]
+    out = jnp.dot(left[...], dw_ref[...], preferred_element_type=F32) + bias_ref[...]
+    out_ref[...] = out.astype(BF16)
+
+
+def first_kernel(
+    by,
+    me_ref,
+    mix_ref,
+    stat_a,
+    stat_b,
+    stat_c,
+    stat_d,
+    gain_ref,
+    shift_ref,
+    dw_ref,
+    bias_ref,
+    out_ref,
+    affine_ref,
+    left,
+):
     stat = (stat_a[...] + stat_b[...]) + (stat_c[...] + stat_d[...])
     scale, offset = group_scale(
         stat[0:1, :], stat[1:2, :], 16384, 8, gain_ref[...], shift_ref[...]
     )
-    for g in range(8):
-        for par in range(2):
-            one = silu(mix_ref[par, 2 * g] * scale + offset)
-            two = silu(mix_ref[par, 2 * g + 1] * scale + offset)
-            pooled = ((one + two) * 0.5).astype(BF16)
-            for r in range(4):
-                lane = ((r & 1) * 2 + par) * 256
-                to = g * 64 + (r >> 1) * 32
-                left[to : to + 32, lane : lane + 256] = pooled[32 * r : 32 * r + 32]
-    out = jnp.dot(left[...], dw_ref[...], preferred_element_type=F32) + bias_ref[...]
-    out_ref[...] = out.astype(BF16)
+    scale = scale * 0.5
+    offset = offset * 0.5
+    affine_ref[0:1, :] = scale
+    affine_ref[1:2, :] = offset
+    quarter((me_ref[0] + by) & 3, mix_ref, scale, offset, dw_ref, bias_ref, out_ref, left)
+
+
+def next_kernel(by, me_ref, mix_ref, affine_ref, dw_ref, bias_ref, out_ref, left):
+    scale = affine_ref[0:1, :]
+    offset = affine_ref[1:2, :]
+    quarter((me_ref[0] + by) & 3, mix_ref, scale, offset, dw_ref, bias_ref, out_ref, left)
+
+
+def place_kernel(me_ref, own, one, two, three, out_ref, sems):
+    copies = [
+        pltpu.make_async_copy(part, out_ref.at[(me_ref[0] + 4 - by) & 3], sems.at[by])
+        for by, part in enumerate((own, one, two, three))
+    ]
+    for copy in copies:
+        copy.start()
+    for copy in copies:
+        copy.wait()
 
 
 def stem_places():
@@ -306,6 +343,8 @@
     index = lax.axis_index("clip")
     core = (index % 2).astype(jnp.int32).reshape(1)
     row = lax.axis_index("row").astype(jnp.int32).reshape(1)
+    me = lax.axis_index("tm").astype(jnp.int32).reshape(1)
+    core, row, me = lax.optimization_barrier((core, row, me))
     pairs = [(i, i ^ 1) for i in range(16)]
     frames_b = lax.ppermute(frames, "clip", pairs)
     keep_b = lax.ppermute(keep_list, "clip", pairs)
@@ -365,20 +404,44 @@
     others = [
         lax.ppermute(stat, "row", [(i, (i + by) % 4) for i in range(4)]) for by in (1, 2, 3)
     ]
-    latent = call(
-        down_kernel, sds((512, 256), BF16), [VMEM] * 9, [pltpu.VMEM((512, 1024), BF16)], mib=16
+    dw_bias = (down_weight, down_bias.reshape(1, -1))
+    part = sds((128, 256), BF16)
+    room = [pltpu.VMEM((128, 1024), BF16)]
+    parts = {}
+
+    def send(by):
+        return lax.ppermute(parts[by], "tm", [(i, (i + by) % 4) for i in range(4)])
+
+    parts[2], affine = call(
+        functools.partial(first_kernel, 2),
+        (part, sds((2, 256), F32)),
+        [SMEM] + [VMEM] * 9,
+        room,
     )(
+        me,
         mix,
         stat,
         *others,
         mixer_gain.reshape(1, -1),
         mixer_shift.reshape(1, -1),
-        down_weight,
-        down_bias.reshape(1, -1),
-    )
-    return lax.all_to_all(
-        latent.reshape(4, 2, 2, 32, 256), "tm", split_axis=0, concat_axis=0, tiled=True
-    )
+        *dw_bias,
+    )
+    parts[2] = send(2)
+    for by in (1, 3, 0):
+        parts[by] = call(
+            functools.partial(next_kernel, by), part, [SMEM] + [VMEM] * 4, room
+        )(me, mix, affine, *dw_bias)
+        if by:
+            parts[by] = send(by)
+    placed = pl.pallas_call(
+        place_kernel,
+        out_shape=pltpu.HBM((4, 128, 256), BF16),
+        in_specs=[SMEM] + [VMEM] * 4,
+        out_specs=HBM,
+        scratch_shapes=[pltpu.SemaphoreType.DMA((4,))],
+        compiler_params=pltpu.CompilerParams(vmem_limit_bytes=1 << 20),
+    )(me, *(parts[by] for by in range(4)))
+    return placed.reshape(4, 2, 2, 32, 256)
 
 
 def solution(mesh):

time: 63.3 us -> 62.8 us (level); the launches traced: 63 us -> 61.7 us
  blocking collectives: 28.4 us -> 19.2 us
  waiting for transfers between devices: 9.12 us -> 13 us
  starting transfers between devices: 10.6 us -> 14.2 us
  Pallas kernels: 14.1 us -> 15 us
  local copies, waits for them, and re-layouts: 0.73 us -> 0.02 us
    all_to_all x1 -> x0, blocking collectives: 9.18 us -> none  [local(): lax.all_to_all(latent.reshape(4, 2, 2, 32, 256), 'tm', split_axis=0, conc...]
    ppermute x0 -> x3, waiting for transfers between devices: none -> 3.87 us  [send(): return lax.ppermute(parts[by], 'tm', [(i, (i + by) % 4) for i in range(4)])]
    ppermute x0 -> x3, starting transfers between devices: none -> 3.62 us  [send(): return lax.ppermute(parts[by], 'tm', [(i, (i + by) % 4) for i in range(4)])]
    pallas_call x1 -> x5, Pallas kernels: 1.56 us -> 2.51 us  [the longest x3 1.1 us: local(): call(functools.partial(next_kernel, by), part, [SMEM] + [VMEM] * 4, room)]
    unnamed x9 -> x8, local copies, waits for them, and re-layouts: 0.73 us -> 0.02 us
  transfers between devices with their start and end apart: 6 -> 9, of which waited for: 5 -> 8; matrix products, arithmetic and copies ran while one was open for 0% -> 0% of each run, Pallas kernels for 5% -> 5%
where the time goes in v6:
time: 62.8 us; the launch traced here: 61.7 us
  blocking collectives  19.2 us (31%)
  Pallas kernels  15 us (24%)
  starting transfers between devices  14.2 us (23%)
  waiting for transfers between devices  13 us (21%)
    all_to_all x1, blocking collectives, local(): lax.all_to_all(packed, 'clip', split_axis=0, concat_axis=0, tiled=True, a...  19.2 us
    pallas_call x1, Pallas kernels, local(): call(mixer_kernel, (sds((2, 16, 128, 256), F32), sds((2, 256), F32)), [SM...  7.89 us
    all_to_all x1, starting transfers between devices, local(): lax.all_to_all(pieces, ('row', 'tm'), split_axis=0, concat_axis=0, tiled=...  7.48 us
    ppermute x3, waiting for transfers between devices, local(): lax.ppermute(stat, 'row', [(i, (i + by) % 4) for i in range(4)])  4.77 us
    all_to_all x1, waiting for transfers between devices, local(): lax.all_to_all(pieces, ('row', 'tm'), split_axis=0, concat_axis=0, tiled=...  4.27 us
    ppermute x3, waiting for transfers between devices, send(): return lax.ppermute(parts[by], 'tm', [(i, (i + by) % 4) for i in range(4)])  3.87 us
    ppermute x3, starting transfers between devices, send(): return lax.ppermute(parts[by], 'tm', [(i, (i + by) % 4) for i in range(4)])  3.62 us
    ppermute x3, starting transfers between devices, local(): lax.ppermute(stat, 'row', [(i, (i + by) % 4) for i in range(4)])  2.57 us
  transfers between devices with their start and end apart: 9, of which 8 were waited for; matrix products, arithmetic and copies ran while one was open for 0% of the time, Pallas kernels for 5%

profile of v6, /device:TPU:2, one launch (start us, length us, event | category | flops | bytes accessed | tf_op | source)
XLA Modules:
  0.0 61.7 jit_solution(14724967859161300650)
XLA Ops:
  0.0 0.5 collective-permute-start
  0.5 0.9 %shard_map.118 = (s32[8]{0:T(128)S(1)}, s32[64]{0:T(128)S(1)}, bf16[8,3,4,256]{3,2,1,0:T(4,128)(2,1)S(1)}) custom-call(s32[8]{0:T(128)} %keep.1, s32[64]{0:T(128)} %train.1, bf16[8,3,4,256]{3,2,1,0:T(4,128)(2,1)} %fr.1), custom_call_target="tpu_custom_call" | custom-call | tf_op jit(solution)/shard_map/pallas_call | solution.py:351
  1.5 0.8 %shard_map.119 = bf16[8,4,3,4,256]{4,3,2,1,0:T(4,128)(2,1)S(1)} custom-call(s32[1]{0:T(128)} %bitcast.core_ref, s32[8]{0:T(128)S(1)} %get-tuple-element.22.keep_s, s32[8]{0:T(128)S(1)} %collective-permute-done.keep_t, s32[64]{0:T(128)S(1)} %get-tuple-element.23.train_s, bf16[8,3,4,256]{3,2,1,0:T(4,128)(2,1)S(1)} %get-tuple-element.24.fra, ...), custom_call_target="tpu_custom_call" | custom-call | tf_op jit(solution)/shard_map/pallas_call | solution.py:357
  2.3 19.2 %all_to_all.10.recv_ref = bf16[8,4,3,4,256]{4,3,2,1,0:T(4,128)(2,1)S(1)} all-to-all(bf16[8,4,3,4,256]{4,3,2,1,0:T(4,128)(2,1)S(1)} %shard_map.119), channel_id=1, replica_groups={{0,32,64,96,128,160,192,224},{16,48,80,112,144,176,208,240},{1,33,65,97..., dimensions={0} | all-to-all | bytes 393216 | tf_op jit(solution)/shard_map/all_to_all | solution.py:361
  21.5 0.8 %shard_map.120 = bf16[16,3,4,256]{3,2,1,0:T(4,128)(2,1)} custom-call(bf16[8,4,3,4,256]{4,3,2,1,0:T(4,128)(2,1)S(1)} %all_to_all.10.recv_ref), custom_call_target="tpu_custom_call" | custom-call | tf_op jit(solution)/shard_map/pallas_call | solution.py:364
  22.4 7.5 %all-to-all-start.1 = ((bf16[16,3,4,256]{3,2,1,0:T(4,128)(2,1)}), bf16[16,3,4,256]{3,2,1,0:T(4,128)(2,1)S(1)}, u32[]{:S(2)}, u32[]{:S(2)}) async-start(bf16[16,3,4,256]{3,2,1,0:T(4,128)(2,1)} %shard_map.120), calls=%async_computation.1 | async-start | bytes 196608 | tf_op jit(solution)/shard_map/all_to_all | solution.py:380
  29.9 2.1 %shard_map.121 = (bf16[8,256,128]{2,1,0:T(8,128)(2,1)S(1)}, bf16[4,1152,256]{2,1,0:T(8,128)(2,1)S(1)}) custom-call(bf16[2048,81]{1,0:T(8,128)(2,1)} %constant.27.clone.places_hbm, bf16[81,128]{1,0:T(8,128)(2,1)} %stem_hbm.1, bf16[3456,256]{1,0:T(8,128)(2,1)} %bitcast.16), custom_call_target="tpu_custom_call" | custom-call | tf_op jit(solution)/shard_map/pallas_call | solution.py:369
  32.0 4.3 %all-to-all-done.1.raw_ref = bf16[16,3,4,256]{3,2,1,0:T(4,128)(2,1)S(1)} async-done(((bf16[16,3,4,256]{3,2,1,0:T(4,128)(2,1)}), bf16[16,3,4,256]{3,2,1,0:T(4,128)(2,1)S(1)}, u32[]{:S(2)}, u32[]{:S(2)}) %all-to-all-start.1) | async-done | bytes 98336 | tf_op jit(solution)/shard_map/all_to_all | solution.py:380
  36.3 7.9 %shard_map.122 = (f32[2,16,128,256]{3,2,1,0:T(8,128)S(1)}, f32[2,256]{1,0:T(2,128)S(1)}) custom-call(s32[1]{0:T(128)} %bitcast.1.y_ref, bf16[16,3,4,256]{3,2,1,0:T(4,128)(2,1)S(1)} %all-to-all-done.1.raw_ref, bf16[8,256,128]{2,1,0:T(8,128)(2,1)S(1)} %get-tuple-element.27.w4_ref, f32[1,128]{1,0:T(1,128)} %bitcast.17, f32[1,128]{1,0:T(1,128)} %bitcast.18, ...), custom_call_target="tpu_custom_call" | custom-call | tf_op jit(solution)/shard_map/pallas_call | solution.py:381
  44.2 1.1 %collective-permute-start.4 = (f32[2,256]{1,0:T(2,128)S(1)}, f32[2,256]{1,0:T(2,128)S(1)}, u32[]{:S(2)}, u32[]{:S(2)}) collective-permute-start(f32[2,256]{1,0:T(2,128)S(1)} %get-tuple-element.30.stat_a), channel_id=1, source_target_pairs={{0,12},{4,0},{8,4},{12,8},{1,13},{5,1},{9,5},{13,9},{2,14},{6,2},{... | collective-permute-start | bytes 6152 | tf_op jit(solution)/shard_map/ppermute | solution.py:405
  45.3 1.5 %collective-permute-start.3 = (f32[2,256]{1,0:T(2,128)S(1)}, f32[2,256]{1,0:T(2,128)S(1)}, u32[]{:S(2)}, u32[]{:S(2)}) collective-permute-start(f32[2,256]{1,0:T(2,128)S(1)} %get-tuple-element.30.stat_a), channel_id=1, source_target_pairs={{0,8},{4,12},{8,0},{12,4},{1,9},{5,13},{9,1},{13,5},{2,10},{6,14},... | collective-permute-start | bytes 6152 | tf_op jit(solution)/shard_map/ppermute | solution.py:405
  46.8 1.1 %collective-permute-done.4.stat_d = f32[2,256]{1,0:T(2,128)S(1)} collective-permute-done((f32[2,256]{1,0:T(2,128)S(1)}, f32[2,256]{1,0:T(2,128)S(1)}, u32[]{:S(2)}, u32[]{:S(2)}) %collective-permute-start.4) | collective-permute-done | bytes 2080 | tf_op jit(solution)/shard_map/ppermute | solution.py:405
  47.8 2.5 %collective-permute-done.3.stat_c = f32[2,256]{1,0:T(2,128)S(1)} collective-permute-done((f32[2,256]{1,0:T(2,128)S(1)}, f32[2,256]{1,0:T(2,128)S(1)}, u32[]{:S(2)}, u32[]{:S(2)}) %collective-permute-start.3) | collective-permute-done | bytes 2080 | tf_op jit(solution)/shard_map/ppermute | solution.py:405
  50.3 1.2 %collective-permute-done.2.stat_b = f32[2,256]{1,0:T(2,128)S(1)} collective-permute-done((f32[2,256]{1,0:T(2,128)S(1)}, f32[2,256]{1,0:T(2,128)S(1)}, u32[]{:S(2)}, u32[]{:S(2)}) %collective-permute-start.2) | collective-permute-done | bytes 2080 | tf_op jit(solution)/shard_map/ppermute | solution.py:405
  51.5 0.7 %shard_map.123 = (bf16[128,256]{1,0:T(8,128)(2,1)S(1)}, f32[2,256]{1,0:T(2,128)S(1)}) custom-call(s32[1]{0:T(128)} %bitcast.2.me_ref, f32[2,16,128,256]{3,2,1,0:T(8,128)S(1)} %get-tuple-element.29.mix_ref, f32[2,256]{1,0:T(2,128)S(1)} %get-tuple-element.30.stat_a, f32[2,256]{1,0:T(2,128)S(1)} %collective-permute-done.2.stat_b, ...), custom_call_target="tpu_custom_call" | custom-call | tf_op jit(solution)/shard_map/pallas_call | solution.py:415
  52.2 0.4 shard_map.126
  52.6 0.4 shard_map.125
  53.0 0.9 %collective-permute-start.5 = (bf16[128,256]{1,0:T(8,128)(2,1)S(1)}, bf16[128,256]{1,0:T(8,128)(2,1)S(1)}, u32[]{:S(2)}, u32[]{:S(2)}) collective-permute-start(bf16[128,256]{1,0:T(8,128)(2,1)S(1)} %shard_map.125), channel_id=1, source_target_pairs={{0,1},{1,2},{2,3},{3,0},{4,5},{5,6},{6,7},{7,4},{8,9},{9,10},{10,1... | collective-permute-start | bytes 196616 | tf_op jit(solution)/shard_map/ppermute | solution.py:413
  53.9 1.2 %collective-permute-start.7 = (bf16[128,256]{1,0:T(8,128)(2,1)S(1)}, bf16[128,256]{1,0:T(8,128)(2,1)S(1)}, u32[]{:S(2)}, u32[]{:S(2)}) collective-permute-start(bf16[128,256]{1,0:T(8,128)(2,1)S(1)} %shard_map.126), channel_id=1, source_target_pairs={{0,3},{1,0},{2,1},{3,2},{4,7},{5,4},{6,5},{7,6},{8,11},{9,8},{10,9... | collective-permute-start | bytes 196616 | tf_op jit(solution)/shard_map/ppermute | solution.py:413
  55.1 1.5 %collective-permute-start.6 = (bf16[128,256]{1,0:T(8,128)(2,1)S(1)}, bf16[128,256]{1,0:T(8,128)(2,1)S(1)}, u32[]{:S(2)}, u32[]{:S(2)}) collective-permute-start(bf16[128,256]{1,0:T(8,128)(2,1)S(1)} %get-tuple-element.32), channel_id=1, source_target_pairs={{0,2},{1,3},{2,0},{3,1},{4,6},{5,7},{6,4},{7,5},{8,10},{9,11},{10,... | collective-permute-start | bytes 196616 | tf_op jit(solution)/shard_map/ppermute | solution.py:413
  56.6 0.4 shard_map.124.own
  57.3 0.8 %collective-permute-done.7.three = bf16[128,256]{1,0:T(8,128)(2,1)S(1)} collective-permute-done((bf16[128,256]{1,0:T(8,128)(2,1)S(1)}, bf16[128,256]{1,0:T(8,128)(2,1)S(1)}, u32[]{:S(2)}, u32[]{:S(2)}) %collective-permute-start.7) | collective-permute-done | bytes 65568 | tf_op jit(solution)/shard_map/ppermute | solution.py:413
  58.1 2.7 %collective-permute-done.6.two = bf16[128,256]{1,0:T(8,128)(2,1)S(1)} collective-permute-done((bf16[128,256]{1,0:T(8,128)(2,1)S(1)}, bf16[128,256]{1,0:T(8,128)(2,1)S(1)}, u32[]{:S(2)}, u32[]{:S(2)}) %collective-permute-start.6) | collective-permute-done | bytes 65568 | tf_op jit(solution)/shard_map/ppermute | solution.py:413
  60.8 0.7 %shard_map.127 = bf16[4,128,256]{2,1,0:T(8,128)(2,1)} custom-call(s32[1]{0:T(128)} %bitcast.2.me_ref, bf16[128,256]{1,0:T(8,128)(2,1)S(1)} %shard_map.124.own, bf16[128,256]{1,0:T(8,128)(2,1)S(1)} %collective-permute-done.5.one, bf16[128,256]{1,0:T(8,128)(2,1)S(1)} %collective-permute-done.6.two, bf16[128,256]{1,0:T(8,128)(2,1)S(1)} %collective-permute-done.7.three), custom_call_target="tpu_custom_call" | custom-call | tf_op jit(solution)/shard_map/pallas_call | solution.py:436
  (13 shorter events, 0.5 us)
Async XLA Ops:
  0.0 1.5 %collective-permute-start.1 = (bf16[8,3,4,256]{3,2,1,0:T(4,128)(2,1)}, bf16[8,3,4,256]{3,2,1,0:T(4,128)(2,1)S(1)}, u32[]{:S(2)}, u32[]{:S(2)}) collective-permute-start(bf16[8,3,4,256]{3,2,1,0:T(4,128)(2,1)} %fr.1), channel_id=1, source_target_pairs={{0,16},{16,0},{32,48},{48,32},{64,80},{80,64},{96,112},{112,96},{1... | collective-permute-start | bytes 147464 | tf_op jit(solution)/shard_map/ppermute | solution.py:349
  0.0 1.5 %collective-permute-start = (s32[8]{0:T(128)}, s32[8]{0:T(128)S(1)}, u32[]{:S(2)}, u32[]{:S(2)}) collective-permute-start(s32[8]{0:T(128)} %keep.1), channel_id=1, source_target_pairs={{0,16},{16,0},{32,48},{48,32},{64,80},{80,64},{96,112},{112,96},{1... | collective-permute-start | bytes 104 | tf_op jit(solution)/shard_map/ppermute | solution.py:350
  22.4 13.9 %all-to-all-start.1 = ((bf16[16,3,4,256]{3,2,1,0:T(4,128)(2,1)}), bf16[16,3,4,256]{3,2,1,0:T(4,128)(2,1)S(1)}, u32[]{:S(2)}, u32[]{:S(2)}) async-start(bf16[16,3,4,256]{3,2,1,0:T(4,128)(2,1)} %shard_map.120), calls=%async_computation.1 | async-start | bytes 196608 | tf_op jit(solution)/shard_map/all_to_all | solution.py:380
  29.8 21.7 %copy-start = (bf16[1024,256]{1,0:T(8,128)(2,1)S(1)}, bf16[1024,256]{1,0:T(8,128)(2,1)}, u32[]{:S(2)}) copy-start(bf16[1024,256]{1,0:T(8,128)(2,1)} %dw_ref.7) | copy-start | bytes 1572868
  29.8 21.7 %copy-start.1 = (f32[256]{0:T(256)S(1)}, f32[256]{0:T(256)}, u32[]{:S(2)}) copy-start(f32[256]{0:T(256)} %param.22) | copy-start | bytes 3076
  29.9 21.7 %copy-start.2 = (f32[256]{0:T(256)S(1)}, f32[256]{0:T(256)}, u32[]{:S(2)}) copy-start(f32[256]{0:T(256)} %param.19) | copy-start | bytes 3076
  29.9 21.7 %copy-start.3 = (f32[256]{0:T(256)S(1)}, f32[256]{0:T(256)}, u32[]{:S(2)}) copy-start(f32[256]{0:T(256)} %param.20) | copy-start | bytes 3076
  44.2 3.7 %collective-permute-start.4 = (f32[2,256]{1,0:T(2,128)S(1)}, f32[2,256]{1,0:T(2,128)S(1)}, u32[]{:S(2)}, u32[]{:S(2)}) collective-permute-start(f32[2,256]{1,0:T(2,128)S(1)} %get-tuple-element.30.stat_a), channel_id=1, source_target_pairs={{0,12},{4,0},{8,4},{12,8},{1,13},{5,1},{9,5},{13,9},{2,14},{6,2},{... | collective-permute-start | bytes 6152 | tf_op jit(solution)/shard_map/ppermute | solution.py:405
  45.3 5.1 %collective-permute-start.3 = (f32[2,256]{1,0:T(2,128)S(1)}, f32[2,256]{1,0:T(2,128)S(1)}, u32[]{:S(2)}, u32[]{:S(2)}) collective-permute-start(f32[2,256]{1,0:T(2,128)S(1)} %get-tuple-element.30.stat_a), channel_id=1, source_target_pairs={{0,8},{4,12},{8,0},{12,4},{1,9},{5,13},{9,1},{13,5},{2,10},{6,14},... | collective-permute-start | bytes 6152 | tf_op jit(solution)/shard_map/ppermute | solution.py:405
  46.7 4.8 %collective-permute-start.2 = (f32[2,256]{1,0:T(2,128)S(1)}, f32[2,256]{1,0:T(2,128)S(1)}, u32[]{:S(2)}, u32[]{:S(2)}) collective-permute-start(f32[2,256]{1,0:T(2,128)S(1)} %get-tuple-element.30.stat_a), channel_id=1, source_target_pairs={{0,4},{4,8},{8,12},{12,0},{1,5},{5,9},{9,13},{13,1},{2,6},{6,10},{... | collective-permute-start | bytes 6152 | tf_op jit(solution)/shard_map/ppermute | solution.py:405
  53.0 4.3 %collective-permute-start.5 = (bf16[128,256]{1,0:T(8,128)(2,1)S(1)}, bf16[128,256]{1,0:T(8,128)(2,1)S(1)}, u32[]{:S(2)}, u32[]{:S(2)}) collective-permute-start(bf16[128,256]{1,0:T(8,128)(2,1)S(1)} %shard_map.125), channel_id=1, source_target_pairs={{0,1},{1,2},{2,3},{3,0},{4,5},{5,6},{6,7},{7,4},{8,9},{9,10},{10,1... | collective-permute-start | bytes 196616 | tf_op jit(solution)/shard_map/ppermute | solution.py:413
  53.9 4.3 %collective-permute-start.7 = (bf16[128,256]{1,0:T(8,128)(2,1)S(1)}, bf16[128,256]{1,0:T(8,128)(2,1)S(1)}, u32[]{:S(2)}, u32[]{:S(2)}) collective-permute-start(bf16[128,256]{1,0:T(8,128)(2,1)S(1)} %shard_map.126), channel_id=1, source_target_pairs={{0,3},{1,0},{2,1},{3,2},{4,7},{5,4},{6,5},{7,6},{8,11},{9,8},{10,9... | collective-permute-start | bytes 196616 | tf_op jit(solution)/shard_map/ppermute | solution.py:413
  55.1 5.8 %collective-permute-start.6 = (bf16[128,256]{1,0:T(8,128)(2,1)S(1)}, bf16[128,256]{1,0:T(8,128)(2,1)S(1)}, u32[]{:S(2)}, u32[]{:S(2)}) collective-permute-start(bf16[128,256]{1,0:T(8,128)(2,1)S(1)} %get-tuple-element.32), channel_id=1, source_target_pairs={{0,2},{1,3},{2,0},{3,1},{4,6},{5,7},{6,4},{7,5},{8,10},{9,11},{10,... | collective-permute-start | bytes 196616 | tf_op jit(solution)/shard_map/ppermute | solution.py:413

commit v7 on v6

--- a/solution.py
+++ b/solution.py
@@ -93,9 +93,14 @@
     n = total.shape[1]
     gi = iota((n, n), 0) // per_group
     gj = iota((n, n), 1) // per_group
-    member = (gi == gj).astype(F32)
+    member = (gi == gj).astype(F32).astype(BF16)
     both = jnp.concatenate([total, square, jnp.zeros((6, n), F32)], axis=0)
-    sums = jnp.dot(both, member, precision=lax.Precision.HIGHEST, preferred_element_type=F32)
+    high = both.astype(BF16).astype(F32)
+    rest = both - high
+    middle = rest.astype(BF16).astype(F32)
+    split = jnp.concatenate([high, middle, rest - middle, jnp.zeros((8, n), F32)], axis=0)
+    sums = jnp.dot(split.astype(BF16), member, preferred_element_type=F32)
+    sums = sums[0:8] + (sums[8:16] + sums[16:24])
     sums = sums * (1.0 / (cells * per_group))
     mean = sums[0:1]
     spread = sums[1:2] - mean * mean
@@ -412,8 +417,8 @@
     def send(by):
         return lax.ppermute(parts[by], "tm", [(i, (i + by) % 4) for i in range(4)])
 
-    parts[2], affine = call(
-        functools.partial(first_kernel, 2),
+    parts[3], affine = call(
+        functools.partial(first_kernel, 3),
         (part, sds((2, 256), F32)),
         [SMEM] + [VMEM] * 9,
         room,
@@ -426,8 +431,8 @@
         mixer_shift.reshape(1, -1),
         *dw_bias,
     )
-    parts[2] = send(2)
-    for by in (1, 3, 0):
+    parts[3] = send(3)
+    for by in (2, 1, 0):
         parts[by] = call(
             functools.partial(next_kernel, by), part, [SMEM] + [VMEM] * 4, room
         )(me, mix, affine, *dw_bias)

time: 62.8 us -> 61.9 us (0.986); the launches traced: 61.7 us -> 61.5 us
  transfers between devices with their start and end apart: 9 -> 9, of which waited for: 8 -> 7; matrix products, arithmetic and copies ran while one was open for 0% -> 0% of each run, Pallas kernels for 5% -> 5%
where the time goes in v7:
time: 61.9 us; the launch traced here: 61.5 us
  blocking collectives  19.2 us (31%)
  Pallas kernels  14.9 us (24%)
  starting transfers between devices  14.8 us (24%)
  waiting for transfers between devices  12.4 us (20%)
    all_to_all x1, blocking collectives, local(): lax.all_to_all(packed, 'clip', split_axis=0, concat_axis=0, tiled=True, a...  19.2 us
    pallas_call x1, Pallas kernels, local(): call(mixer_kernel, (sds((2, 16, 128, 256), F32), sds((2, 256), F32)), [SM...  7.87 us
    all_to_all x1, starting transfers between devices, local(): lax.all_to_all(pieces, ('row', 'tm'), split_axis=0, concat_axis=0, tiled=...  7.48 us
    ppermute x3, waiting for transfers between devices, local(): lax.ppermute(stat, 'row', [(i, (i + by) % 4) for i in range(4)])  4.76 us
    all_to_all x1, waiting for transfers between devices, local(): lax.all_to_all(pieces, ('row', 'tm'), split_axis=0, concat_axis=0, tiled=...  4.27 us
    ppermute x3, starting transfers between devices, send(): return lax.ppermute(parts[by], 'tm', [(i, (i + by) % 4) for i in range(4)])  4.23 us
    ppermute x3, waiting for transfers between devices, send(): return lax.ppermute(parts[by], 'tm', [(i, (i + by) % 4) for i in range(4)])  3.27 us
    ppermute x3, starting transfers between devices, local(): lax.ppermute(stat, 'row', [(i, (i + by) % 4) for i in range(4)])  2.56 us
  transfers between devices with their start and end apart: 9, of which 7 were waited for; matrix products, arithmetic and copies ran while one was open for 0% of the time, Pallas kernels for 5%

profile of v7, /device:TPU:2, one launch (start us, length us, event | category | flops | bytes accessed | tf_op | source)
XLA Modules:
  0.0 61.5 jit_solution(10340370771977307347)
XLA Ops:
  0.0 0.5 collective-permute-start
  0.5 0.9 %shard_map.118 = (s32[8]{0:T(128)S(1)}, s32[64]{0:T(128)S(1)}, bf16[8,3,4,256]{3,2,1,0:T(4,128)(2,1)S(1)}) custom-call(s32[8]{0:T(128)} %keep.1, s32[64]{0:T(128)} %train.1, bf16[8,3,4,256]{3,2,1,0:T(4,128)(2,1)} %fr.1), custom_call_target="tpu_custom_call" | custom-call | tf_op jit(solution)/shard_map/pallas_call | solution.py:356
  1.5 0.8 %shard_map.119 = bf16[8,4,3,4,256]{4,3,2,1,0:T(4,128)(2,1)S(1)} custom-call(s32[1]{0:T(128)} %bitcast.core_ref, s32[8]{0:T(128)S(1)} %get-tuple-element.22.keep_s, s32[8]{0:T(128)S(1)} %collective-permute-done.keep_t, s32[64]{0:T(128)S(1)} %get-tuple-element.23.train_s, bf16[8,3,4,256]{3,2,1,0:T(4,128)(2,1)S(1)} %get-tuple-element.24.fra, ...), custom_call_target="tpu_custom_call" | custom-call | tf_op jit(solution)/shard_map/pallas_call | solution.py:362
  2.3 19.2 %all_to_all.10.recv_ref = bf16[8,4,3,4,256]{4,3,2,1,0:T(4,128)(2,1)S(1)} all-to-all(bf16[8,4,3,4,256]{4,3,2,1,0:T(4,128)(2,1)S(1)} %shard_map.119), channel_id=1, replica_groups={{0,32,64,96,128,160,192,224},{16,48,80,112,144,176,208,240},{1,33,65,97..., dimensions={0} | all-to-all | bytes 393216 | tf_op jit(solution)/shard_map/all_to_all | solution.py:366
  21.5 0.8 %shard_map.120 = bf16[16,3,4,256]{3,2,1,0:T(4,128)(2,1)} custom-call(bf16[8,4,3,4,256]{4,3,2,1,0:T(4,128)(2,1)S(1)} %all_to_all.10.recv_ref), custom_call_target="tpu_custom_call" | custom-call | tf_op jit(solution)/shard_map/pallas_call | solution.py:369
  22.4 7.5 %all-to-all-start.1 = ((bf16[16,3,4,256]{3,2,1,0:T(4,128)(2,1)}), bf16[16,3,4,256]{3,2,1,0:T(4,128)(2,1)S(1)}, u32[]{:S(2)}, u32[]{:S(2)}) async-start(bf16[16,3,4,256]{3,2,1,0:T(4,128)(2,1)} %shard_map.120), calls=%async_computation.1 | async-start | bytes 196608 | tf_op jit(solution)/shard_map/all_to_all | solution.py:385
  29.9 2.1 %shard_map.121 = (bf16[8,256,128]{2,1,0:T(8,128)(2,1)S(1)}, bf16[4,1152,256]{2,1,0:T(8,128)(2,1)S(1)}) custom-call(bf16[2048,81]{1,0:T(8,128)(2,1)} %constant.27.clone.places_hbm, bf16[81,128]{1,0:T(8,128)(2,1)} %stem_hbm.1, bf16[3456,256]{1,0:T(8,128)(2,1)} %bitcast.16), custom_call_target="tpu_custom_call" | custom-call | tf_op jit(solution)/shard_map/pallas_call | solution.py:374
  32.0 4.3 %all-to-all-done.1.raw_ref = bf16[16,3,4,256]{3,2,1,0:T(4,128)(2,1)S(1)} async-done(((bf16[16,3,4,256]{3,2,1,0:T(4,128)(2,1)}), bf16[16,3,4,256]{3,2,1,0:T(4,128)(2,1)S(1)}, u32[]{:S(2)}, u32[]{:S(2)}) %all-to-all-start.1) | async-done | bytes 98336 | tf_op jit(solution)/shard_map/all_to_all | solution.py:385
  36.3 7.9 %shard_map.122 = (f32[2,16,128,256]{3,2,1,0:T(8,128)S(1)}, f32[2,256]{1,0:T(2,128)S(1)}) custom-call(s32[1]{0:T(128)} %bitcast.1.y_ref, bf16[16,3,4,256]{3,2,1,0:T(4,128)(2,1)S(1)} %all-to-all-done.1.raw_ref, bf16[8,256,128]{2,1,0:T(8,128)(2,1)S(1)} %get-tuple-element.27.w4_ref, f32[1,128]{1,0:T(1,128)} %bitcast.17, f32[1,128]{1,0:T(1,128)} %bitcast.18, ...), custom_call_target="tpu_custom_call" | custom-call | tf_op jit(solution)/shard_map/pallas_call | solution.py:386
  44.2 1.1 %collective-permute-start.4 = (f32[2,256]{1,0:T(2,128)S(1)}, f32[2,256]{1,0:T(2,128)S(1)}, u32[]{:S(2)}, u32[]{:S(2)}) collective-permute-start(f32[2,256]{1,0:T(2,128)S(1)} %get-tuple-element.30.stat_a), channel_id=1, source_target_pairs={{0,12},{4,0},{8,4},{12,8},{1,13},{5,1},{9,5},{13,9},{2,14},{6,2},{... | collective-permute-start | bytes 6152 | tf_op jit(solution)/shard_map/ppermute | solution.py:410
  45.2 1.5 %collective-permute-start.3 = (f32[2,256]{1,0:T(2,128)S(1)}, f32[2,256]{1,0:T(2,128)S(1)}, u32[]{:S(2)}, u32[]{:S(2)}) collective-permute-start(f32[2,256]{1,0:T(2,128)S(1)} %get-tuple-element.30.stat_a), channel_id=1, source_target_pairs={{0,8},{4,12},{8,0},{12,4},{1,9},{5,13},{9,1},{13,5},{2,10},{6,14},... | collective-permute-start | bytes 6152 | tf_op jit(solution)/shard_map/ppermute | solution.py:410
  46.7 1.1 %collective-permute-done.4.stat_d = f32[2,256]{1,0:T(2,128)S(1)} collective-permute-done((f32[2,256]{1,0:T(2,128)S(1)}, f32[2,256]{1,0:T(2,128)S(1)}, u32[]{:S(2)}, u32[]{:S(2)}) %collective-permute-start.4) | collective-permute-done | bytes 2080 | tf_op jit(solution)/shard_map/ppermute | solution.py:410
  47.8 2.5 %collective-permute-done.3.stat_c = f32[2,256]{1,0:T(2,128)S(1)} collective-permute-done((f32[2,256]{1,0:T(2,128)S(1)}, f32[2,256]{1,0:T(2,128)S(1)}, u32[]{:S(2)}, u32[]{:S(2)}) %collective-permute-start.3) | collective-permute-done | bytes 2080 | tf_op jit(solution)/shard_map/ppermute | solution.py:410
  50.3 1.2 %collective-permute-done.2.stat_b = f32[2,256]{1,0:T(2,128)S(1)} collective-permute-done((f32[2,256]{1,0:T(2,128)S(1)}, f32[2,256]{1,0:T(2,128)S(1)}, u32[]{:S(2)}, u32[]{:S(2)}) %collective-permute-start.2) | collective-permute-done | bytes 2080 | tf_op jit(solution)/shard_map/ppermute | solution.py:410
  51.5 0.5 shard_map.123
  52.0 0.4 shard_map.126
  52.4 0.4 shard_map.125
  52.8 0.9 %collective-permute-start.5 = (bf16[128,256]{1,0:T(8,128)(2,1)S(1)}, bf16[128,256]{1,0:T(8,128)(2,1)S(1)}, u32[]{:S(2)}, u32[]{:S(2)}) collective-permute-start(bf16[128,256]{1,0:T(8,128)(2,1)S(1)} %shard_map.125), channel_id=1, source_target_pairs={{0,1},{1,2},{2,3},{3,0},{4,5},{5,6},{6,7},{7,4},{8,9},{9,10},{10,1... | collective-permute-start | bytes 196616 | tf_op jit(solution)/shard_map/ppermute | solution.py:418
  53.7 2.7 %collective-permute-start.6 = (bf16[128,256]{1,0:T(8,128)(2,1)S(1)}, bf16[128,256]{1,0:T(8,128)(2,1)S(1)}, u32[]{:S(2)}, u32[]{:S(2)}) collective-permute-start(bf16[128,256]{1,0:T(8,128)(2,1)S(1)} %shard_map.126), channel_id=1, source_target_pairs={{0,2},{1,3},{2,0},{3,1},{4,6},{5,7},{6,4},{7,5},{8,10},{9,11},{10,... | collective-permute-start | bytes 196616 | tf_op jit(solution)/shard_map/ppermute | solution.py:418
  56.4 0.6 %collective-permute-start.7 = (bf16[128,256]{1,0:T(8,128)(2,1)S(1)}, bf16[128,256]{1,0:T(8,128)(2,1)S(1)}, u32[]{:S(2)}, u32[]{:S(2)}) collective-permute-start(bf16[128,256]{1,0:T(8,128)(2,1)S(1)} %get-tuple-element.32), channel_id=1, source_target_pairs={{0,3},{1,0},{2,1},{3,2},{4,7},{5,4},{6,5},{7,6},{8,11},{9,8},{10,9... | collective-permute-start | bytes 196616 | tf_op jit(solution)/shard_map/ppermute | solution.py:418
  57.0 0.4 shard_map.124.own
  57.4 2.1 %collective-permute-done.6.two = bf16[128,256]{1,0:T(8,128)(2,1)S(1)} collective-permute-done((bf16[128,256]{1,0:T(8,128)(2,1)S(1)}, bf16[128,256]{1,0:T(8,128)(2,1)S(1)}, u32[]{:S(2)}, u32[]{:S(2)}) %collective-permute-start.6) | collective-permute-done | bytes 65568 | tf_op jit(solution)/shard_map/ppermute | solution.py:418
  59.5 1.2 %collective-permute-done.7.three = bf16[128,256]{1,0:T(8,128)(2,1)S(1)} collective-permute-done((bf16[128,256]{1,0:T(8,128)(2,1)S(1)}, bf16[128,256]{1,0:T(8,128)(2,1)S(1)}, u32[]{:S(2)}, u32[]{:S(2)}) %collective-permute-start.7) | collective-permute-done | bytes 65568 | tf_op jit(solution)/shard_map/ppermute | solution.py:418
  60.6 0.7 %shard_map.127 = bf16[4,128,256]{2,1,0:T(8,128)(2,1)} custom-call(s32[1]{0:T(128)} %bitcast.2.me_ref, bf16[128,256]{1,0:T(8,128)(2,1)S(1)} %shard_map.124.own, bf16[128,256]{1,0:T(8,128)(2,1)S(1)} %collective-permute-done.5.one, bf16[128,256]{1,0:T(8,128)(2,1)S(1)} %collective-permute-done.6.two, bf16[128,256]{1,0:T(8,128)(2,1)S(1)} %collective-permute-done.7.three), custom_call_target="tpu_custom_call" | custom-call | tf_op jit(solution)/shard_map/pallas_call | solution.py:441
  (13 shorter events, 0.2 us)
Async XLA Ops:
  0.0 1.5 %collective-permute-start.1 = (bf16[8,3,4,256]{3,2,1,0:T(4,128)(2,1)}, bf16[8,3,4,256]{3,2,1,0:T(4,128)(2,1)S(1)}, u32[]{:S(2)}, u32[]{:S(2)}) collective-permute-start(bf16[8,3,4,256]{3,2,1,0:T(4,128)(2,1)} %fr.1), channel_id=1, source_target_pairs={{0,16},{16,0},{32,48},{48,32},{64,80},{80,64},{96,112},{112,96},{1... | collective-permute-start | bytes 147464 | tf_op jit(solution)/shard_map/ppermute | solution.py:354
  0.0 1.5 %collective-permute-start = (s32[8]{0:T(128)}, s32[8]{0:T(128)S(1)}, u32[]{:S(2)}, u32[]{:S(2)}) collective-permute-start(s32[8]{0:T(128)} %keep.1), channel_id=1, source_target_pairs={{0,16},{16,0},{32,48},{48,32},{64,80},{80,64},{96,112},{112,96},{1... | collective-permute-start | bytes 104 | tf_op jit(solution)/shard_map/ppermute | solution.py:355
  22.4 13.9 %all-to-all-start.1 = ((bf16[16,3,4,256]{3,2,1,0:T(4,128)(2,1)}), bf16[16,3,4,256]{3,2,1,0:T(4,128)(2,1)S(1)}, u32[]{:S(2)}, u32[]{:S(2)}) async-start(bf16[16,3,4,256]{3,2,1,0:T(4,128)(2,1)} %shard_map.120), calls=%async_computation.1 | async-start | bytes 196608 | tf_op jit(solution)/shard_map/all_to_all | solution.py:385
  29.8 21.7 %copy-start = (bf16[1024,256]{1,0:T(8,128)(2,1)S(1)}, bf16[1024,256]{1,0:T(8,128)(2,1)}, u32[]{:S(2)}) copy-start(bf16[1024,256]{1,0:T(8,128)(2,1)} %dw_ref.7) | copy-start | bytes 1572868
  29.8 21.7 %copy-start.1 = (f32[256]{0:T(256)S(1)}, f32[256]{0:T(256)}, u32[]{:S(2)}) copy-start(f32[256]{0:T(256)} %param.22) | copy-start | bytes 3076
  29.9 21.6 %copy-start.2 = (f32[256]{0:T(256)S(1)}, f32[256]{0:T(256)}, u32[]{:S(2)}) copy-start(f32[256]{0:T(256)} %param.19) | copy-start | bytes 3076
  29.9 21.6 %copy-start.3 = (f32[256]{0:T(256)S(1)}, f32[256]{0:T(256)}, u32[]{:S(2)}) copy-start(f32[256]{0:T(256)} %param.20) | copy-start | bytes 3076
  44.2 3.7 %collective-permute-start.4 = (f32[2,256]{1,0:T(2,128)S(1)}, f32[2,256]{1,0:T(2,128)S(1)}, u32[]{:S(2)}, u32[]{:S(2)}) collective-permute-start(f32[2,256]{1,0:T(2,128)S(1)} %get-tuple-element.30.stat_a), channel_id=1, source_target_pairs={{0,12},{4,0},{8,4},{12,8},{1,13},{5,1},{9,5},{13,9},{2,14},{6,2},{... | collective-permute-start | bytes 6152 | tf_op jit(solution)/shard_map/ppermute | solution.py:410
  45.2 5.1 %collective-permute-start.3 = (f32[2,256]{1,0:T(2,128)S(1)}, f32[2,256]{1,0:T(2,128)S(1)}, u32[]{:S(2)}, u32[]{:S(2)}) collective-permute-start(f32[2,256]{1,0:T(2,128)S(1)} %get-tuple-element.30.stat_a), channel_id=1, source_target_pairs={{0,8},{4,12},{8,0},{12,4},{1,9},{5,13},{9,1},{13,5},{2,10},{6,14},... | collective-permute-start | bytes 6152 | tf_op jit(solution)/shard_map/ppermute | solution.py:410
  46.7 4.8 %collective-permute-start.2 = (f32[2,256]{1,0:T(2,128)S(1)}, f32[2,256]{1,0:T(2,128)S(1)}, u32[]{:S(2)}, u32[]{:S(2)}) collective-permute-start(f32[2,256]{1,0:T(2,128)S(1)} %get-tuple-element.30.stat_a), channel_id=1, source_target_pairs={{0,4},{4,8},{8,12},{12,0},{1,5},{5,9},{9,13},{13,1},{2,6},{6,10},{... | collective-permute-start | bytes 6152 | tf_op jit(solution)/shard_map/ppermute | solution.py:410
  52.8 4.6 %collective-permute-start.5 = (bf16[128,256]{1,0:T(8,128)(2,1)S(1)}, bf16[128,256]{1,0:T(8,128)(2,1)S(1)}, u32[]{:S(2)}, u32[]{:S(2)}) collective-permute-start(bf16[128,256]{1,0:T(8,128)(2,1)S(1)} %shard_map.125), channel_id=1, source_target_pairs={{0,1},{1,2},{2,3},{3,0},{4,5},{5,6},{6,7},{7,4},{8,9},{9,10},{10,1... | collective-permute-start | bytes 196616 | tf_op jit(solution)/shard_map/ppermute | solution.py:418
  53.7 5.8 %collective-permute-start.6 = (bf16[128,256]{1,0:T(8,128)(2,1)S(1)}, bf16[128,256]{1,0:T(8,128)(2,1)S(1)}, u32[]{:S(2)}, u32[]{:S(2)}) collective-permute-start(bf16[128,256]{1,0:T(8,128)(2,1)S(1)} %shard_map.126), channel_id=1, source_target_pairs={{0,2},{1,3},{2,0},{3,1},{4,6},{5,7},{6,4},{7,5},{8,10},{9,11},{10,... | collective-permute-start | bytes 196616 | tf_op jit(solution)/shard_map/ppermute | solution.py:418
  56.4 4.3 %collective-permute-start.7 = (bf16[128,256]{1,0:T(8,128)(2,1)S(1)}, bf16[128,256]{1,0:T(8,128)(2,1)S(1)}, u32[]{:S(2)}, u32[]{:S(2)}) collective-permute-start(bf16[128,256]{1,0:T(8,128)(2,1)S(1)} %get-tuple-element.32), channel_id=1, source_target_pairs={{0,3},{1,0},{2,1},{3,2},{4,7},{5,4},{6,5},{7,6},{8,11},{9,8},{10,9... | collective-permute-start | bytes 196616 | tf_op jit(solution)/shard_map/ppermute | solution.py:418

commit v8 on v7

--- a/solution.py
+++ b/solution.py
@@ -22,16 +22,20 @@
     return lax.broadcasted_iota(jnp.int32, shape, dim)
 
 
-def weights_kernel(places_hbm, stem_hbm, mw_hbm, w4_ref, taps_ref, places, stem, mw, sems):
+def weights_kernel(
+    places_hbm, stem_hbm, mw_hbm, w4_ref, taps_ref, places, stem, mw, padded, sems
+):
     pairs = ((places_hbm, places), (stem_hbm, stem), (mw_hbm, mw))
     copies = [pltpu.make_async_copy(src, dst, sems.at[i]) for i, (src, dst) in enumerate(pairs)]
     for copy in copies:
         copy.start()
+    padded[...] = jnp.zeros_like(padded)
     copies[0].wait()
     copies[1].wait()
+    padded[0:81, :] = stem[...]
     for n in range(8):
         part = places[256 * n : 256 * n + 256, :]
-        w4_ref[n] = jnp.dot(part, stem[...], preferred_element_type=F32).astype(BF16)
+        w4_ref[n] = jnp.dot(part, padded[...], preferred_element_type=F32).astype(BF16)
     copies[2].wait()
     for k in range(9):
         g0, g1, g2 = (mw[384 * k + 128 * c : 384 * k + 128 * c + 128] for c in range(3))
@@ -215,7 +219,8 @@
     steps = [(a, b) for a in range(3) for b in range(3)]
     tail_even = jnp.concatenate([taps_ref[0, 1024:], taps_ref[1, 1024:]], axis=0)
     tail_odd = jnp.concatenate([taps_ref[1, 1024:], -taps_ref[3, 1024:]], axis=0)
-    tail_both = taps_ref[2, 1024:]
+    tail_both = jnp.concatenate([taps_ref[2, 1024:], jnp.zeros((128, 256), BF16)], axis=0)
+    blank = jnp.zeros((512, 128), BF16)
     for k in range(16):
         make_hidden(k)
     for f in range(0, 16, 4):
@@ -231,7 +236,8 @@
         t = [tap(k, 2, 2) for k in range(4)]
         even = jnp.dot(jnp.concatenate([t[0], t[1]], axis=1), tail_even, preferred_element_type=F32)
         odd = jnp.dot(jnp.concatenate([t[1], t[3]], axis=1), tail_odd, preferred_element_type=F32)
-        both = jnp.dot(t[2], tail_both, preferred_element_type=F32) + m[2]
+        both = jnp.concatenate([t[2], blank], axis=1)
+        both = jnp.dot(both, tail_both, preferred_element_type=F32) + m[2]
         even = even + m[0] + (m[1] + both)
         odd = odd - m[3] + (m[1] - both)
         for par, out in enumerate((even, odd)):
@@ -304,7 +310,7 @@
 
 
 def stem_places():
-    place = np.zeros((8, 256, 81), np.float32)
+    place = np.zeros((8, 256, 128), np.float32)
     for fo in range(4):
         for par in range(2):
             for a in range(3):
@@ -313,7 +319,7 @@
                         for ch in range(3):
                             row = b * 72 + (fo + a) * 12 + (par + c) * 3 + ch
                             place[fo * 2 + par, row, ((a * 3 + b) * 3 + c) * 3 + ch] = 1
-    return place.reshape(2048, 81)
+    return place.reshape(2048, 128)
 
 
 def in_hbm(array):
@@ -376,9 +382,10 @@
         (sds((8, 256, 128), BF16), sds((4, 1152, 256), BF16)),
         [HBM] * 3,
         [
-            pltpu.VMEM((2048, 81), BF16),
+            pltpu.VMEM((2048, 128), BF16),
             pltpu.VMEM((81, 128), BF16),
             pltpu.VMEM((3456, 256), BF16),
+            pltpu.VMEM((128, 128), BF16),
             pltpu.SemaphoreType.DMA((3,)),
         ],
     )(in_hbm(places), in_hbm(stem_weight), in_hbm(mixer_weight.reshape(3456, 256)))

time: 61.9 us -> 61.9 us (level)
  no operation moved by 1% of the time
where the time goes in v8:
time: 61.9 us; the launch traced here: 61.5 us
  blocking collectives  19.2 us (31%)
  Pallas kernels  14.9 us (24%)
  starting transfers between devices  14.8 us (24%)
  waiting for transfers between devices  12.4 us (20%)
    all_to_all x1, blocking collectives, local(): lax.all_to_all(packed, 'clip', split_axis=0, concat_axis=0, tiled=True, a...  19.2 us
    pallas_call x1, Pallas kernels, local(): call(mixer_kernel, (sds((2, 16, 128, 256), F32), sds((2, 256), F32)), [SM...  7.87 us
    all_to_all x1, starting transfers between devices, local(): lax.all_to_all(pieces, ('row', 'tm'), split_axis=0, concat_axis=0, tiled=...  7.48 us
    ppermute x3, waiting for transfers between devices, local(): lax.ppermute(stat, 'row', [(i, (i + by) % 4) for i in range(4)])  4.76 us
    all_to_all x1, waiting for transfers between devices, local(): lax.all_to_all(pieces, ('row', 'tm'), split_axis=0, concat_axis=0, tiled=...  4.27 us
    ppermute x3, starting transfers between devices, send(): return lax.ppermute(parts[by], 'tm', [(i, (i + by) % 4) for i in range(4)])  4.23 us
    ppermute x3, waiting for transfers between devices, send(): return lax.ppermute(parts[by], 'tm', [(i, (i + by) % 4) for i in range(4)])  3.27 us
    ppermute x3, starting transfers between devices, local(): lax.ppermute(stat, 'row', [(i, (i + by) % 4) for i in range(4)])  2.56 us
  transfers between devices with their start and end apart: 9, of which 7 were waited for; matrix products, arithmetic and copies ran while one was open for 0% of the time, Pallas kernels for 5%

profile of v8, /device:TPU:2, one launch (start us, length us, event | category | flops | bytes accessed | tf_op | source)
XLA Modules:
  0.0 61.5 jit_solution(12373532584798927958)
XLA Ops:
  0.0 0.5 collective-permute-start
  0.5 0.9 %shard_map.118 = (s32[8]{0:T(128)S(1)}, s32[64]{0:T(128)S(1)}, bf16[8,3,4,256]{3,2,1,0:T(4,128)(2,1)S(1)}) custom-call(s32[8]{0:T(128)} %keep.1, s32[64]{0:T(128)} %train.1, bf16[8,3,4,256]{3,2,1,0:T(4,128)(2,1)} %fr.1), custom_call_target="tpu_custom_call" | custom-call | tf_op jit(solution)/shard_map/pallas_call | solution.py:362
  1.5 0.8 %shard_map.119 = bf16[8,4,3,4,256]{4,3,2,1,0:T(4,128)(2,1)S(1)} custom-call(s32[1]{0:T(128)} %bitcast.core_ref, s32[8]{0:T(128)S(1)} %get-tuple-element.22.keep_s, s32[8]{0:T(128)S(1)} %collective-permute-done.keep_t, s32[64]{0:T(128)S(1)} %get-tuple-element.23.train_s, bf16[8,3,4,256]{3,2,1,0:T(4,128)(2,1)S(1)} %get-tuple-element.24.fra, ...), custom_call_target="tpu_custom_call" | custom-call | tf_op jit(solution)/shard_map/pallas_call | solution.py:368
  2.3 19.2 %all_to_all.10.recv_ref = bf16[8,4,3,4,256]{4,3,2,1,0:T(4,128)(2,1)S(1)} all-to-all(bf16[8,4,3,4,256]{4,3,2,1,0:T(4,128)(2,1)S(1)} %shard_map.119), channel_id=1, replica_groups={{0,32,64,96,128,160,192,224},{16,48,80,112,144,176,208,240},{1,33,65,97..., dimensions={0} | all-to-all | bytes 393216 | tf_op jit(solution)/shard_map/all_to_all | solution.py:372
  21.5 0.8 %shard_map.120 = bf16[16,3,4,256]{3,2,1,0:T(4,128)(2,1)} custom-call(bf16[8,4,3,4,256]{4,3,2,1,0:T(4,128)(2,1)S(1)} %all_to_all.10.recv_ref), custom_call_target="tpu_custom_call" | custom-call | tf_op jit(solution)/shard_map/pallas_call | solution.py:375
  22.4 7.5 %all-to-all-start.1 = ((bf16[16,3,4,256]{3,2,1,0:T(4,128)(2,1)}), bf16[16,3,4,256]{3,2,1,0:T(4,128)(2,1)S(1)}, u32[]{:S(2)}, u32[]{:S(2)}) async-start(bf16[16,3,4,256]{3,2,1,0:T(4,128)(2,1)} %shard_map.120), calls=%async_computation.1 | async-start | bytes 196608 | tf_op jit(solution)/shard_map/all_to_all | solution.py:392
  29.9 2.1 %shard_map.121 = (bf16[8,256,128]{2,1,0:T(8,128)(2,1)S(1)}, bf16[4,1152,256]{2,1,0:T(8,128)(2,1)S(1)}) custom-call(bf16[2048,128]{1,0:T(8,128)(2,1)} %constant.27.clone.places_hbm, bf16[81,128]{1,0:T(8,128)(2,1)} %stem_hbm.1, bf16[3456,256]{1,0:T(8,128)(2,1)} %bitcast.16), custom_call_target="tpu_custom_call" | custom-call | tf_op jit(solution)/shard_map/pallas_call | solution.py:380
  32.0 4.3 %all-to-all-done.1.raw_ref = bf16[16,3,4,256]{3,2,1,0:T(4,128)(2,1)S(1)} async-done(((bf16[16,3,4,256]{3,2,1,0:T(4,128)(2,1)}), bf16[16,3,4,256]{3,2,1,0:T(4,128)(2,1)S(1)}, u32[]{:S(2)}, u32[]{:S(2)}) %all-to-all-start.1) | async-done | bytes 98336 | tf_op jit(solution)/shard_map/all_to_all | solution.py:392
  36.3 7.9 %shard_map.122 = (f32[2,16,128,256]{3,2,1,0:T(8,128)S(1)}, f32[2,256]{1,0:T(2,128)S(1)}) custom-call(s32[1]{0:T(128)} %bitcast.1.y_ref, bf16[16,3,4,256]{3,2,1,0:T(4,128)(2,1)S(1)} %all-to-all-done.1.raw_ref, bf16[8,256,128]{2,1,0:T(8,128)(2,1)S(1)} %get-tuple-element.27.w4_ref, f32[1,128]{1,0:T(1,128)} %bitcast.17, f32[1,128]{1,0:T(1,128)} %bitcast.18, ...), custom_call_target="tpu_custom_call" | custom-call | tf_op jit(solution)/shard_map/pallas_call | solution.py:393
  44.2 1.1 %collective-permute-start.4 = (f32[2,256]{1,0:T(2,128)S(1)}, f32[2,256]{1,0:T(2,128)S(1)}, u32[]{:S(2)}, u32[]{:S(2)}) collective-permute-start(f32[2,256]{1,0:T(2,128)S(1)} %get-tuple-element.30.stat_a), channel_id=1, source_target_pairs={{0,12},{4,0},{8,4},{12,8},{1,13},{5,1},{9,5},{13,9},{2,14},{6,2},{... | collective-permute-start | bytes 6152 | tf_op jit(solution)/shard_map/ppermute | solution.py:417
  45.2 1.5 %collective-permute-start.3 = (f32[2,256]{1,0:T(2,128)S(1)}, f32[2,256]{1,0:T(2,128)S(1)}, u32[]{:S(2)}, u32[]{:S(2)}) collective-permute-start(f32[2,256]{1,0:T(2,128)S(1)} %get-tuple-element.30.stat_a), channel_id=1, source_target_pairs={{0,8},{4,12},{8,0},{12,4},{1,9},{5,13},{9,1},{13,5},{2,10},{6,14},... | collective-permute-start | bytes 6152 | tf_op jit(solution)/shard_map/ppermute | solution.py:417
  46.7 1.1 %collective-permute-done.4.stat_d = f32[2,256]{1,0:T(2,128)S(1)} collective-permute-done((f32[2,256]{1,0:T(2,128)S(1)}, f32[2,256]{1,0:T(2,128)S(1)}, u32[]{:S(2)}, u32[]{:S(2)}) %collective-permute-start.4) | collective-permute-done | bytes 2080 | tf_op jit(solution)/shard_map/ppermute | solution.py:417
  47.8 2.5 %collective-permute-done.3.stat_c = f32[2,256]{1,0:T(2,128)S(1)} collective-permute-done((f32[2,256]{1,0:T(2,128)S(1)}, f32[2,256]{1,0:T(2,128)S(1)}, u32[]{:S(2)}, u32[]{:S(2)}) %collective-permute-start.3) | collective-permute-done | bytes 2080 | tf_op jit(solution)/shard_map/ppermute | solution.py:417
  50.3 1.2 %collective-permute-done.2.stat_b = f32[2,256]{1,0:T(2,128)S(1)} collective-permute-done((f32[2,256]{1,0:T(2,128)S(1)}, f32[2,256]{1,0:T(2,128)S(1)}, u32[]{:S(2)}, u32[]{:S(2)}) %collective-permute-start.2) | collective-permute-done | bytes 2080 | tf_op jit(solution)/shard_map/ppermute | solution.py:417
  51.5 0.5 shard_map.123
  52.0 0.4 shard_map.126
  52.4 0.4 shard_map.125
  52.8 0.9 %collective-permute-start.5 = (bf16[128,256]{1,0:T(8,128)(2,1)S(1)}, bf16[128,256]{1,0:T(8,128)(2,1)S(1)}, u32[]{:S(2)}, u32[]{:S(2)}) collective-permute-start(bf16[128,256]{1,0:T(8,128)(2,1)S(1)} %shard_map.125), channel_id=1, source_target_pairs={{0,1},{1,2},{2,3},{3,0},{4,5},{5,6},{6,7},{7,4},{8,9},{9,10},{10,1... | collective-permute-start | bytes 196616 | tf_op jit(solution)/shard_map/ppermute | solution.py:425
  53.7 2.7 %collective-permute-start.6 = (bf16[128,256]{1,0:T(8,128)(2,1)S(1)}, bf16[128,256]{1,0:T(8,128)(2,1)S(1)}, u32[]{:S(2)}, u32[]{:S(2)}) collective-permute-start(bf16[128,256]{1,0:T(8,128)(2,1)S(1)} %shard_map.126), channel_id=1, source_target_pairs={{0,2},{1,3},{2,0},{3,1},{4,6},{5,7},{6,4},{7,5},{8,10},{9,11},{10,... | collective-permute-start | bytes 196616 | tf_op jit(solution)/shard_map/ppermute | solution.py:425
  56.4 0.6 %collective-permute-start.7 = (bf16[128,256]{1,0:T(8,128)(2,1)S(1)}, bf16[128,256]{1,0:T(8,128)(2,1)S(1)}, u32[]{:S(2)}, u32[]{:S(2)}) collective-permute-start(bf16[128,256]{1,0:T(8,128)(2,1)S(1)} %get-tuple-element.32), channel_id=1, source_target_pairs={{0,3},{1,0},{2,1},{3,2},{4,7},{5,4},{6,5},{7,6},{8,11},{9,8},{10,9... | collective-permute-start | bytes 196616 | tf_op jit(solution)/shard_map/ppermute | solution.py:425
  57.0 0.4 shard_map.124.own
  57.4 2.1 %collective-permute-done.6.two = bf16[128,256]{1,0:T(8,128)(2,1)S(1)} collective-permute-done((bf16[128,256]{1,0:T(8,128)(2,1)S(1)}, bf16[128,256]{1,0:T(8,128)(2,1)S(1)}, u32[]{:S(2)}, u32[]{:S(2)}) %collective-permute-start.6) | collective-permute-done | bytes 65568 | tf_op jit(solution)/shard_map/ppermute | solution.py:425
  59.5 1.2 %collective-permute-done.7.three = bf16[128,256]{1,0:T(8,128)(2,1)S(1)} collective-permute-done((bf16[128,256]{1,0:T(8,128)(2,1)S(1)}, bf16[128,256]{1,0:T(8,128)(2,1)S(1)}, u32[]{:S(2)}, u32[]{:S(2)}) %collective-permute-start.7) | collective-permute-done | bytes 65568 | tf_op jit(solution)/shard_map/ppermute | solution.py:425
  60.6 0.7 %shard_map.127 = bf16[4,128,256]{2,1,0:T(8,128)(2,1)} custom-call(s32[1]{0:T(128)} %bitcast.2.me_ref, bf16[128,256]{1,0:T(8,128)(2,1)S(1)} %shard_map.124.own, bf16[128,256]{1,0:T(8,128)(2,1)S(1)} %collective-permute-done.5.one, bf16[128,256]{1,0:T(8,128)(2,1)S(1)} %collective-permute-done.6.two, bf16[128,256]{1,0:T(8,128)(2,1)S(1)} %collective-permute-done.7.three), custom_call_target="tpu_custom_call" | custom-call | tf_op jit(solution)/shard_map/pallas_call | solution.py:448
  (13 shorter events, 0.2 us)
Async XLA Ops:
  0.0 1.5 %collective-permute-start.1 = (bf16[8,3,4,256]{3,2,1,0:T(4,128)(2,1)}, bf16[8,3,4,256]{3,2,1,0:T(4,128)(2,1)S(1)}, u32[]{:S(2)}, u32[]{:S(2)}) collective-permute-start(bf16[8,3,4,256]{3,2,1,0:T(4,128)(2,1)} %fr.1), channel_id=1, source_target_pairs={{0,16},{16,0},{32,48},{48,32},{64,80},{80,64},{96,112},{112,96},{1... | collective-permute-start | bytes 147464 | tf_op jit(solution)/shard_map/ppermute | solution.py:360
  0.0 1.5 %collective-permute-start = (s32[8]{0:T(128)}, s32[8]{0:T(128)S(1)}, u32[]{:S(2)}, u32[]{:S(2)}) collective-permute-start(s32[8]{0:T(128)} %keep.1), channel_id=1, source_target_pairs={{0,16},{16,0},{32,48},{48,32},{64,80},{80,64},{96,112},{112,96},{1... | collective-permute-start | bytes 104 | tf_op jit(solution)/shard_map/ppermute | solution.py:361
  22.4 13.9 %all-to-all-start.1 = ((bf16[16,3,4,256]{3,2,1,0:T(4,128)(2,1)}), bf16[16,3,4,256]{3,2,1,0:T(4,128)(2,1)S(1)}, u32[]{:S(2)}, u32[]{:S(2)}) async-start(bf16[16,3,4,256]{3,2,1,0:T(4,128)(2,1)} %shard_map.120), calls=%async_computation.1 | async-start | bytes 196608 | tf_op jit(solution)/shard_map/all_to_all | solution.py:392
  29.8 21.7 %copy-start = (bf16[1024,256]{1,0:T(8,128)(2,1)S(1)}, bf16[1024,256]{1,0:T(8,128)(2,1)}, u32[]{:S(2)}) copy-start(bf16[1024,256]{1,0:T(8,128)(2,1)} %dw_ref.7) | copy-start | bytes 1572868
  29.8 21.7 %copy-start.1 = (f32[256]{0:T(256)S(1)}, f32[256]{0:T(256)}, u32[]{:S(2)}) copy-start(f32[256]{0:T(256)} %param.22) | copy-start | bytes 3076
  29.9 21.6 %copy-start.2 = (f32[256]{0:T(256)S(1)}, f32[256]{0:T(256)}, u32[]{:S(2)}) copy-start(f32[256]{0:T(256)} %param.19) | copy-start | bytes 3076
  29.9 21.6 %copy-start.3 = (f32[256]{0:T(256)S(1)}, f32[256]{0:T(256)}, u32[]{:S(2)}) copy-start(f32[256]{0:T(256)} %param.20) | copy-start | bytes 3076
  44.2 3.7 %collective-permute-start.4 = (f32[2,256]{1,0:T(2,128)S(1)}, f32[2,256]{1,0:T(2,128)S(1)}, u32[]{:S(2)}, u32[]{:S(2)}) collective-permute-start(f32[2,256]{1,0:T(2,128)S(1)} %get-tuple-element.30.stat_a), channel_id=1, source_target_pairs={{0,12},{4,0},{8,4},{12,8},{1,13},{5,1},{9,5},{13,9},{2,14},{6,2},{... | collective-permute-start | bytes 6152 | tf_op jit(solution)/shard_map/ppermute | solution.py:417
  45.2 5.1 %collective-permute-start.3 = (f32[2,256]{1,0:T(2,128)S(1)}, f32[2,256]{1,0:T(2,128)S(1)}, u32[]{:S(2)}, u32[]{:S(2)}) collective-permute-start(f32[2,256]{1,0:T(2,128)S(1)} %get-tuple-element.30.stat_a), channel_id=1, source_target_pairs={{0,8},{4,12},{8,0},{12,4},{1,9},{5,13},{9,1},{13,5},{2,10},{6,14},... | collective-permute-start | bytes 6152 | tf_op jit(solution)/shard_map/ppermute | solution.py:417
  46.7 4.8 %collective-permute-start.2 = (f32[2,256]{1,0:T(2,128)S(1)}, f32[2,256]{1,0:T(2,128)S(1)}, u32[]{:S(2)}, u32[]{:S(2)}) collective-permute-start(f32[2,256]{1,0:T(2,128)S(1)} %get-tuple-element.30.stat_a), channel_id=1, source_target_pairs={{0,4},{4,8},{8,12},{12,0},{1,5},{5,9},{9,13},{13,1},{2,6},{6,10},{... | collective-permute-start | bytes 6152 | tf_op jit(solution)/shard_map/ppermute | solution.py:417
  52.8 4.6 %collective-permute-start.5 = (bf16[128,256]{1,0:T(8,128)(2,1)S(1)}, bf16[128,256]{1,0:T(8,128)(2,1)S(1)}, u32[]{:S(2)}, u32[]{:S(2)}) collective-permute-start(bf16[128,256]{1,0:T(8,128)(2,1)S(1)} %shard_map.125), channel_id=1, source_target_pairs={{0,1},{1,2},{2,3},{3,0},{4,5},{5,6},{6,7},{7,4},{8,9},{9,10},{10,1... | collective-permute-start | bytes 196616 | tf_op jit(solution)/shard_map/ppermute | solution.py:425
  53.7 5.8 %collective-permute-start.6 = (bf16[128,256]{1,0:T(8,128)(2,1)S(1)}, bf16[128,256]{1,0:T(8,128)(2,1)S(1)}, u32[]{:S(2)}, u32[]{:S(2)}) collective-permute-start(bf16[128,256]{1,0:T(8,128)(2,1)S(1)} %shard_map.126), channel_id=1, source_target_pairs={{0,2},{1,3},{2,0},{3,1},{4,6},{5,7},{6,4},{7,5},{8,10},{9,11},{10,... | collective-permute-start | bytes 196616 | tf_op jit(solution)/shard_map/ppermute | solution.py:425
  56.4 4.3 %collective-permute-start.7 = (bf16[128,256]{1,0:T(8,128)(2,1)S(1)}, bf16[128,256]{1,0:T(8,128)(2,1)S(1)}, u32[]{:S(2)}, u32[]{:S(2)}) collective-permute-start(bf16[128,256]{1,0:T(8,128)(2,1)S(1)} %get-tuple-element.32), channel_id=1, source_target_pairs={{0,3},{1,0},{2,1},{3,2},{4,7},{5,4},{6,5},{7,6},{8,11},{9,8},{10,9... | collective-permute-start | bytes 196616 | tf_op jit(solution)/shard_map/ppermute | solution.py:425
